TPU v7x, 256 devices: a whole 4x4x8 slice. The times are simulated.
256 devices in a mesh: gx: 64 (over y_hi, z, x), gy: 4 (over y_lo, core).
Axes of the slice: x: 4, y: 4 (y_hi: 2, y_lo: 2; y = y_hi * 2 + y_lo), z: 8, core: 2. Of those that a mesh axis runs over, the one named last changes fastest.
Arguments:
- features: bfloat16 [2048, 512, 128], P(('gx', 'gy')), may hold values from -6 to 6
- weights: bfloat16 [27, 128, 128], replicated, may hold values from -0.109375 to 0.109375
- cotangent: bfloat16 [2048, 512, 128], P(('gx', 'gy')), may hold values from -6 to 6
- occupancy: int32 [2048, 512], P(('gx', 'gy')), may hold values 0 or 1
- slot_pos: int32 [2048], P(('gx', 'gy')), may hold values from -1 to 15, as said below
Outputs:
- outputs: bfloat16 [2048, 512, 128], P(('gx', 'gy'))
- grad_input: bfloat16 [2048, 512, 128], P(('gx', 'gy'))
- grad_weight: float32 [27, 128, 128], replicated
Inputs may be any that keep to these rules, and one draw needn't show every extreme that they name: `slot_pos`: on each device the 8 slots name distinct positions of its region; live slots come first and the rest hold -1; each device has at least 4 live slots, and some device has all 8 live.
All inputs are finite; a program needn't handle non-finite values. No bound on the sum of `occupancy` on one device may be relied on, other than what follows from the above.
Results may differ from a plain program's by a relative error of at most 0.001.
Values may be sent and summed in bfloat16 or wider, within the bound.
No kernel may reach another device: no remote copies, remote signals or barrier semaphores. Data moves between devices by JAX's collectives and lax.ppermute only.
A program may use at most 64 MiB of HBM per device.

v0:
```python
import math

import jax
import jax.numpy as jnp
from jax import lax
from jax.sharding import PartitionSpec as P

BRICK = 8
REGION_X = 4
REGION_Y = 2
REGION_Z = 2


def with_halo(value, sides, width):
    for axis, dim in sides:
        size, length = (lax.axis_size(axis), value.shape[dim])
        up = [(i, (i + 1) % size) for i in range(size - 1)]
        down = [(j, i) for i, j in up]
        last = lax.slice_in_dim(value, length - width, length, axis=dim)
        leading = lax.slice_in_dim(value, 0, width, axis=dim)
        before = lax.ppermute(last, axis, up)
        after = lax.ppermute(leading, axis, down)
        value = jnp.concatenate([before, value, after], axis=dim)
    return value


def offset_list():
    result = []
    for along_x in (-1, 0, 1):
        for along_y in (-1, 0, 1):
            for along_z in (-1, 0, 1):
                result.append((along_x, along_y, along_z))
    return result


def brick_patches(padded, corner, first_offset, offset_count):
    channels = padded.shape[-1]
    block_span = BRICK + 2
    starts = (corner[0], corner[1], corner[2], jnp.zeros((), jnp.int32))
    block = lax.dynamic_slice(padded, starts, (block_span, block_span, block_span, channels))
    columns = []
    for along_x, along_y, along_z in offset_list()[first_offset : first_offset + offset_count]:
        window_cells = block[
            along_x + 1 : along_x + 1 + BRICK,
            along_y + 1 : along_y + 1 + BRICK,
            along_z + 1 : along_z + 1 + BRICK,
        ]
        columns.append(window_cells.reshape(BRICK**3, channels))
    return jnp.concatenate(columns, axis=1)


def shards(features, weights, cotangent, occupancy, slot_pos):
    slot_count, voxels, channels = features.shape
    positions = REGION_X * REGION_Y * REGION_Z
    active = (occupancy == 1) & (slot_pos >= 0)[:, None]
    zero_value = jnp.zeros((), features.dtype)
    masked_in = jnp.where(active[:, :, None], features, zero_value)
    masked_cot = jnp.where(active[:, :, None], cotangent, zero_value)
    one_hot = (jnp.arange(positions, dtype=jnp.int32)[:, None] == slot_pos[None, :]).astype(
        jnp.bfloat16
    )
    w_forward = weights.reshape(27 * channels, channels)
    w_backward = weights[::-1].transpose(0, 2, 1).reshape(27 * channels, channels)

    def local_grid(values):
        placed = jnp.dot(
            one_hot,
            values.reshape(slot_count, voxels * channels),
            preferred_element_type=jnp.float32,
        ).astype(jnp.bfloat16)
        voxel_cells = placed.reshape(REGION_X, REGION_Y, REGION_Z, BRICK, BRICK, BRICK, channels)
        voxel_cells = voxel_cells.transpose(0, 3, 1, 4, 2, 5, 6).reshape(
            REGION_X * BRICK, REGION_Y * BRICK, REGION_Z * BRICK, channels
        )
        padded = with_halo(voxel_cells, (("gx", 0), ("gy", 1)), 1)
        return jnp.pad(padded, ((0, 0), (0, 0), (1, 1), (0, 0)))

    def brick_corner(slot_index):
        position = jnp.maximum(slot_pos[slot_index], 0)
        return (
            position // (REGION_Y * REGION_Z) * BRICK,
            position // REGION_Z % REGION_Y * BRICK,
            position % REGION_Z * BRICK,
        )

    grid_x = local_grid(masked_in)
    slot_ids = jnp.arange(slot_count, dtype=jnp.int32)
    devices = lax.axis_size("gx") * lax.axis_size("gy")
    scale = 1.0 / math.sqrt(float(devices * slot_count * voxels))

    def make_forward():

        def forward_step(running, slot_index):
            patches = brick_patches(grid_x, brick_corner(slot_index), 0, 27)
            total = jnp.dot(patches, w_forward, preferred_element_type=jnp.float32)
            keep_mask = active[slot_index].astype(jnp.float32)[:, None]
            result = (total * keep_mask).astype(jnp.bfloat16)
            terms = jnp.einsum(
                "vk,vc->kc", patches, masked_cot[slot_index], preferred_element_type=jnp.float32
            )
            running = running + terms.reshape(27, channels, channels)
            return (running, result)

        return forward_step

    local_grad, outputs = lax.scan(
        make_forward(), jnp.zeros((27, channels, channels), jnp.float32), slot_ids
    )
    grad_weight = lax.psum(local_grad, ("gx", "gy")) * scale
    grid_dy = local_grid(masked_cot)

    def backward_step(running, slot_index):
        patches = brick_patches(grid_dy, brick_corner(slot_index), 0, 27)
        total = jnp.dot(patches, w_backward, preferred_element_type=jnp.float32)
        keep_mask = active[slot_index].astype(jnp.float32)[:, None]
        return (running, (total * keep_mask).astype(jnp.bfloat16))

    unused, grad_input = lax.scan(backward_step, jnp.zeros((), jnp.float32), slot_ids)
    return (outputs, grad_input, grad_weight)


def solution(mesh):
    return jax.shard_map(
        shards,
        mesh=mesh,
        in_specs=(
            P(("gx", "gy"), None, None),
            P(),
            P(("gx", "gy"), None, None),
            P(("gx", "gy"), None),
            P(("gx", "gy")),
        ),
        out_specs=(P(("gx", "gy"), None, None), P(("gx", "gy"), None, None), P()),
        check_vma=False,
    )
```

profile of v0, /device:TPU:1, one launch (start us, length us, event | category | flops | bytes accessed | tf_op | source)
XLA Modules:
  0.0 522.6 jit_solution(13381091320044146938)
XLA Ops:
  14.4 4.6 collective-permute-start
  27.4 5.7 %collective-permute-start.3 = (bf16[34,1,16,128]{3,2,1,0:T(8,128)(2,1)}, bf16[34,1,16,128]{3,2,1,0:T(8,128)(2,1)S(1)}, u32[]{:S(2)}, u32[]{:S(2)}) collective-permute-start(bf16[34,1,16,128]{3,2,1,0:T(8,128)(2,1)} %get-tuple-element.396), channel_id=1, source_target_pairs={{1,0},{2,1},{3,2},{5,4},{6,5},{7,6},{9,8},{10,9},{11,10},{13,12},{... | collective-permute-start | bytes 417800 | tf_op jit(solution)/shard_map/ppermute | solution.py:22
  43.4 5.6 %select_maximum_fusion.4 = bf16[34,18,18,128]{3,2,1,0:T(8,128)(2,1)} fusion(bf16[34,1,16,128]{3,2,1,0:T(8,128)(2,1)S(1)} %collective-permute-done.3, bf16[34,1,16,128]{3,2,1,0:T(8,128)(2,1)} %collective-permute-done.2, bf16[1,16,16,128]{3,2,1,0:T(8,128)(2,1)S(1)} %collective-permute-done.1, bf16[32,16,16,128]{3,2,1,0:T(8,128)(2,1)S(1)} %bitcast.277, ...), kind=kLoop, calls=%fused_computation.131 | loop fusion | flops 25380864 | bytes 5326848 | tf_op jit(solution)/shard_map/concatenate | solution.py:23
  50.1 196.6 %while.30 = (s32[]{:T(128)}, f32[27,128,128]{2,1,0:T(8,128)}, bf16[8,512,128]{2,1,0:T(8,128)(2,1)}, s32[8]{0:T(128)S(1)}, s32[8]{0:T(128)S(1)}, /*index=5*/bf16[...) while((s32[]{:T(128)}, f32[27,128,128]{2,1,0:T(8,128)}, ...), condition=%wide.region_1.2_spmd.clone, body=%wide.region_0.1_spmd.clone.sunk | while | flops 906986048 | bytes 64853388 | solution.py:106
  54.2 7.3 %constant_dynamic-slice_fusion.57 = (bf16[8,8,8,128]{3,2,1,0:T(8,128)(2,1)S(1)}, bf16[8,8,8,128]{3,2,1,0:T(8,128)(2,1)S(1)}, bf16[8,8,8,128]{3,2,1,0:T(8,128)(2,...) fusion(bf16[34,18,18,128]{3,2,1,0:T(8,128)(2,1)} %get-tuple-ele, ...), kind=kLoop, calls=%fused_computation.121.clone.1 | loop fusion | bytes 7077924 | tf_op jit(solution)/shard_map/while/body/eval_jaxpr/slice | solution.py:43
  64.4 4.4 copy.28
  77.9 8.0 %constant_dynamic-slice_fusion.57 = (bf16[8,8,8,128]{3,2,1,0:T(8,128)(2,1)S(1)}, bf16[8,8,8,128]{3,2,1,0:T(8,128)(2,1)S(1)}, bf16[8,8,8,128]{3,2,1,0:T(8,128)(2,...) fusion(bf16[34,18,18,128]{3,2,1,0:T(8,128)(2,1)} %get-tuple-ele, ...), kind=kLoop, calls=%fused_computation.121.clone.1 | loop fusion | bytes 7077924 | tf_op jit(solution)/shard_map/while/body/eval_jaxpr/slice | solution.py:43
  88.9 4.4 copy.28
  93.3 4.0 select_add_fusion.2
  103.1 8.2 %constant_dynamic-slice_fusion.57 = (bf16[8,8,8,128]{3,2,1,0:T(8,128)(2,1)S(1)}, bf16[8,8,8,128]{3,2,1,0:T(8,128)(2,1)S(1)}, bf16[8,8,8,128]{3,2,1,0:T(8,128)(2,...) fusion(bf16[34,18,18,128]{3,2,1,0:T(8,128)(2,1)} %get-tuple-ele, ...), kind=kLoop, calls=%fused_computation.121.clone.1 | loop fusion | bytes 7077924 | tf_op jit(solution)/shard_map/while/body/eval_jaxpr/slice | solution.py:43
  114.2 4.4 copy.28
  128.4 8.9 %constant_dynamic-slice_fusion.57 = (bf16[8,8,8,128]{3,2,1,0:T(8,128)(2,1)S(1)}, bf16[8,8,8,128]{3,2,1,0:T(8,128)(2,1)S(1)}, bf16[8,8,8,128]{3,2,1,0:T(8,128)(2,...) fusion(bf16[34,18,18,128]{3,2,1,0:T(8,128)(2,1)} %get-tuple-ele, ...), kind=kLoop, calls=%fused_computation.121.clone.1 | loop fusion | bytes 7077924 | tf_op jit(solution)/shard_map/while/body/eval_jaxpr/slice | solution.py:43
  140.2 4.4 copy.28
  154.5 7.2 %constant_dynamic-slice_fusion.57 = (bf16[8,8,8,128]{3,2,1,0:T(8,128)(2,1)S(1)}, bf16[8,8,8,128]{3,2,1,0:T(8,128)(2,1)S(1)}, bf16[8,8,8,128]{3,2,1,0:T(8,128)(2,...) fusion(bf16[34,18,18,128]{3,2,1,0:T(8,128)(2,1)} %get-tuple-ele, ...), kind=kLoop, calls=%fused_computation.121.clone.1 | loop fusion | bytes 7077924 | tf_op jit(solution)/shard_map/while/body/eval_jaxpr/slice | solution.py:43
  164.6 4.4 copy.28
  178.8 6.8 %constant_dynamic-slice_fusion.57 = (bf16[8,8,8,128]{3,2,1,0:T(8,128)(2,1)S(1)}, bf16[8,8,8,128]{3,2,1,0:T(8,128)(2,1)S(1)}, bf16[8,8,8,128]{3,2,1,0:T(8,128)(2,...) fusion(bf16[34,18,18,128]{3,2,1,0:T(8,128)(2,1)} %get-tuple-ele, ...), kind=kLoop, calls=%fused_computation.121.clone.1 | loop fusion | bytes 7077924 | tf_op jit(solution)/shard_map/while/body/eval_jaxpr/slice | solution.py:43
  188.5 4.4 copy.28
  202.8 6.8 %constant_dynamic-slice_fusion.57 = (bf16[8,8,8,128]{3,2,1,0:T(8,128)(2,1)S(1)}, bf16[8,8,8,128]{3,2,1,0:T(8,128)(2,1)S(1)}, bf16[8,8,8,128]{3,2,1,0:T(8,128)(2,...) fusion(bf16[34,18,18,128]{3,2,1,0:T(8,128)(2,1)} %get-tuple-ele, ...), kind=kLoop, calls=%fused_computation.121.clone.1 | loop fusion | bytes 7077924 | tf_op jit(solution)/shard_map/while/body/eval_jaxpr/slice | solution.py:43
  212.5 4.4 copy.28
  226.7 6.8 %constant_dynamic-slice_fusion.57 = (bf16[8,8,8,128]{3,2,1,0:T(8,128)(2,1)S(1)}, bf16[8,8,8,128]{3,2,1,0:T(8,128)(2,1)S(1)}, bf16[8,8,8,128]{3,2,1,0:T(8,128)(2,...) fusion(bf16[34,18,18,128]{3,2,1,0:T(8,128)(2,1)} %get-tuple-ele, ...), kind=kLoop, calls=%fused_computation.121.clone.1 | loop fusion | bytes 7077924 | tf_op jit(solution)/shard_map/while/body/eval_jaxpr/slice | solution.py:43
  236.5 4.4 copy.28
  246.7 6.1 %select_maximum_fusion = bf16[34,18,18,128]{3,2,1,0:T(8,128)(2,1)} fusion(bf16[34,1,16,128]{3,2,1,0:T(8,128)(2,1)} %collective-permute-done.7, bf16[34,1,16,128]{3,2,1,0:T(8,128)(2,1)} %collective-permute-done.6, bf16[1,16,16,128]{3,2,1,0:T(8,128)(2,1)} %copy-done.10, bf16[32,16,16,128]{3,2,1,0:T(8,128)(2,1)} %bitcast.274, ...), kind=kLoop, calls=%fused_computation.127 | loop fusion | flops 25380864 | bytes 5326848 | tf_op jit(solution)/shard_map/concatenate | solution.py:23
  253.0 108.7 %while.29 = (s32[]{:T(128)}, bf16[8,512,128]{2,1,0:T(8,128)(2,1)S(1)}, s32[8]{0:T(128)S(1)}, s32[8]{0:T(128)S(1)}, bf16[34,18,18,128]{3,2,1,0:T(8,128)(2,1)}, /*...) while((s32[]{:T(128)}, ...), condition=%wide.region_3.4_spmd, body=%wide.region_2.3_spmd.sunk | while | flops 453116480 | bytes 18715932 | solution.py:118
  256.8 7.3 %constant_dynamic-slice_fusion.56 = (bf16[8,8,8,128]{3,2,1,0:T(8,128)(2,1)S(1)}, bf16[8,8,8,128]{3,2,1,0:T(8,128)(2,1)S(1)}, bf16[8,8,8,128]{3,2,1,0:T(8,128)(2,...) fusion(bf16[34,18,18,128]{3,2,1,0:T(8,128)(2,1)} %get-tuple-ele, ...), kind=kLoop, calls=%fused_computation.58.clone.1 | loop fusion | bytes 7077924 | tf_op jit(solution)/shard_map/while/body/eval_jaxpr/slice | solution.py:43
  270.2 8.0 %constant_dynamic-slice_fusion.56 = (bf16[8,8,8,128]{3,2,1,0:T(8,128)(2,1)S(1)}, bf16[8,8,8,128]{3,2,1,0:T(8,128)(2,1)S(1)}, bf16[8,8,8,128]{3,2,1,0:T(8,128)(2,...) fusion(bf16[34,18,18,128]{3,2,1,0:T(8,128)(2,1)} %get-tuple-ele, ...), kind=kLoop, calls=%fused_computation.58.clone.1 | loop fusion | bytes 7077924 | tf_op jit(solution)/shard_map/while/body/eval_jaxpr/slice | solution.py:43
  284.3 8.2 %constant_dynamic-slice_fusion.56 = (bf16[8,8,8,128]{3,2,1,0:T(8,128)(2,1)S(1)}, bf16[8,8,8,128]{3,2,1,0:T(8,128)(2,1)S(1)}, bf16[8,8,8,128]{3,2,1,0:T(8,128)(2,...) fusion(bf16[34,18,18,128]{3,2,1,0:T(8,128)(2,1)} %get-tuple-ele, ...), kind=kLoop, calls=%fused_computation.58.clone.1 | loop fusion | bytes 7077924 | tf_op jit(solution)/shard_map/while/body/eval_jaxpr/slice | solution.py:43
  298.5 8.9 %constant_dynamic-slice_fusion.56 = (bf16[8,8,8,128]{3,2,1,0:T(8,128)(2,1)S(1)}, bf16[8,8,8,128]{3,2,1,0:T(8,128)(2,1)S(1)}, bf16[8,8,8,128]{3,2,1,0:T(8,128)(2,...) fusion(bf16[34,18,18,128]{3,2,1,0:T(8,128)(2,1)} %get-tuple-ele, ...), kind=kLoop, calls=%fused_computation.58.clone.1 | loop fusion | bytes 7077924 | tf_op jit(solution)/shard_map/while/body/eval_jaxpr/slice | solution.py:43
  313.5 7.2 %constant_dynamic-slice_fusion.56 = (bf16[8,8,8,128]{3,2,1,0:T(8,128)(2,1)S(1)}, bf16[8,8,8,128]{3,2,1,0:T(8,128)(2,1)S(1)}, bf16[8,8,8,128]{3,2,1,0:T(8,128)(2,...) fusion(bf16[34,18,18,128]{3,2,1,0:T(8,128)(2,1)} %get-tuple-ele, ...), kind=kLoop, calls=%fused_computation.58.clone.1 | loop fusion | bytes 7077924 | tf_op jit(solution)/shard_map/while/body/eval_jaxpr/slice | solution.py:43
  326.7 6.8 %constant_dynamic-slice_fusion.56 = (bf16[8,8,8,128]{3,2,1,0:T(8,128)(2,1)S(1)}, bf16[8,8,8,128]{3,2,1,0:T(8,128)(2,1)S(1)}, bf16[8,8,8,128]{3,2,1,0:T(8,128)(2,...) fusion(bf16[34,18,18,128]{3,2,1,0:T(8,128)(2,1)} %get-tuple-ele, ...), kind=kLoop, calls=%fused_computation.58.clone.1 | loop fusion | bytes 7077924 | tf_op jit(solution)/shard_map/while/body/eval_jaxpr/slice | solution.py:43
  339.7 6.8 %constant_dynamic-slice_fusion.56 = (bf16[8,8,8,128]{3,2,1,0:T(8,128)(2,1)S(1)}, bf16[8,8,8,128]{3,2,1,0:T(8,128)(2,1)S(1)}, bf16[8,8,8,128]{3,2,1,0:T(8,128)(2,...) fusion(bf16[34,18,18,128]{3,2,1,0:T(8,128)(2,1)} %get-tuple-ele, ...), kind=kLoop, calls=%fused_computation.58.clone.1 | loop fusion | bytes 7077924 | tf_op jit(solution)/shard_map/while/body/eval_jaxpr/slice | solution.py:43
  352.6 6.8 %constant_dynamic-slice_fusion.56 = (bf16[8,8,8,128]{3,2,1,0:T(8,128)(2,1)S(1)}, bf16[8,8,8,128]{3,2,1,0:T(8,128)(2,1)S(1)}, bf16[8,8,8,128]{3,2,1,0:T(8,128)(2,...) fusion(bf16[34,18,18,128]{3,2,1,0:T(8,128)(2,1)} %get-tuple-ele, ...), kind=kLoop, calls=%fused_computation.58.clone.1 | loop fusion | bytes 7077924 | tf_op jit(solution)/shard_map/while/body/eval_jaxpr/slice | solution.py:43
  361.7 151.2 %all-reduce.4.cloned.1.call-done = f32[27,128,128]{2,1,0:T(8,128)} async-done(((f32[27,128,128]{2,1,0:T(8,128)}), f32[27,128,128]{2,1,0:T(8,128)}) %all-reduce.4.cloned.1.call-update) | async-done | bytes 1769488 | tf_op jit(solution)/shard_map/psum | solution.py:109
  (608 shorter events, 128.5 us)
Async XLA Ops:
  7.2 4.3 copy-start.12
  7.2 505.7 %all-reduce.4.cloned.1.call-start = ((), (), s32[]{:S(2)}) async-start(), calls=%async_computation | async-start | bytes 3538944 | tf_op jit(solution)/shard_map/psum | solution.py:109
  11.5 7.5 %copy-start.5 = (bf16[8,512,128]{2,1,0:T(8,128)(2,1)}, bf16[8,512,128]{2,1,0:T(8,128)(2,1)S(1)}, u32[]{:S(2)}) copy-start(bf16[8,512,128]{2,1,0:T(8,128)(2,1)S(1)} %get-tuple-element.615) | copy-start | bytes 3145732
  13.1 13.5 %copy-start.3 = (bf16[4,2,2,8,8,8,128]{6,5,2,4,1,3,0:T(8,128)(2,1)}, bf16[4,2,2,8,8,8,128]{6,5,2,4,1,3,0:T(8,128)(2,1)S(1)}, u32[]{:S(2)}) copy-start(bf16[4,2,2,8,8,8,128]{6,5,2,4,1,3,0:T(8,128)(2,1)S(1)} %copy.12) | copy-start | bytes 6291460
  13.1 13.5 %collective-permute-start.1 = (bf16[1,16,16,128]{3,2,1,0:T(8,128)(2,1)S(1)}, bf16[1,16,16,128]{3,2,1,0:T(8,128)(2,1)S(1)}, u32[]{:S(2)}, u32[]{:S(2)}) collective-permute-start(bf16[1,16,16,128]{3,2,1,0:T(8,128)(2,1)S(1)} %get-tuple-element.400), channel_id=1, source_target_pairs={{4,0},{8,4},{12,8},{16,12},{20,16},{24,20},{28,24},{32,28},{36,32}... | collective-permute-start | bytes 196616 | tf_op jit(solution)/shard_map/ppermute | solution.py:22
  14.4 12.2 %collective-permute-start = (bf16[1,16,16,128]{3,2,1,0:T(8,128)(2,1)S(1)}, bf16[1,16,16,128]{3,2,1,0:T(8,128)(2,1)S(1)}, u32[]{:S(2)}, u32[]{:S(2)}) collective-permute-start(bf16[1,16,16,128]{3,2,1,0:T(8,128)(2,1)S(1)} %get-tuple-element.399), channel_id=1, source_target_pairs={{0,4},{4,8},{8,12},{12,16},{16,20},{20,24},{24,28},{28,32},{32,36}... | collective-permute-start | bytes 196616 | tf_op jit(solution)/shard_map/ppermute | solution.py:21
  20.2 14.8 %copy-start.7 = (bf16[27,128,128]{2,1,0:T(8,128)(2,1)S(1)}, bf16[27,128,128]{2,1,0:T(8,128)(2,1)}, u32[]{:S(2)}) copy-start(bf16[27,128,128]{2,1,0:T(8,128)(2,1)} %param.10) | copy-start | bytes 2654212
  20.6 16.9 %copy-start.2 = (bf16[4,8,2,8,2,8,128]{6,5,4,3,2,1,0:T(8,128)(2,1)}, bf16[4,8,2,8,2,8,128]{6,5,4,3,2,1,0:T(8,128)(2,1)S(1)}, u32[]{:S(2)}) copy-start(bf16[4,8,2,8,2,8,128]{6,5,4,3,2,1,0:T(8,128)(2,1)S(1)} %copy.13) | copy-start | bytes 6291460
  21.3 15.4 %collective-permute-start.5 = (bf16[1,16,16,128]{3,2,1,0:T(8,128)(2,1)}, bf16[1,16,16,128]{3,2,1,0:T(8,128)(2,1)S(1)}, u32[]{:S(2)}, u32[]{:S(2)}) collective-permute-start(bf16[1,16,16,128]{3,2,1,0:T(8,128)(2,1)} %get-tuple-element.398), channel_id=1, source_target_pairs={{4,0},{8,4},{12,8},{16,12},{20,16},{24,20},{28,24},{32,28},{36,32}... | collective-permute-start | bytes 196616 | tf_op jit(solution)/shard_map/ppermute | solution.py:22
  22.6 14.1 %collective-permute-start.4 = (bf16[1,16,16,128]{3,2,1,0:T(8,128)(2,1)}, bf16[1,16,16,128]{3,2,1,0:T(8,128)(2,1)S(1)}, u32[]{:S(2)}, u32[]{:S(2)}) collective-permute-start(bf16[1,16,16,128]{3,2,1,0:T(8,128)(2,1)} %get-tuple-element.397), channel_id=1, source_target_pairs={{0,4},{4,8},{8,12},{12,16},{16,20},{20,24},{24,28},{28,32},{32,36}... | collective-permute-start | bytes 196616 | tf_op jit(solution)/shard_map/ppermute | solution.py:21
  27.4 16.0 %collective-permute-start.3 = (bf16[34,1,16,128]{3,2,1,0:T(8,128)(2,1)}, bf16[34,1,16,128]{3,2,1,0:T(8,128)(2,1)S(1)}, u32[]{:S(2)}, u32[]{:S(2)}) collective-permute-start(bf16[34,1,16,128]{3,2,1,0:T(8,128)(2,1)} %get-tuple-element.396), channel_id=1, source_target_pairs={{1,0},{2,1},{3,2},{5,4},{6,5},{7,6},{9,8},{10,9},{11,10},{13,12},{... | collective-permute-start | bytes 417800 | tf_op jit(solution)/shard_map/ppermute | solution.py:22
  33.0 10.3 %collective-permute-start.2 = (bf16[34,1,16,128]{3,2,1,0:T(8,128)(2,1)S(1)}, bf16[34,1,16,128]{3,2,1,0:T(8,128)(2,1)}, u32[]{:S(2)}, u32[]{:S(2)}) collective-permute-start(bf16[34,1,16,128]{3,2,1,0:T(8,128)(2,1)S(1)} %get-tuple-element.395), channel_id=1, source_target_pairs={{0,1},{1,2},{2,3},{4,5},{5,6},{6,7},{8,9},{9,10},{10,11},{12,13},{... | collective-permute-start | bytes 417800 | tf_op jit(solution)/shard_map/ppermute | solution.py:21
  36.7 6.7 %copy-start.4 = (bf16[4,2,2,8,8,8,128]{6,5,2,4,1,3,0:T(8,128)(2,1)S(1)}, bf16[4,2,2,8,8,8,128]{6,5,2,4,1,3,0:T(8,128)(2,1)}, u32[]{:S(2)}) copy-start(bf16[4,2,2,8,8,8,128]{6,5,2,4,1,3,0:T(8,128)(2,1)} %copy-done.3) | copy-start | bytes 6291460
  36.7 12.2 %copy-start.10 = (bf16[1,16,16,128]{3,2,1,0:T(8,128)(2,1)}, bf16[1,16,16,128]{3,2,1,0:T(8,128)(2,1)S(1)}, u32[]{:S(2)}) copy-start(bf16[1,16,16,128]{3,2,1,0:T(8,128)(2,1)S(1)} %collective-permute-done.5) | copy-start | bytes 196612
  36.7 12.2 %copy-start.11 = (bf16[1,16,16,128]{3,2,1,0:T(8,128)(2,1)}, bf16[1,16,16,128]{3,2,1,0:T(8,128)(2,1)S(1)}, u32[]{:S(2)}) copy-start(bf16[1,16,16,128]{3,2,1,0:T(8,128)(2,1)S(1)} %collective-permute-done.4) | copy-start | bytes 196612
  37.5 209.2 %collective-permute-start.7 = (bf16[34,1,16,128]{3,2,1,0:T(8,128)(2,1)}, bf16[34,1,16,128]{3,2,1,0:T(8,128)(2,1)}, u32[]{:S(2)}, u32[]{:S(2)}) collective-permute-start(bf16[34,1,16,128]{3,2,1,0:T(8,128)(2,1)} %get-tuple-element.394), channel_id=1, source_target_pairs={{1,0},{2,1},{3,2},{5,4},{6,5},{7,6},{9,8},{10,9},{11,10},{13,12},{... | collective-permute-start | bytes 417800 | tf_op jit(solution)/shard_map/ppermute | solution.py:22
  40.6 206.1 %collective-permute-start.6 = (bf16[34,1,16,128]{3,2,1,0:T(8,128)(2,1)}, bf16[34,1,16,128]{3,2,1,0:T(8,128)(2,1)}, u32[]{:S(2)}, u32[]{:S(2)}) collective-permute-start(bf16[34,1,16,128]{3,2,1,0:T(8,128)(2,1)} %get-tuple-element.393), channel_id=1, source_target_pairs={{0,1},{1,2},{2,3},{4,5},{5,6},{6,7},{8,9},{9,10},{10,11},{12,13},{... | collective-permute-start | bytes 417800 | tf_op jit(solution)/shard_map/ppermute | solution.py:21
  93.3 4.0 copy-start.1
  93.3 4.0 copy-start.8
  118.6 4.0 copy-start.1
  118.6 4.0 copy-start.8
  144.6 4.0 copy-start.1
  144.6 4.0 copy-start.8
  168.9 4.0 copy-start.1
  192.9 4.0 copy-start.1
  192.9 4.0 copy-start.8
  216.9 4.0 copy-start.1
  216.9 4.0 copy-start.8
  240.9 4.0 copy-start.1
  240.9 4.0 copy-start.8
  246.7 6.3 %copy-start.9 = (bf16[27,128,128]{2,1,0:T(8,128)(2,1)S(1)}, bf16[27,128,128]{2,1,0:T(8,128)(2,1)}, u32[]{:S(2)}) copy-start(bf16[27,128,128]{2,1,0:T(8,128)(2,1)} %copy.14) | copy-start | bytes 2654212
  361.7 154.1 %copy-start.6 = (bf16[8,512,128]{2,1,0:T(8,128)(2,1)}, bf16[8,512,128]{2,1,0:T(8,128)(2,1)S(1)}, u32[]{:S(2)}) copy-start(bf16[8,512,128]{2,1,0:T(8,128)(2,1)S(1)} %get-tuple-element.272) | copy-start | bytes 3145732
  (11 other events, 25.1 us)
Sparse Core Ops, SparseCore 0:
  246.8 266.0 all-reduce.3
where the time goes:
time: 525 us; the launch traced here: 523 us
  local copies, waits for them, and re-layouts  209 us (40%)
  waiting for transfers between devices  151 us (29%)
  matrix products  55.7 us (11%)
  loops' own time  47.4 us (9%)
  starting transfers between devices  24.6 us (5%)
  other arithmetic  20.4 us (4%)
  between operations  14.4 us (3%)
    psum x1, waiting for transfers between devices, shards(): grad_weight = lax.psum(local_grad, ('gx', 'gy')) * scale  151 us
    slice x16, local copies, waits for them, and re-layouts, brick_patches(): block[along_x + 1:along_x + 1 + BRICK, along_y + 1:along_y + 1 + BRICK, a...  120 us
    dot_general x8, local copies, waits for them, and re-layouts, forward_step(): jnp.einsum('vk,vc->kc', patches, masked_cot[slot_index], preferred_elemen...  35 us
    dot_general x8, matrix products, forward_step(): jnp.einsum('vk,vc->kc', patches, masked_cot[slot_index], preferred_elemen...  31.3 us
    while x464, local copies, waits for them, and re-layouts  28.1 us
    another operation x1, loops' own time, shards(): lax.scan(make_forward(), jnp.zeros((27, channels, channels), jnp.float32)...  24.3 us
    another operation x1, loops' own time, shards(): lax.scan(backward_step, jnp.zeros((), jnp.float32), slot_ids)  23.1 us
    dot_general x8, matrix products, forward_step(): total = jnp.dot(patches, w_forward, preferred_element_type=jnp.float32)  14 us
  transfers between devices with their start and end apart: 9, of which 1 were waited for; matrix products, arithmetic and copies ran while one was open for 50% of the time, Pallas kernels for 0%

commit v1 on v0

v1 whole, which is shorter than its diff:
```python
import itertools
import math

import jax
import jax.numpy as jnp
from jax import lax
from jax.experimental import pallas as pl
from jax.experimental.pallas import tpu as pltpu
from jax.sharding import Mesh, PartitionSpec as P

AXES = ("y_hi", "z", "x", "y_lo", "core")
SLOTS = 8
VOX = 512
CH = 128
NX, NY, NZ = 32, 16, 16
OFFSETS = 27
KROW = 9 * CH
BLOCKS = 16
BROWS = 112
F32 = jnp.float32
BF16 = jnp.bfloat16
VMEM = pl.BlockSpec(memory_space=pltpu.VMEM)
SMEM = pl.BlockSpec(memory_space=pltpu.SMEM)


def brick_of(pos):
    return pos >> 2, (pos >> 1) & 1, pos & 1


def mask_columns(occ_ref):
    return jnp.where(occ_ref[...] == 1, 1.0, 0.0).astype(F32).T


def place_kernel(pos_ref, occ_ref, feat_ref, cot_ref, xg_ref, cg_ref, lo_ref, hi_ref, yl_ref, yh_ref, xt_ref, cells):
    columns = mask_columns(occ_ref)
    for t, (src, dst) in enumerate(((cot_ref, cg_ref), (feat_ref, xg_ref))):

        def clear(x, carry):
            cells[x] = jnp.zeros((NY, 2, 8, CH), F32)
            return carry

        lax.fori_loop(0, NX, clear, 0)
        for s in range(SLOTS):
            pos = pos_ref[s]

            @pl.when(pos >= 0)
            def _():
                bx, by, bz = brick_of(pos)
                keep = jnp.broadcast_to(columns[:, s : s + 1], (VOX, CH))
                value = jnp.where(keep > 0.5, src[s].astype(F32), 0.0)
                cells[pl.ds(bx * 8, 8), pl.ds(by * 8, 8), bz] = value.reshape(8, 8, 8, CH)
                if t == 1:
                    xt_ref[s] = value.T.astype(BF16)

        def emit(x, carry):
            dst[x] = cells[x].reshape(NY, NZ, CH).astype(BF16)
            return carry

        lax.fori_loop(0, NX, emit, 0)
        lo_ref[t] = dst[0]
        hi_ref[t] = dst[NX - 1]
        yl_ref[t] = dst[:, 0]
        yh_ref[t] = dst[:, NY - 1]


def place(slot_pos, occupancy, features, cotangent):
    plane = jax.ShapeDtypeStruct((2, NY, NZ, CH), BF16)
    side = jax.ShapeDtypeStruct((2, NX, NZ, CH), BF16)
    grid = jax.ShapeDtypeStruct((NX, NY, NZ, CH), BF16)
    return pl.pallas_call(
        place_kernel,
        out_shape=(grid, grid, plane, plane, side, side, jax.ShapeDtypeStruct((SLOTS, CH, VOX), BF16)),
        in_specs=[SMEM, VMEM, VMEM, VMEM],
        out_specs=(VMEM,) * 7,
        scratch_shapes=[pltpu.VMEM((NX, NY, 2, 8, CH), F32)],
        compiler_params=pltpu.CompilerParams(vmem_limit_bytes=32 << 20),
        name="place",
    )(slot_pos, occupancy, features, cotangent)


def assemble(grid_ref, xlo_ref, xhi_ref, ylo_ref, yhi_ref, halo):
    def shifted(v):
        n = v.shape[0]
        flat = v.astype(F32).reshape(n * NZ, CH)
        z = lax.broadcasted_iota(jnp.int32, flat.shape, 0) & (NZ - 1)
        back = jnp.where(z == 0, 0.0, pltpu.roll(flat, 1, axis=0))
        ahead = jnp.where(z == NZ - 1, 0.0, pltpu.roll(flat, n * NZ - 1, axis=0))
        return [a.reshape(n, 2, 8, CH) for a in (back, flat, ahead)]

    def put_plane(x, v):
        for r, a in enumerate(shifted(v)):
            for bz in range(2):
                halo[r, bz, x, pl.ds(1, NY)] = a[:, bz]

    def body(x, carry):
        put_plane(x + 1, grid_ref[x])
        return carry

    lax.fori_loop(0, NX, body, 0)
    put_plane(0, xlo_ref[...])
    put_plane(NX + 1, xhi_ref[...])
    for y, ref in ((0, ylo_ref), (NY + 1, yhi_ref)):
        for r, a in enumerate(shifted(ref[...])):
            for bz in range(2):
                halo[r, bz, :, y] = a[:, bz]


def build_patches(pos, halo, patch_ref):
    bx, by, bz = brick_of(pos)
    for x in range(10):
        for q in range(3):
            for r in range(3):
                rows = halo[r, bz, bx * 8 + x, pl.ds(by * 8 + q, 8)]
                k = (q * 3 + r) * CH
                patch_ref[0, x, :, k : k + CH] = rows.reshape(64, CH).astype(BF16)


def patch_rows(patch_ref, p):
    return patch_ref[0, pl.ds(p, 8)].reshape(VOX, KROW)


def patches_kernel(pos_ref, grid_ref, xlo_ref, xhi_ref, ylo_ref, yhi_ref, patch_ref, halo):
    s = pl.program_id(0)

    @pl.when(s == 0)
    def _():
        assemble(grid_ref, xlo_ref, xhi_ref, ylo_ref, yhi_ref, halo)

    pos = pos_ref[s]

    @pl.when(pos >= 0)
    def _():
        build_patches(pos, halo, patch_ref)


def weight_kernel(pos_ref, meta_ref, grid_ref, xlo_ref, xhi_ref, ylo_ref, yhi_ref, xt_ref, patch_ref, keep_ref, send_ref, halo, total):
    s = pl.program_id(0)

    @pl.when(s == 0)
    def _():
        assemble(grid_ref, xlo_ref, xhi_ref, ylo_ref, yhi_ref, halo)

        def clear(o, carry):
            total[pl.ds(pl.multiple_of(o * CH, CH), CH)] = jnp.zeros((CH, CH), F32)
            return carry

        lax.fori_loop(0, OFFSETS + 1, clear, 0)

    pos = pos_ref[s]

    @pl.when(pos >= 0)
    def _():
        build_patches(pos, halo, patch_ref)
        for p in range(3):
            terms = jnp.dot(xt_ref[0], patch_rows(patch_ref, p), preferred_element_type=F32)
            for k in range(9):
                row = (OFFSETS - 1 - (p * 9 + k)) * CH
                total[row : row + CH] += terms[:, k * CH : (k + 1) * CH]

    @pl.when(s == SLOTS - 1)
    def _():
        core, own, other = meta_ref[0], meta_ref[1], meta_ref[2]

        def emit(j, carry):
            at = pl.multiple_of((core * BLOCKS + (j ^ own)) * BROWS, 8)
            keep_ref[j] = total[pl.ds(at, BROWS)]
            at = pl.multiple_of(((1 - core) * BLOCKS + (j ^ other)) * BROWS, 8)
            send_ref[j] = total[pl.ds(at, BROWS)]
            return carry

        lax.fori_loop(0, BLOCKS, emit, 0)


PATCH_SHAPE = jax.ShapeDtypeStruct((SLOTS, 10, 64, KROW), BF16)
PATCH_SPEC = pl.BlockSpec((1, 10, 64, KROW), lambda s, *_: (s, 0, 0, 0))
HALO = pltpu.VMEM((3, 2, NX + 2, NY + 2, 8, CH), F32)


def patches(slot_pos, grid, faces):
    return pl.pallas_call(
        patches_kernel,
        out_shape=PATCH_SHAPE,
        grid=(SLOTS,),
        in_specs=[SMEM] + [VMEM] * 5,
        out_specs=PATCH_SPEC,
        scratch_shapes=[HALO],
        compiler_params=pltpu.CompilerParams(vmem_limit_bytes=40 << 20),
        cost_estimate=pl.CostEstimate(flops=0, bytes_accessed=30 << 20, transcendentals=0),
        name="patches",
    )(slot_pos, grid, *faces)


def weight_gradient(slot_pos, meta, grid, faces, xt):
    half = jax.ShapeDtypeStruct((BLOCKS, BROWS, CH), F32)
    return pl.pallas_call(
        weight_kernel,
        out_shape=(PATCH_SHAPE, half, half),
        grid=(SLOTS,),
        in_specs=[SMEM, SMEM] + [VMEM] * 5 + [pl.BlockSpec((1, CH, VOX), lambda s: (s, 0, 0))],
        out_specs=(PATCH_SPEC, VMEM, VMEM),
        scratch_shapes=[HALO, pltpu.VMEM(((OFFSETS + 1) * CH, CH), F32)],
        compiler_params=pltpu.CompilerParams(vmem_limit_bytes=48 << 20),
        cost_estimate=pl.CostEstimate(flops=2 * 4096 * OFFSETS * CH * CH, bytes_accessed=30 << 20, transcendentals=0),
        name="weight_gradient",
    )(slot_pos, meta, grid, *faces, xt)


def conv_kernel(first, pos_ref, occ_ref, patch_ref, w_ref, *rest):
    out_ref = rest[-1]
    s = first + pl.program_id(0)
    pos = pos_ref[s]

    @pl.when(pos >= 0)
    def _():
        columns = mask_columns(occ_ref)
        total = jnp.dot(patch_rows(patch_ref, 0), w_ref[:KROW], preferred_element_type=F32)
        for p in range(1, 3):
            total += jnp.dot(patch_rows(patch_ref, p), w_ref[p * KROW : (p + 1) * KROW], preferred_element_type=F32)
        lane = lax.broadcasted_iota(jnp.int32, columns.shape, 1)
        keep = jnp.sum(jnp.where(lane == s, columns, 0.0), axis=1, keepdims=True)
        out_ref[0] = jnp.where(jnp.broadcast_to(keep, (VOX, CH)) > 0.5, total, 0.0).astype(BF16)

    @pl.when(pos < 0)
    def _():
        out_ref[0] = jnp.zeros((VOX, CH), BF16)


def convolve(slot_pos, occupancy, patch, weights, out, first, count):
    aliased = {} if out is None else {4: 0}
    extra = () if out is None else (out,)
    return pl.pallas_call(
        lambda *refs: conv_kernel(first, *refs),
        out_shape=jax.ShapeDtypeStruct((SLOTS, VOX, CH), BF16),
        grid=(count,),
        in_specs=[SMEM, VMEM, pl.BlockSpec((1, 10, 64, KROW), lambda i: (first + i, 0, 0, 0)), VMEM]
        + [pl.BlockSpec(memory_space=pl.ANY)] * len(extra),
        out_specs=pl.BlockSpec((1, VOX, CH), lambda i: (first + i, 0, 0)),
        input_output_aliases=aliased,
        compiler_params=pltpu.CompilerParams(vmem_limit_bytes=16 << 20),
        cost_estimate=pl.CostEstimate(flops=count * 4 * VOX * OFFSETS * CH * CH, bytes_accessed=count << 20, transcendentals=0),
        name="convolve",
    )(slot_pos, occupancy, patch, weights, *extra)


def finish_kernel(meta_ref, own_ref, other_ref, out_ref, rows):
    core, own, other = meta_ref[0], meta_ref[1], meta_ref[2]

    def place_block(j, carry):
        at = pl.multiple_of((core * BLOCKS + (j ^ own)) * BROWS, 8)
        rows[pl.ds(at, BROWS)] = own_ref[j]
        at = pl.multiple_of(((1 - core) * BLOCKS + (j ^ other)) * BROWS, 8)
        rows[pl.ds(at, BROWS)] = other_ref[j]
        return carry

    lax.fori_loop(0, BLOCKS, place_block, 0)
    scale = 1.0 / math.sqrt(float(256 * SLOTS * VOX))

    def emit(o, carry):
        out_ref[o] = rows[pl.ds(pl.multiple_of(o * CH, CH), CH)] * scale
        return carry

    lax.fori_loop(0, OFFSETS, emit, 0)


def finish(meta, own, other):
    return pl.pallas_call(
        finish_kernel,
        out_shape=jax.ShapeDtypeStruct((OFFSETS, CH, CH), F32),
        in_specs=[SMEM, VMEM, VMEM],
        out_specs=VMEM,
        scratch_shapes=[pltpu.VMEM(((OFFSETS + 1) * CH, CH), F32)],
        compiler_params=pltpu.CompilerParams(vmem_limit_bytes=24 << 20),
        name="finish",
    )(meta, own, other)


def make_shards(sizes):
    everyone = list(itertools.product(*[range(n) for n in sizes]))
    n_y_lo, n_core = sizes[3], sizes[4]
    narrow = n_y_lo * n_core
    wide = len(everyone) // narrow

    def number(at):
        flat = 0
        for a, n in zip(at, sizes):
            flat = flat * n + a
        return flat

    def mate(at, axis, k):
        y_hi, z, x, y_lo, core = at
        if isinstance(axis, tuple):
            axis = axis[core]
        y = y_hi * n_y_lo + y_lo
        if axis == "core":
            core ^= k
        elif axis == "x":
            x ^= k
        elif axis == "y":
            y ^= k
        else:
            z ^= k
        return (y // n_y_lo, z, x, y % n_y_lo, core)

    def swap(value, axis, k):
        return lax.ppermute(value, AXES, [(number(a), number(mate(a, axis, k))) for a in everyone])

    def shift_wide(value, step):
        pairs = [(i * narrow + j, (i + step) * narrow + j) for i in range(wide) for j in range(narrow) if 0 <= i + step < wide]
        return lax.ppermute(value, AXES, pairs)

    def shift_narrow(value, step):
        pairs = [(i * narrow + j, i * narrow + j + step) for i in range(wide) for j in range(narrow) if 0 <= j + step < narrow]
        return lax.ppermute(value, AXES, pairs)

    first, second = ("y", "x"), ("x", "y")

    def scatter(value, axis):
        n = value.shape[0] // 4
        parts = [swap(value[k * n : (k + 1) * n], axis, k) for k in (2, 1, 3)]
        return value[:n] + parts[0] + parts[1] + parts[2]

    def gather(value, axis):
        got = {k: swap(value, axis, k) for k in (2, 1, 3)}
        return jnp.concatenate([value, got[1], got[2], got[3]], axis=0)

    def double(value, axis, ks):
        total = value
        for part in [swap(value, axis, k) for k in ks]:
            total = total + part
        return total

    def shards(features, weights, cotangent, occupancy, slot_pos):
        core = lax.axis_index("core")
        x_at = lax.axis_index("x")
        y_at = lax.axis_index("y_hi") * n_y_lo + lax.axis_index("y_lo")
        yx, xy = y_at * 4 + x_at, x_at * 4 + y_at
        meta = jnp.stack([core, jnp.where(core == 0, yx, xy), jnp.where(core == 0, xy, yx)]).astype(jnp.int32)
        xg, cg, lo, hi, side_lo, side_hi, xt = place(slot_pos, occupancy, features, cotangent)
        before = shift_wide(hi, 1)
        after = shift_wide(lo, -1)
        rim_hi = jnp.concatenate([before[:, None, NY - 1], side_hi, after[:, None, NY - 1]], axis=1)
        rim_lo = jnp.concatenate([before[:, None, 0], side_lo, after[:, None, 0]], axis=1)
        left = shift_narrow(rim_hi, 1)
        right = shift_narrow(rim_lo, -1)
        cot_faces = (before[0], after[0], left[0], right[0])
        in_faces = (before[1], after[1], left[1], right[1])
        cot_patch, keep, send = weight_gradient(slot_pos, meta, cg, cot_faces, xt)
        in_patch = patches(slot_pos, xg, in_faces)
        w_forward = weights.reshape(OFFSETS * CH, CH)
        w_backward = weights[::-1].transpose(0, 2, 1).reshape(OFFSETS * CH, CH)

        total = keep + swap(send, "core", 1)
        total = scatter(total, first)
        total = scatter(total, second)
        total = double(total, "z", (2, 1, 3))
        total = double(total, "z", (4,))
        total = gather(total, second)
        total = gather(total, first)
        grad_weight = finish(meta, total, swap(total, "core", 1))

        outputs = grad_input = None
        for s in range(0, SLOTS, 2):
            outputs = convolve(slot_pos, occupancy, in_patch, w_forward, outputs, s, 2)
        for s in range(0, SLOTS, 2):
            grad_input = convolve(slot_pos, occupancy, cot_patch, w_backward, grad_input, s, 2)
        return outputs, grad_input, grad_weight

    return shards


def solution(mesh):
    sizes = (2, 8, 4, 2, 2)
    fine = Mesh(mesh.devices.reshape(sizes), AXES)
    return jax.shard_map(
        make_shards(sizes),
        mesh=fine,
        in_specs=(P(AXES, None, None), P(), P(AXES, None, None), P(AXES, None), P(AXES)),
        out_specs=(P(AXES, None, None), P(AXES, None, None), P()),
        check_vma=False,
    )
```

time: 525 us -> 143 us (0.27)
  local copies, waits for them, and re-layouts: 209 us -> 10.4 us
  waiting for transfers between devices: 151 us -> 29 us
  matrix products: 55.7 us -> 0 us
  loops' own time: 47.4 us -> 0 us
  Pallas kernels: 0 us -> 43.9 us
  starting transfers between devices: 24.6 us -> 58.5 us
  other arithmetic: 20.4 us -> 0.38 us
  between operations: 14.4 us -> 0.96 us
    psum x1 -> x0, waiting for transfers between devices: 151 us -> none  [shards(): grad_weight = lax.psum(local_grad, ('gx', 'gy')) * scale]
    slice x18 -> x4, local copies, waits for them, and re-layouts: 121 us -> 0.06 us  [the longest x2 0.06 us: scatter(): parts = [swap(value[k * n:(k + 1) * n], axis, k) for k in (2, 1, 3)]]
    dot_general x26 -> x0, matrix products: 55.7 us -> none  [the longest x8 31.3 us: forward_step(): jnp.einsum('vk,vc->kc', patches, masked_cot[slot_index], preferred_elemen...]
    another operation x2 -> x0, loops' own time: 47.4 us -> none  [the longest x1 24.3 us: shards(): lax.scan(make_forward(), jnp.zeros((27, channels, channels), jnp.float32)...]
    pallas_call x0 -> x12, Pallas kernels: none -> 43.9 us  [the longest x8 23.1 us: convolve(): pl.pallas_call(lambda *refs: conv_kernel(first, *refs), out_shape=jax.Sha...]
    dot_general x8 -> x0, local copies, waits for them, and re-layouts: 35 us -> none  [forward_step(): jnp.einsum('vk,vc->kc', patches, masked_cot[slot_index], preferred_elemen...]
    ppermute x8 -> x22, starting transfers between devices: 24.6 us -> 58.5 us  [the longest x18 45.2 us: swap(): lax.ppermute(value, AXES, [(number(a), number(mate(a, axis, k))) for a in...]
    ppermute x8 -> x22, waiting for transfers between devices: 0.02 us -> 29 us  [the longest x18 21.3 us: swap(): lax.ppermute(value, AXES, [(number(a), number(mate(a, axis, k))) for a in...]
  transfers between devices with their start and end apart: 9 -> 22, of which waited for: 1 -> 15; matrix products, arithmetic and copies ran while one was open for 50% -> 1% of each run, Pallas kernels for 0% -> 19%
where the time goes in v1:
time: 143 us
  starting transfers between devices  58.5 us (41%)
  Pallas kernels  43.9 us (31%)
  waiting for transfers between devices  29 us (20%)
  local copies, waits for them, and re-layouts  10.4 us (7%)
    ppermute x18, starting transfers between devices, swap(): lax.ppermute(value, AXES, [(number(a), number(mate(a, axis, k))) for a in...  45.2 us
    pallas_call x8, Pallas kernels, convolve(): pl.pallas_call(lambda *refs: conv_kernel(first, *refs), out_shape=jax.Sha...  23.1 us
    ppermute x18, waiting for transfers between devices, swap(): lax.ppermute(value, AXES, [(number(a), number(mate(a, axis, k))) for a in...  21.3 us
    pallas_call x1, Pallas kernels, weight_gradient(): pl.pallas_call(weight_kernel, out_shape=(PATCH_SHAPE, half, half), grid=(...  10.7 us
    unnamed x33, local copies, waits for them, and re-layouts  8.93 us
    ppermute x2, starting transfers between devices, shift_narrow(): return lax.ppermute(value, AXES, pairs)  7.12 us
    ppermute x2, starting transfers between devices, shift_wide(): return lax.ppermute(value, AXES, pairs)  6.2 us
    ppermute x2, waiting for transfers between devices, shift_narrow(): return lax.ppermute(value, AXES, pairs)  5.89 us
  transfers between devices with their start and end apart: 22, of which 15 were waited for; matrix products, arithmetic and copies ran while one was open for 1% of the time, Pallas kernels for 19%

profile of v1, /device:TPU:1, one launch (start us, length us, event | category | flops | bytes accessed | tf_op | source)
XLA Modules:
  0.0 143.2 jit_solution(125161758394764750)
XLA Ops:
  4.5 4.2 %place.1 = (bf16[32,16,16,128]{3,2,1,0:T(8,128)(2,1)S(1)}, bf16[32,16,16,128]{3,2,1,0:T(8,128)(2,1)S(1)}, bf16[2,16,16,128]{3,2,1,0:T(8,128)(2,1)S(1)}, bf16[2,1...) custom-call(s32[8]{0:T(128)S(1)} %copy-done.7, ...), custom_call_target="tpu_custom_call" | custom-call | tf_op jit(solution)/shard_map/place/pallas_call | solution.py:70
  12.6 4.9 %collective-permute-start = (bf16[2,16,16,128]{3,2,1,0:T(8,128)(2,1)S(1)}, bf16[2,16,16,128]{3,2,1,0:T(8,128)(2,1)S(1)}, u32[]{:S(2)}, u32[]{:S(2)}) collective-permute-start(bf16[2,16,16,128]{3,2,1,0:T(8,128)(2,1)S(1)} %get-tuple-element.14), channel_id=1, source_target_pairs={{0,4},{1,5},{2,6},{3,7},{4,8},{5,9},{6,10},{7,11},{8,12},{9,13},{1... | collective-permute-start | bytes 393224 | tf_op jit(solution)/shard_map/ppermute | solution.py:309
  18.0 1.5 %collective-permute-done = bf16[2,16,16,128]{3,2,1,0:T(8,128)(2,1)S(1)} collective-permute-done((bf16[2,16,16,128]{3,2,1,0:T(8,128)(2,1)S(1)}, bf16[2,16,16,128]{3,2,1,0:T(8,128)(2,1)S(1)}, u32[]{:S(2)}, u32[]{:S(2)}) %collective-permute-start) | collective-permute-done | bytes 131104 | tf_op jit(solution)/shard_map/ppermute | solution.py:309
  19.5 5.2 %collective-permute-start.2 = (bf16[2,34,16,128]{3,2,1,0:T(8,128)(2,1)S(1)}, bf16[2,34,16,128]{3,2,1,0:T(8,128)(2,1)S(1)}, u32[]{:S(2)}, u32[]{:S(2)}) collective-permute-start(bf16[2,34,16,128]{3,2,1,0:T(8,128)(2,1)S(1)} %pad_maximum_fusion), channel_id=1, source_target_pairs={{0,1},{1,2},{2,3},{4,5},{5,6},{6,7},{8,9},{9,10},{10,11},{12,13},{... | collective-permute-start | bytes 835592 | tf_op jit(solution)/shard_map/ppermute | solution.py:313
  24.8 1.9 %collective-permute-start.3 = (bf16[2,34,16,128]{3,2,1,0:T(8,128)(2,1)S(1)}, bf16[2,34,16,128]{3,2,1,0:T(8,128)(2,1)S(1)}, u32[]{:S(2)}, u32[]{:S(2)}) collective-permute-start(bf16[2,34,16,128]{3,2,1,0:T(8,128)(2,1)S(1)} %pad_maximum_fusion.1), channel_id=1, source_target_pairs={{1,0},{2,1},{3,2},{5,4},{6,5},{7,6},{9,8},{10,9},{11,10},{13,12},{... | collective-permute-start | bytes 835592 | tf_op jit(solution)/shard_map/ppermute | solution.py:313
  26.7 1.5 %collective-permute-done.2 = bf16[2,34,16,128]{3,2,1,0:T(8,128)(2,1)S(1)} collective-permute-done((bf16[2,34,16,128]{3,2,1,0:T(8,128)(2,1)S(1)}, bf16[2,34,16,128]{3,2,1,0:T(8,128)(2,1)S(1)}, u32[]{:S(2)}, u32[]{:S(2)}) %collective-permute-start.2) | collective-permute-done | bytes 278560 | tf_op jit(solution)/shard_map/ppermute | solution.py:313
  28.2 4.4 %collective-permute-done.3 = bf16[2,34,16,128]{3,2,1,0:T(8,128)(2,1)S(1)} collective-permute-done((bf16[2,34,16,128]{3,2,1,0:T(8,128)(2,1)S(1)}, bf16[2,34,16,128]{3,2,1,0:T(8,128)(2,1)S(1)}, u32[]{:S(2)}, u32[]{:S(2)}) %collective-permute-start.3) | collective-permute-done | bytes 278560 | tf_op jit(solution)/shard_map/ppermute | solution.py:313
  32.7 10.7 %weight_gradient.1 = (bf16[8,10,64,1152]{3,2,1,0:T(8,128)(2,1)}, f32[16,112,128]{2,1,0:T(8,128)S(1)}, f32[16,112,128]{2,1,0:T(8,128)S(1)}) custom-call(s32[8]{0:T(128)S(1)} %copy-done.8, s32[3]{0:T(128)S(1)} %pad_add_fusion.meta_ref, bf16[32,16,16,128]{3,2,1,0:T(8,128)(2,1)S(1)} %copy-done.10, bf16[16,16,128]{2,1,0:T(8,128)(2,1)S(1)} %get-tuple-element.37.xlo_ref, ...), custom_call_target="tpu_custom_call" | custom-call | flops 3623878656 | bytes 31457280 | tf_op jit(solution)/shard_map/weight_gradient/pallas_call | solution.py:195
  43.4 2.5 %collective-permute-done.4 = f32[16,112,128]{2,1,0:T(8,128)S(1)} collective-permute-done((f32[16,112,128]{2,1,0:T(8,128)S(1)}, f32[16,112,128]{2,1,0:T(8,128)S(1)}, u32[]{:S(2)}, u32[]{:S(2)}) %collective-permute-start.4) | collective-permute-done | bytes 917536 | tf_op jit(solution)/shard_map/ppermute | solution.py:305
  46.1 4.8 %collective-permute-start.7 = (f32[4,112,128]{2,1,0:T(8,128)S(1)}, f32[4,112,128]{2,1,0:T(8,128)S(1)}, u32[]{:S(2)}, u32[]{:S(2)}) collective-permute-start(f32[4,112,128]{2,1,0:T(8,128)S(1)} %get-tuple-element.26), channel_id=1, source_target_pairs={{0,130},{1,13},{2,128},{3,15},{4,134},{5,9},{6,132},{7,11},{8,138}... | collective-permute-start | bytes 688136 | tf_op jit(solution)/shard_map/ppermute | solution.py:305
  52.2 2.1 %collective-permute-done.7 = f32[4,112,128]{2,1,0:T(8,128)S(1)} collective-permute-done((f32[4,112,128]{2,1,0:T(8,128)S(1)}, f32[4,112,128]{2,1,0:T(8,128)S(1)}, u32[]{:S(2)}, u32[]{:S(2)}) %collective-permute-start.7) | collective-permute-done | bytes 229408 | tf_op jit(solution)/shard_map/ppermute | solution.py:305
  54.3 1.5 %collective-permute-done.6 = f32[4,112,128]{2,1,0:T(8,128)S(1)} collective-permute-done((f32[4,112,128]{2,1,0:T(8,128)S(1)}, f32[4,112,128]{2,1,0:T(8,128)S(1)}, u32[]{:S(2)}, u32[]{:S(2)}) %collective-permute-start.6) | collective-permute-done | bytes 229408 | tf_op jit(solution)/shard_map/ppermute | solution.py:305
  55.8 2.3 %collective-permute-done.5 = f32[4,112,128]{2,1,0:T(8,128)S(1)} collective-permute-done((f32[4,112,128]{2,1,0:T(8,128)S(1)}, f32[4,112,128]{2,1,0:T(8,128)S(1)}, u32[]{:S(2)}, u32[]{:S(2)}) %collective-permute-start.5) | collective-permute-done | bytes 229408 | tf_op jit(solution)/shard_map/ppermute | solution.py:305
  58.1 14.4 %collective-permute-start.10 = (f32[1,112,128]{2,1,0:T(8,128)S(1)}, f32[1,112,128]{2,1,0:T(8,128)S(1)}, u32[]{:S(2)}, u32[]{:S(2)}) collective-permute-start(f32[1,112,128]{2,1,0:T(8,128)S(1)} %get-tuple-element.33), channel_id=1, source_target_pairs={{0,12},{1,131},{2,14},{3,129},{4,8},{5,135},{6,10},{7,133},{8,4},{... | collective-permute-start | bytes 172040 | tf_op jit(solution)/shard_map/ppermute | solution.py:305
  74.1 1.8 %collective-permute-done.9 = f32[1,112,128]{2,1,0:T(8,128)S(1)} collective-permute-done((f32[1,112,128]{2,1,0:T(8,128)S(1)}, f32[1,112,128]{2,1,0:T(8,128)S(1)}, u32[]{:S(2)}, u32[]{:S(2)}) %collective-permute-start.9) | collective-permute-done | bytes 57376 | tf_op jit(solution)/shard_map/ppermute | solution.py:305
  75.9 1.4 collective-permute-done.8
  77.5 3.4 %collective-permute-start.11 = (f32[1,112,128]{2,1,0:T(8,128)S(1)}, f32[1,112,128]{2,1,0:T(8,128)S(1)}, u32[]{:S(2)}, u32[]{:S(2)}) collective-permute-start(f32[1,112,128]{2,1,0:T(8,128)S(1)} %fusion.3), channel_id=1, source_target_pairs={{0,32},{1,33},{2,34},{3,35},{4,36},{5,37},{6,38},{7,39},{8,40},{9,... | collective-permute-start | bytes 172040 | tf_op jit(solution)/shard_map/ppermute | solution.py:305
  82.4 1.6 %copy-done.2 = bf16[32,16,16,128]{3,2,1,0:T(8,128)(2,1)S(1)} copy-done((bf16[32,16,16,128]{3,2,1,0:T(8,128)(2,1)S(1)}, bf16[32,16,16,128]{3,2,1,0:T(8,128)(2,1)}, u32[]{:S(2)}) %copy-start.2) | copy-done | bytes 2097176
  83.9 3.7 %patches.1.refs_2_ = bf16[8,10,64,1152]{3,2,1,0:T(8,128)(2,1)S(1)} custom-call(s32[8]{0:T(128)S(1)} %copy-done.8, bf16[32,16,16,128]{3,2,1,0:T(8,128)(2,1)S(1)} %copy-done.2, bf16[16,16,128]{2,1,0:T(8,128)(2,1)S(1)} %get-tuple-element.38.xlo_ref, bf16[16,16,128]{2,1,0:T(8,128)(2,1)S(1)} %get-tuple-element.36.xhi_ref, ...), custom_call_target="tpu_custom_call" | custom-call | bytes 31457280 | tf_op jit(solution)/shard_map/patches/pallas_call | solution.py:180
  88.0 3.4 %convolve.8.refs_4_ = bf16[8,512,128]{2,1,0:T(8,128)(2,1)} custom-call(s32[8]{0:T(128)S(1)} %copy-done.8, s32[8,512]{1,0:T(8,128)S(1)} %copy-done.4, bf16[8,10,64,1152]{3,2,1,0:T(8,128)(2,1)S(1)} %patches.1.refs_2_, bf16[3456,128]{1,0:T(8,128)(2,1)S(1)} %bitcast.25), custom_call_target="tpu_custom_call" | custom-call | flops 1811939328 | bytes 2097152 | tf_op jit(solution)/shard_map/convolve/pallas_call | solution.py:231
  91.4 4.1 %collective-permute-done.14 = f32[1,112,128]{2,1,0:T(8,128)S(1)} collective-permute-done((f32[1,112,128]{2,1,0:T(8,128)S(1)}, f32[1,112,128]{2,1,0:T(8,128)S(1)}, u32[]{:S(2)}, u32[]{:S(2)}) %collective-permute-start.14) | collective-permute-done | bytes 57376 | tf_op jit(solution)/shard_map/ppermute | solution.py:305
  97.5 2.0 %collective-permute-start.17 = (f32[1,112,128]{2,1,0:T(8,128)S(1)}, f32[1,112,128]{2,1,0:T(8,128)S(1)}, u32[]{:S(2)}, u32[]{:S(2)}) collective-permute-start(f32[1,112,128]{2,1,0:T(8,128)S(1)} %get-tuple-element.24), channel_id=1, source_target_pairs={{0,12},{1,131},{2,14},{3,129},{4,8},{5,135},{6,10},{7,133},{8,4},{... | collective-permute-start | bytes 172040 | tf_op jit(solution)/shard_map/ppermute | solution.py:305
  99.4 3.4 %convolve.9.refs_4_ = bf16[8,512,128]{2,1,0:T(8,128)(2,1)} custom-call(s32[8]{0:T(128)S(1)} %copy-done.8, s32[8,512]{1,0:T(8,128)S(1)} %copy-done.4, bf16[8,10,64,1152]{3,2,1,0:T(8,128)(2,1)S(1)} %patches.1.refs_2_, bf16[3456,128]{1,0:T(8,128)(2,1)S(1)} %bitcast.26, bf16[8,512,128]{2,1,0:T(8,128)(2,1)} %convolve.8.refs_4_), custom_call_target="tpu_custom_call", output_to_operand_aliasing={{}: (4, {})} | custom-call | flops 1811939328 | bytes 2097152 | tf_op jit(solution)/shard_map/convolve/pallas_call | solution.py:231
  104.0 2.8 %collective-permute-start.20 = (f32[4,112,128]{2,1,0:T(8,128)S(1)}, f32[4,112,128]{2,1,0:T(8,128)S(1)}, u32[]{:S(2)}, u32[]{:S(2)}) collective-permute-start(f32[4,112,128]{2,1,0:T(8,128)S(1)} %pad_maximum_fusion.2), channel_id=1, source_target_pairs={{0,130},{1,13},{2,128},{3,15},{4,134},{5,9},{6,132},{7,11},{8,138}... | collective-permute-start | bytes 688136 | tf_op jit(solution)/shard_map/ppermute | solution.py:305
  107.9 2.1 %collective-permute-done.19 = f32[4,112,128]{2,1,0:T(8,128)S(1)} collective-permute-done((f32[4,112,128]{2,1,0:T(8,128)S(1)}, f32[4,112,128]{2,1,0:T(8,128)S(1)}, u32[]{:S(2)}, u32[]{:S(2)}) %collective-permute-start.19) | collective-permute-done | bytes 229408 | tf_op jit(solution)/shard_map/ppermute | solution.py:305
  110.0 2.3 %collective-permute-done.20 = f32[4,112,128]{2,1,0:T(8,128)S(1)} collective-permute-done((f32[4,112,128]{2,1,0:T(8,128)S(1)}, f32[4,112,128]{2,1,0:T(8,128)S(1)}, u32[]{:S(2)}, u32[]{:S(2)}) %collective-permute-start.20) | collective-permute-done | bytes 229408 | tf_op jit(solution)/shard_map/ppermute | solution.py:305
  112.4 11.6 %collective-permute-start.21 = (f32[16,112,128]{2,1,0:T(8,128)S(1)}, f32[16,112,128]{2,1,0:T(8,128)S(1)}, u32[]{:S(2)}, u32[]{:S(2)}) collective-permute-start(f32[16,112,128]{2,1,0:T(8,128)S(1)} %constant_dynamic-update-slice_fusion.own_ref), channel_id=1, source_target_pairs={{0,1},{1,0},{2,3},{3,2},{4,5},{5,4},{6,7},{7,6},{8,9},{9,8},{10,11... | collective-permute-start | bytes 2752520 | tf_op jit(solution)/shard_map/ppermute | solution.py:305
  124.0 3.4 %convolve.10.refs_4_ = bf16[8,512,128]{2,1,0:T(8,128)(2,1)} custom-call(s32[8]{0:T(128)S(1)} %copy-done.8, s32[8,512]{1,0:T(8,128)S(1)} %copy-done.4, bf16[8,10,64,1152]{3,2,1,0:T(8,128)(2,1)S(1)} %patches.1.refs_2_, bf16[3456,128]{1,0:T(8,128)(2,1)S(1)} %bitcast.27, bf16[8,512,128]{2,1,0:T(8,128)(2,1)} %convolve.9.refs_4_), custom_call_target="tpu_custom_call", output_to_operand_aliasing={{}: (4, {})} | custom-call | flops 1811939328 | bytes 2097152 | tf_op jit(solution)/shard_map/convolve/pallas_call | solution.py:231
  129.5 3.4 %convolve.12.refs_4_ = bf16[8,512,128]{2,1,0:T(8,128)(2,1)} custom-call(s32[8]{0:T(128)S(1)} %copy-done.8, s32[8,512]{1,0:T(8,128)S(1)} %copy-done.4, bf16[8,10,64,1152]{3,2,1,0:T(8,128)(2,1)S(1)} %bitcast.24, bf16[3456,128]{1,0:T(8,128)(2,1)S(1)} %bitcast.29), custom_call_target="tpu_custom_call" | custom-call | flops 1811939328 | bytes 2097152 | tf_op jit(solution)/shard_map/convolve/pallas_call | solution.py:231
  132.9 3.4 %convolve.13.refs_4_ = bf16[8,512,128]{2,1,0:T(8,128)(2,1)} custom-call(s32[8]{0:T(128)S(1)} %copy-done.8, s32[8,512]{1,0:T(8,128)S(1)} %copy-done.4, bf16[8,10,64,1152]{3,2,1,0:T(8,128)(2,1)S(1)} %bitcast.24, bf16[3456,128]{1,0:T(8,128)(2,1)S(1)} %bitcast.30, bf16[8,512,128]{2,1,0:T(8,128)(2,1)} %convolve.12.refs_4_), custom_call_target="tpu_custom_call", output_to_operand_aliasing={{}: (4, {})} | custom-call | flops 1811939328 | bytes 2097152 | tf_op jit(solution)/shard_map/convolve/pallas_call | solution.py:231
  136.3 3.4 %convolve.14.refs_4_ = bf16[8,512,128]{2,1,0:T(8,128)(2,1)} custom-call(s32[8]{0:T(128)S(1)} %copy-done.8, s32[8,512]{1,0:T(8,128)S(1)} %copy-done.4, bf16[8,10,64,1152]{3,2,1,0:T(8,128)(2,1)S(1)} %bitcast.24, bf16[3456,128]{1,0:T(8,128)(2,1)S(1)} %bitcast.31, bf16[8,512,128]{2,1,0:T(8,128)(2,1)} %convolve.13.refs_4_), custom_call_target="tpu_custom_call", output_to_operand_aliasing={{}: (4, {})} | custom-call | flops 1811939328 | bytes 2097152 | tf_op jit(solution)/shard_map/convolve/pallas_call | solution.py:231
  141.0 2.2 %finish.1 = f32[27,128,128]{2,1,0:T(8,128)} custom-call(s32[3]{0:T(128)S(1)} %pad_add_fusion.meta_ref, f32[16,112,128]{2,1,0:T(8,128)S(1)} %constant_dynamic-update-slice_fusion.own_ref, f32[16,112,128]{2,1,0:T(8,128)S(1)} %collective-permute-done.21.other_ref), custom_call_target="tpu_custom_call" | custom-call | tf_op jit(solution)/shard_map/finish/pallas_call | solution.py:266
  (78 shorter events, 20.8 us)
Async XLA Ops:
  4.5 28.2 %copy-start.8 = (s32[8]{0:T(128)S(1)}, s32[8]{0:T(128)}, u32[]{:S(2)}) copy-start(s32[8]{0:T(128)} %refs_0_.15) | copy-start | bytes 100
  8.7 1.3 copy-start.1
  10.0 1.3 copy-start.9
  11.3 6.6 %collective-permute-start.1 = (bf16[2,16,16,128]{3,2,1,0:T(8,128)(2,1)S(1)}, bf16[2,16,16,128]{3,2,1,0:T(8,128)(2,1)S(1)}, u32[]{:S(2)}, u32[]{:S(2)}) collective-permute-start(bf16[2,16,16,128]{3,2,1,0:T(8,128)(2,1)S(1)} %get-tuple-element.15), channel_id=1, source_target_pairs={{4,0},{5,1},{6,2},{7,3},{8,4},{9,5},{10,6},{11,7},{12,8},{13,9},{1... | collective-permute-start | bytes 393224 | tf_op jit(solution)/shard_map/ppermute | solution.py:309
  12.6 6.9 %collective-permute-start = (bf16[2,16,16,128]{3,2,1,0:T(8,128)(2,1)S(1)}, bf16[2,16,16,128]{3,2,1,0:T(8,128)(2,1)S(1)}, u32[]{:S(2)}, u32[]{:S(2)}) collective-permute-start(bf16[2,16,16,128]{3,2,1,0:T(8,128)(2,1)S(1)} %get-tuple-element.14), channel_id=1, source_target_pairs={{0,4},{1,5},{2,6},{3,7},{4,8},{5,9},{6,10},{7,11},{8,12},{9,13},{1... | collective-permute-start | bytes 393224 | tf_op jit(solution)/shard_map/ppermute | solution.py:309
  17.6 15.1 %copy-start.10 = (bf16[32,16,16,128]{3,2,1,0:T(8,128)(2,1)S(1)}, bf16[32,16,16,128]{3,2,1,0:T(8,128)(2,1)}, u32[]{:S(2)}) copy-start(bf16[32,16,16,128]{3,2,1,0:T(8,128)(2,1)} %copy-done.9) | copy-start | bytes 6291460
  19.5 8.7 %collective-permute-start.2 = (bf16[2,34,16,128]{3,2,1,0:T(8,128)(2,1)S(1)}, bf16[2,34,16,128]{3,2,1,0:T(8,128)(2,1)S(1)}, u32[]{:S(2)}, u32[]{:S(2)}) collective-permute-start(bf16[2,34,16,128]{3,2,1,0:T(8,128)(2,1)S(1)} %pad_maximum_fusion), channel_id=1, source_target_pairs={{0,1},{1,2},{2,3},{4,5},{5,6},{6,7},{8,9},{9,10},{10,11},{12,13},{... | collective-permute-start | bytes 835592 | tf_op jit(solution)/shard_map/ppermute | solution.py:313
  24.8 7.9 %collective-permute-start.3 = (bf16[2,34,16,128]{3,2,1,0:T(8,128)(2,1)S(1)}, bf16[2,34,16,128]{3,2,1,0:T(8,128)(2,1)S(1)}, u32[]{:S(2)}, u32[]{:S(2)}) collective-permute-start(bf16[2,34,16,128]{3,2,1,0:T(8,128)(2,1)S(1)} %pad_maximum_fusion.1), channel_id=1, source_target_pairs={{1,0},{2,1},{3,2},{5,4},{6,5},{7,6},{9,8},{10,9},{11,10},{13,12},{... | collective-permute-start | bytes 835592 | tf_op jit(solution)/shard_map/ppermute | solution.py:313
  43.4 2.5 %collective-permute-start.4 = (f32[16,112,128]{2,1,0:T(8,128)S(1)}, f32[16,112,128]{2,1,0:T(8,128)S(1)}, u32[]{:S(2)}, u32[]{:S(2)}) collective-permute-start(f32[16,112,128]{2,1,0:T(8,128)S(1)} %get-tuple-element.22), channel_id=1, source_target_pairs={{0,1},{1,0},{2,3},{3,2},{4,5},{5,4},{6,7},{7,6},{8,9},{9,8},{10,11... | collective-permute-start | bytes 2752520 | tf_op jit(solution)/shard_map/ppermute | solution.py:305
  46.0 35.0 %copy-start = (bf16[27,128,128]{2,1,0:T(8,128)(2,1)S(1)}, bf16[27,128,128]{2,1,0:T(8,128)(2,1)}, u32[]{:S(2)}) copy-start(bf16[27,128,128]{2,1,0:T(8,128)(2,1)} %param.6) | copy-start | bytes 2654212
  46.1 8.3 %collective-permute-start.7 = (f32[4,112,128]{2,1,0:T(8,128)S(1)}, f32[4,112,128]{2,1,0:T(8,128)S(1)}, u32[]{:S(2)}, u32[]{:S(2)}) collective-permute-start(f32[4,112,128]{2,1,0:T(8,128)S(1)} %get-tuple-element.26), channel_id=1, source_target_pairs={{0,130},{1,13},{2,128},{3,15},{4,134},{5,9},{6,132},{7,11},{8,138}... | collective-permute-start | bytes 688136 | tf_op jit(solution)/shard_map/ppermute | solution.py:305
  50.9 4.9 %collective-permute-start.6 = (f32[4,112,128]{2,1,0:T(8,128)S(1)}, f32[4,112,128]{2,1,0:T(8,128)S(1)}, u32[]{:S(2)}, u32[]{:S(2)}) collective-permute-start(f32[4,112,128]{2,1,0:T(8,128)S(1)} %get-tuple-element.27), channel_id=1, source_target_pairs={{0,2},{1,5},{2,0},{3,7},{4,6},{5,1},{6,4},{7,3},{8,10},{9,13},{10,... | collective-permute-start | bytes 688136 | tf_op jit(solution)/shard_map/ppermute | solution.py:305
  50.9 7.1 %collective-permute-start.5 = (f32[4,112,128]{2,1,0:T(8,128)S(1)}, f32[4,112,128]{2,1,0:T(8,128)S(1)}, u32[]{:S(2)}, u32[]{:S(2)}) collective-permute-start(f32[4,112,128]{2,1,0:T(8,128)S(1)} %get-tuple-element.25), channel_id=1, source_target_pairs={{0,128},{1,9},{2,130},{3,11},{4,132},{5,13},{6,134},{7,15},{8,136}... | collective-permute-start | bytes 688136 | tf_op jit(solution)/shard_map/ppermute | solution.py:305
  58.1 16.0 %collective-permute-start.10 = (f32[1,112,128]{2,1,0:T(8,128)S(1)}, f32[1,112,128]{2,1,0:T(8,128)S(1)}, u32[]{:S(2)}, u32[]{:S(2)}) collective-permute-start(f32[1,112,128]{2,1,0:T(8,128)S(1)} %get-tuple-element.33), channel_id=1, source_target_pairs={{0,12},{1,131},{2,14},{3,129},{4,8},{5,135},{6,10},{7,133},{8,4},{... | collective-permute-start | bytes 172040 | tf_op jit(solution)/shard_map/ppermute | solution.py:305
  72.6 3.3 %collective-permute-start.9 = (f32[1,112,128]{2,1,0:T(8,128)S(1)}, f32[1,112,128]{2,1,0:T(8,128)S(1)}, u32[]{:S(2)}, u32[]{:S(2)}) collective-permute-start(f32[1,112,128]{2,1,0:T(8,128)S(1)} %get-tuple-element.34), channel_id=1, source_target_pairs={{0,4},{1,3},{2,6},{3,1},{4,0},{5,7},{6,2},{7,5},{8,12},{9,11},{10,... | collective-permute-start | bytes 172040 | tf_op jit(solution)/shard_map/ppermute | solution.py:305
  72.8 4.5 %collective-permute-start.8 = (f32[1,112,128]{2,1,0:T(8,128)S(1)}, f32[1,112,128]{2,1,0:T(8,128)S(1)}, u32[]{:S(2)}, u32[]{:S(2)}) collective-permute-start(f32[1,112,128]{2,1,0:T(8,128)S(1)} %get-tuple-element.32), channel_id=1, source_target_pairs={{0,8},{1,129},{2,10},{3,131},{4,12},{5,133},{6,14},{7,135},{8,0},{... | collective-permute-start | bytes 172040 | tf_op jit(solution)/shard_map/ppermute | solution.py:305
  77.3 10.3 %collective-permute-start.13 = (f32[1,112,128]{2,1,0:T(8,128)S(1)}, f32[1,112,128]{2,1,0:T(8,128)S(1)}, u32[]{:S(2)}, u32[]{:S(2)}) collective-permute-start(f32[1,112,128]{2,1,0:T(8,128)S(1)} %fusion.3), channel_id=1, source_target_pairs={{0,48},{1,49},{2,50},{3,51},{4,52},{5,53},{6,54},{7,55},{8,56},{9,... | collective-permute-start | bytes 172040 | tf_op jit(solution)/shard_map/ppermute | solution.py:305
  77.4 10.2 %collective-permute-start.12 = (f32[1,112,128]{2,1,0:T(8,128)S(1)}, f32[1,112,128]{2,1,0:T(8,128)S(1)}, u32[]{:S(2)}, u32[]{:S(2)}) collective-permute-start(f32[1,112,128]{2,1,0:T(8,128)S(1)} %fusion.3), channel_id=1, source_target_pairs={{0,16},{1,17},{2,18},{3,19},{4,20},{5,21},{6,22},{7,23},{8,24},{9,... | collective-permute-start | bytes 172040 | tf_op jit(solution)/shard_map/ppermute | solution.py:305
  77.5 10.1 %collective-permute-start.11 = (f32[1,112,128]{2,1,0:T(8,128)S(1)}, f32[1,112,128]{2,1,0:T(8,128)S(1)}, u32[]{:S(2)}, u32[]{:S(2)}) collective-permute-start(f32[1,112,128]{2,1,0:T(8,128)S(1)} %fusion.3), channel_id=1, source_target_pairs={{0,32},{1,33},{2,34},{3,35},{4,36},{5,37},{6,38},{7,39},{8,40},{9,... | collective-permute-start | bytes 172040 | tf_op jit(solution)/shard_map/ppermute | solution.py:305
  82.4 1.6 %copy-start.2 = (bf16[32,16,16,128]{3,2,1,0:T(8,128)(2,1)S(1)}, bf16[32,16,16,128]{3,2,1,0:T(8,128)(2,1)}, u32[]{:S(2)}) copy-start(bf16[32,16,16,128]{3,2,1,0:T(8,128)(2,1)} %copy-done.1) | copy-start | bytes 6291460
  83.9 4.0 %copy-start.4 = (s32[8,512]{1,0:T(8,128)S(1)}, s32[8,512]{1,0:T(8,128)}, u32[]{:S(2)}) copy-start(s32[8,512]{1,0:T(8,128)} %refs_1_.15) | copy-start | bytes 49156
  87.7 7.8 %collective-permute-start.14 = (f32[1,112,128]{2,1,0:T(8,128)S(1)}, f32[1,112,128]{2,1,0:T(8,128)S(1)}, u32[]{:S(2)}, u32[]{:S(2)}) collective-permute-start(f32[1,112,128]{2,1,0:T(8,128)S(1)} %add_add_fusion), channel_id=1, source_target_pairs={{0,64},{1,65},{2,66},{3,67},{4,68},{5,69},{6,70},{7,71},{8,72},{9,... | collective-permute-start | bytes 172040 | tf_op jit(solution)/shard_map/ppermute | solution.py:305
  95.5 7.4 %collective-permute-start.15 = (f32[1,112,128]{2,1,0:T(8,128)S(1)}, f32[1,112,128]{2,1,0:T(8,128)S(1)}, u32[]{:S(2)}, u32[]{:S(2)}) collective-permute-start(f32[1,112,128]{2,1,0:T(8,128)S(1)} %get-tuple-element.24), channel_id=1, source_target_pairs={{0,4},{1,3},{2,6},{3,1},{4,0},{5,7},{6,2},{7,5},{8,12},{9,11},{10,... | collective-permute-start | bytes 172040 | tf_op jit(solution)/shard_map/ppermute | solution.py:305
  96.8 6.1 %collective-permute-start.16 = (f32[1,112,128]{2,1,0:T(8,128)S(1)}, f32[1,112,128]{2,1,0:T(8,128)S(1)}, u32[]{:S(2)}, u32[]{:S(2)}) collective-permute-start(f32[1,112,128]{2,1,0:T(8,128)S(1)} %get-tuple-element.24), channel_id=1, source_target_pairs={{0,8},{1,129},{2,10},{3,131},{4,12},{5,133},{6,14},{7,135},{8,0},{... | collective-permute-start | bytes 172040 | tf_op jit(solution)/shard_map/ppermute | solution.py:305
  97.5 5.4 %collective-permute-start.17 = (f32[1,112,128]{2,1,0:T(8,128)S(1)}, f32[1,112,128]{2,1,0:T(8,128)S(1)}, u32[]{:S(2)}, u32[]{:S(2)}) collective-permute-start(f32[1,112,128]{2,1,0:T(8,128)S(1)} %get-tuple-element.24), channel_id=1, source_target_pairs={{0,12},{1,131},{2,14},{3,129},{4,8},{5,135},{6,10},{7,133},{8,4},{... | collective-permute-start | bytes 172040 | tf_op jit(solution)/shard_map/ppermute | solution.py:305
  102.9 5.0 %collective-permute-start.18 = (f32[4,112,128]{2,1,0:T(8,128)S(1)}, f32[4,112,128]{2,1,0:T(8,128)S(1)}, u32[]{:S(2)}, u32[]{:S(2)}) collective-permute-start(f32[4,112,128]{2,1,0:T(8,128)S(1)} %pad_maximum_fusion.2), channel_id=1, source_target_pairs={{0,2},{1,5},{2,0},{3,7},{4,6},{5,1},{6,4},{7,3},{8,10},{9,13},{10,... | collective-permute-start | bytes 688136 | tf_op jit(solution)/shard_map/ppermute | solution.py:305
  103.0 7.0 %collective-permute-start.19 = (f32[4,112,128]{2,1,0:T(8,128)S(1)}, f32[4,112,128]{2,1,0:T(8,128)S(1)}, u32[]{:S(2)}, u32[]{:S(2)}) collective-permute-start(f32[4,112,128]{2,1,0:T(8,128)S(1)} %pad_maximum_fusion.2), channel_id=1, source_target_pairs={{0,128},{1,9},{2,130},{3,11},{4,132},{5,13},{6,134},{7,15},{8,136}... | collective-permute-start | bytes 688136 | tf_op jit(solution)/shard_map/ppermute | solution.py:305
  104.0 8.3 %collective-permute-start.20 = (f32[4,112,128]{2,1,0:T(8,128)S(1)}, f32[4,112,128]{2,1,0:T(8,128)S(1)}, u32[]{:S(2)}, u32[]{:S(2)}) collective-permute-start(f32[4,112,128]{2,1,0:T(8,128)S(1)} %pad_maximum_fusion.2), channel_id=1, source_target_pairs={{0,130},{1,13},{2,128},{3,15},{4,134},{5,9},{6,132},{7,11},{8,138}... | collective-permute-start | bytes 688136 | tf_op jit(solution)/shard_map/ppermute | solution.py:305
  112.4 28.6 %collective-permute-start.21 = (f32[16,112,128]{2,1,0:T(8,128)S(1)}, f32[16,112,128]{2,1,0:T(8,128)S(1)}, u32[]{:S(2)}, u32[]{:S(2)}) collective-permute-start(f32[16,112,128]{2,1,0:T(8,128)S(1)} %constant_dynamic-update-slice_fusion.own_ref), channel_id=1, source_target_pairs={{0,1},{1,0},{2,3},{3,2},{4,5},{5,4},{6,7},{7,6},{8,9},{9,8},{10,11... | collective-permute-start | bytes 2752520 | tf_op jit(solution)/shard_map/ppermute | solution.py:305
  124.0 4.7 %slice-start = ((s8[11796480]{0:T(1024)(128)(4,1)}), s8[4194304]{0:T(1024)(128)(4,1)S(1)}, s32[]{:S(2)}) async-start(s8[11796480]{0:T(1024)(128)(4,1)} %bitcast.23), calls=%async_computation | async-start | bytes 8388608
  124.0 4.7 %slice-start.1 = ((s8[11796480]{0:T(1024)(128)(4,1)}), s8[4194304]{0:T(1024)(128)(4,1)S(1)}, s32[]{:S(2)}) async-start(s8[11796480]{0:T(1024)(128)(4,1)} %bitcast.23), calls=%async_computation.1 | async-start | bytes 8388608
  127.4 2.1 %slice-start.2 = ((s8[11796480]{0:T(1024)(128)(4,1)}), s8[3407872]{0:T(1024)(128)(4,1)S(1)}, s32[]{:S(2)}) async-start(s8[11796480]{0:T(1024)(128)(4,1)} %bitcast.23), calls=%async_computation.2 | async-start | bytes 6815744
  (4 other events, 3.8 us)

commit v2 on v1

--- a/solution.py
+++ b/solution.py
@@ -23,6 +23,10 @@
 SMEM = pl.BlockSpec(memory_space=pltpu.SMEM)
 
 
+def pin(value, space):
+    return pltpu.with_memory_space_constraint(value, space)
+
+
 def brick_of(pos):
     return pos >> 2, (pos >> 1) & 1, pos & 1
 
@@ -31,9 +35,20 @@
     return jnp.where(occ_ref[...] == 1, 1.0, 0.0).astype(F32).T
 
 
-def place_kernel(pos_ref, occ_ref, feat_ref, cot_ref, xg_ref, cg_ref, lo_ref, hi_ref, yl_ref, yh_ref, xt_ref, cells):
+def place_kernel(pos_ref, meta_ref, occ_ref, feat_hbm, cot_hbm, xg_hbm, cg_hbm, xt_hbm, even_ref, odd_ref, side_even_ref, side_odd_ref, cells, slots, grids, xt, load_sems, grid_sems, xt_sem):
+    def load(t, s):
+        return pltpu.make_async_copy((cot_hbm, feat_hbm)[t].at[s], slots.at[t, s], load_sems.at[t, s])
+
+    def save(t, n):
+        part = pl.ds(n * 8, 8)
+        return pltpu.make_async_copy(grids.at[t, part], (cg_hbm, xg_hbm)[t].at[part], grid_sems.at[t, n])
+
+    for t in range(2):
+        for s in range(SLOTS):
+            load(t, s).start()
     columns = mask_columns(occ_ref)
-    for t, (src, dst) in enumerate(((cot_ref, cg_ref), (feat_ref, xg_ref))):
+    core, odd_x = meta_ref[0], meta_ref[3]
+    for t in range(2):
 
         def clear(x, carry):
             cells[x] = jnp.zeros((NY, 2, 8, CH), F32)
@@ -41,44 +56,66 @@
 
         lax.fori_loop(0, NX, clear, 0)
         for s in range(SLOTS):
+            load(t, s).wait()
             pos = pos_ref[s]
 
             @pl.when(pos >= 0)
             def _():
                 bx, by, bz = brick_of(pos)
                 keep = jnp.broadcast_to(columns[:, s : s + 1], (VOX, CH))
-                value = jnp.where(keep > 0.5, src[s].astype(F32), 0.0)
+                value = jnp.where(keep > 0.5, slots[t, s].astype(F32), 0.0)
                 cells[pl.ds(bx * 8, 8), pl.ds(by * 8, 8), bz] = value.reshape(8, 8, 8, CH)
                 if t == 1:
-                    xt_ref[s] = value.T.astype(BF16)
+                    xt[s] = value.T.astype(BF16)
+
+        if t == 1:
+            save_xt = pltpu.make_async_copy(xt, xt_hbm, xt_sem)
+            save_xt.start()
 
         def emit(x, carry):
-            dst[x] = cells[x].reshape(NY, NZ, CH).astype(BF16)
+            grids[t, x] = cells[x].reshape(NY, NZ, CH).astype(BF16)
             return carry
 
-        lax.fori_loop(0, NX, emit, 0)
-        lo_ref[t] = dst[0]
-        hi_ref[t] = dst[NX - 1]
-        yl_ref[t] = dst[:, 0]
-        yh_ref[t] = dst[:, NY - 1]
-
-
-def place(slot_pos, occupancy, features, cotangent):
+        for n in range(4):
+            lax.fori_loop(n * 8, n * 8 + 8, emit, 0)
+            save(t, n).start()
+        even_ref[t] = grids[t, (NX - 1) * (1 - odd_x)]
+        odd_ref[t] = grids[t, (NX - 1) * odd_x]
+        side_even_ref[t] = grids[t, :, (NY - 1) * (1 - core)]
+        side_odd_ref[t] = grids[t, :, (NY - 1) * core]
+    save_xt.wait()
+    for t in range(2):
+        for n in range(4):
+            save(t, n).wait()
+
+
+def place(slot_pos, meta, occupancy, features, cotangent):
     plane = jax.ShapeDtypeStruct((2, NY, NZ, CH), BF16)
     side = jax.ShapeDtypeStruct((2, NX, NZ, CH), BF16)
-    grid = jax.ShapeDtypeStruct((NX, NY, NZ, CH), BF16)
+    grid = pltpu.HBM((NX, NY, NZ, CH), BF16)
+    hbm = pl.BlockSpec(memory_space=pltpu.HBM)
     return pl.pallas_call(
         place_kernel,
-        out_shape=(grid, grid, plane, plane, side, side, jax.ShapeDtypeStruct((SLOTS, CH, VOX), BF16)),
-        in_specs=[SMEM, VMEM, VMEM, VMEM],
-        out_specs=(VMEM,) * 7,
-        scratch_shapes=[pltpu.VMEM((NX, NY, 2, 8, CH), F32)],
-        compiler_params=pltpu.CompilerParams(vmem_limit_bytes=32 << 20),
+        out_shape=(grid, grid, pltpu.HBM((SLOTS, CH, VOX), BF16), plane, plane, side, side),
+        in_specs=[SMEM, SMEM, VMEM, hbm, hbm],
+        out_specs=(hbm,) * 3 + (VMEM,) * 4,
+        scratch_shapes=[
+            pltpu.VMEM((NX, NY, 2, 8, CH), F32),
+            pltpu.VMEM((2, SLOTS, VOX, CH), BF16),
+            pltpu.VMEM((2, NX, NY, NZ, CH), BF16),
+            pltpu.VMEM((SLOTS, CH, VOX), BF16),
+            pltpu.SemaphoreType.DMA((2, SLOTS)),
+            pltpu.SemaphoreType.DMA((2, 4)),
+            pltpu.SemaphoreType.DMA,
+        ],
+        compiler_params=pltpu.CompilerParams(vmem_limit_bytes=24 << 20),
         name="place",
-    )(slot_pos, occupancy, features, cotangent)
-
-
-def assemble(grid_ref, xlo_ref, xhi_ref, ylo_ref, yhi_ref, halo):
+    )(slot_pos, meta, occupancy, pin(features, pltpu.HBM), pin(cotangent, pltpu.HBM))
+
+
+def assemble(meta_ref, grid_ref, even_ref, odd_ref, side_even_ref, side_odd_ref, halo):
+    core, odd_x = meta_ref[0], meta_ref[3]
+
     def shifted(v):
         n = v.shape[0]
         flat = v.astype(F32).reshape(n * NZ, CH)
@@ -97,9 +134,9 @@
         return carry
 
     lax.fori_loop(0, NX, body, 0)
-    put_plane(0, xlo_ref[...])
-    put_plane(NX + 1, xhi_ref[...])
-    for y, ref in ((0, ylo_ref), (NY + 1, yhi_ref)):
+    put_plane((NX + 1) * (1 - odd_x), even_ref[...])
+    put_plane((NX + 1) * odd_x, odd_ref[...])
+    for y, ref in (((NY + 1) * (1 - core), side_even_ref), ((NY + 1) * core, side_odd_ref)):
         for r, a in enumerate(shifted(ref[...])):
             for bz in range(2):
                 halo[r, bz, :, y] = a[:, bz]
@@ -119,12 +156,13 @@
     return patch_ref[0, pl.ds(p, 8)].reshape(VOX, KROW)
 
 
-def patches_kernel(pos_ref, grid_ref, xlo_ref, xhi_ref, ylo_ref, yhi_ref, patch_ref, halo):
+def patches_kernel(pos_ref, meta_ref, *refs):
+    patch_ref, halo = refs[5:]
     s = pl.program_id(0)
 
     @pl.when(s == 0)
     def _():
-        assemble(grid_ref, xlo_ref, xhi_ref, ylo_ref, yhi_ref, halo)
+        assemble(meta_ref, *refs[:5], halo)
 
     pos = pos_ref[s]
 
@@ -133,12 +171,13 @@
         build_patches(pos, halo, patch_ref)
 
 
-def weight_kernel(pos_ref, meta_ref, grid_ref, xlo_ref, xhi_ref, ylo_ref, yhi_ref, xt_ref, patch_ref, keep_ref, send_ref, halo, total):
+def weight_kernel(pos_ref, meta_ref, *refs):
+    xt_ref, patch_ref, keep_ref, send_ref, halo, total = refs[5:]
     s = pl.program_id(0)
 
     @pl.when(s == 0)
     def _():
-        assemble(grid_ref, xlo_ref, xhi_ref, ylo_ref, yhi_ref, halo)
+        assemble(meta_ref, *refs[:5], halo)
 
         def clear(o, carry):
             total[pl.ds(pl.multiple_of(o * CH, CH), CH)] = jnp.zeros((CH, CH), F32)
@@ -171,27 +210,27 @@
         lax.fori_loop(0, BLOCKS, emit, 0)
 
 
-PATCH_SHAPE = jax.ShapeDtypeStruct((SLOTS, 10, 64, KROW), BF16)
+PATCH_SHAPE = pltpu.HBM((SLOTS, 10, 64, KROW), BF16)
 PATCH_SPEC = pl.BlockSpec((1, 10, 64, KROW), lambda s, *_: (s, 0, 0, 0))
 HALO = pltpu.VMEM((3, 2, NX + 2, NY + 2, 8, CH), F32)
 
 
-def patches(slot_pos, grid, faces):
+def patches(slot_pos, meta, grid, faces):
     return pl.pallas_call(
         patches_kernel,
         out_shape=PATCH_SHAPE,
         grid=(SLOTS,),
-        in_specs=[SMEM] + [VMEM] * 5,
+        in_specs=[SMEM, SMEM] + [VMEM] * 5,
         out_specs=PATCH_SPEC,
         scratch_shapes=[HALO],
-        compiler_params=pltpu.CompilerParams(vmem_limit_bytes=40 << 20),
+        compiler_params=pltpu.CompilerParams(vmem_limit_bytes=28 << 20),
         cost_estimate=pl.CostEstimate(flops=0, bytes_accessed=30 << 20, transcendentals=0),
         name="patches",
-    )(slot_pos, grid, *faces)
+    )(slot_pos, meta, grid, *faces)
 
 
 def weight_gradient(slot_pos, meta, grid, faces, xt):
-    half = jax.ShapeDtypeStruct((BLOCKS, BROWS, CH), F32)
+    half = pltpu.VMEM((BLOCKS, BROWS, CH), F32)
     return pl.pallas_call(
         weight_kernel,
         out_shape=(PATCH_SHAPE, half, half),
@@ -199,7 +238,7 @@
         in_specs=[SMEM, SMEM] + [VMEM] * 5 + [pl.BlockSpec((1, CH, VOX), lambda s: (s, 0, 0))],
         out_specs=(PATCH_SPEC, VMEM, VMEM),
         scratch_shapes=[HALO, pltpu.VMEM(((OFFSETS + 1) * CH, CH), F32)],
-        compiler_params=pltpu.CompilerParams(vmem_limit_bytes=48 << 20),
+        compiler_params=pltpu.CompilerParams(vmem_limit_bytes=32 << 20),
         cost_estimate=pl.CostEstimate(flops=2 * 4096 * OFFSETS * CH * CH, bytes_accessed=30 << 20, transcendentals=0),
         name="weight_gradient",
     )(slot_pos, meta, grid, *faces, xt)
@@ -239,7 +278,7 @@
         compiler_params=pltpu.CompilerParams(vmem_limit_bytes=16 << 20),
         cost_estimate=pl.CostEstimate(flops=count * 4 * VOX * OFFSETS * CH * CH, bytes_accessed=count << 20, transcendentals=0),
         name="convolve",
-    )(slot_pos, occupancy, patch, weights, *extra)
+    )(slot_pos, occupancy, pin(patch, pltpu.HBM), weights, *extra)
 
 
 def finish_kernel(meta_ref, own_ref, other_ref, out_ref, rows):
@@ -304,66 +343,93 @@
     def swap(value, axis, k):
         return lax.ppermute(value, AXES, [(number(a), number(mate(a, axis, k))) for a in everyone])
 
-    def shift_wide(value, step):
-        pairs = [(i * narrow + j, (i + step) * narrow + j) for i in range(wide) for j in range(narrow) if 0 <= i + step < wide]
+    def exchange_wide(value, start):
+        pairs = [(i * narrow + j, k * narrow + j) for a in range(start, wide - 1, 2) for i, k in ((a, a + 1), (a + 1, a)) for j in range(narrow)]
         return lax.ppermute(value, AXES, pairs)
 
-    def shift_narrow(value, step):
-        pairs = [(i * narrow + j, i * narrow + j + step) for i in range(wide) for j in range(narrow) if 0 <= j + step < narrow]
+    def exchange_narrow(value, start):
+        pairs = [(i * narrow + j, i * narrow + k) for i in range(wide) for a in range(start, narrow - 1, 2) for j, k in ((a, a + 1), (a + 1, a))]
         return lax.ppermute(value, AXES, pairs)
 
     first, second = ("y", "x"), ("x", "y")
+
+    def tie(*values):
+        return lax.optimization_barrier(values)
 
     def scatter(value, axis):
         n = value.shape[0] // 4
-        parts = [swap(value[k * n : (k + 1) * n], axis, k) for k in (2, 1, 3)]
-        return value[:n] + parts[0] + parts[1] + parts[2]
-
-    def gather(value, axis):
-        got = {k: swap(value, axis, k) for k in (2, 1, 3)}
-        return jnp.concatenate([value, got[1], got[2], got[3]], axis=0)
-
-    def double(value, axis, ks):
-        total = value
-        for part in [swap(value, axis, k) for k in ks]:
+        return [swap(value[k * n : (k + 1) * n], axis, k) for k in (2, 1, 3)]
+
+    def add(value, parts):
+        total = value[: parts[0].shape[0]]
+        for part in parts:
             total = total + part
         return total
+
+    def copies(value, axis, ks):
+        return [swap(value, axis, k) for k in ks]
+
+    def join(value, parts):
+        return jnp.concatenate([value, parts[1], parts[0], parts[2]], axis=0)
 
     def shards(features, weights, cotangent, occupancy, slot_pos):
         core = lax.axis_index("core")
         x_at = lax.axis_index("x")
         y_at = lax.axis_index("y_hi") * n_y_lo + lax.axis_index("y_lo")
         yx, xy = y_at * 4 + x_at, x_at * 4 + y_at
-        meta = jnp.stack([core, jnp.where(core == 0, yx, xy), jnp.where(core == 0, xy, yx)]).astype(jnp.int32)
-        xg, cg, lo, hi, side_lo, side_hi, xt = place(slot_pos, occupancy, features, cotangent)
-        before = shift_wide(hi, 1)
-        after = shift_wide(lo, -1)
-        rim_hi = jnp.concatenate([before[:, None, NY - 1], side_hi, after[:, None, NY - 1]], axis=1)
-        rim_lo = jnp.concatenate([before[:, None, 0], side_lo, after[:, None, 0]], axis=1)
-        left = shift_narrow(rim_hi, 1)
-        right = shift_narrow(rim_lo, -1)
-        cot_faces = (before[0], after[0], left[0], right[0])
-        in_faces = (before[1], after[1], left[1], right[1])
-        cot_patch, keep, send = weight_gradient(slot_pos, meta, cg, cot_faces, xt)
-        in_patch = patches(slot_pos, xg, in_faces)
+        odd_x = x_at & 1
+        meta = jnp.stack([core, jnp.where(core == 0, yx, xy), jnp.where(core == 0, xy, yx), odd_x]).astype(jnp.int32)
+        xg, cg, xt, even, odd, side_even, side_odd = place(slot_pos, meta, occupancy, features, cotangent)
+        even, odd, source = tie(even, odd, weights)
+        even = exchange_wide(even, 0)
+        odd = exchange_wide(odd, 1)
+        w_backward = source[::-1].transpose(0, 2, 1).reshape(OFFSETS * CH, CH)
+        even, odd, w_backward = tie(even, odd, w_backward)
+        before, after = jnp.where(odd_x == 0, odd, even), jnp.where(odd_x == 0, even, odd)
+
+        def rim(side, top):
+            ends = [jnp.where(top, v[:, None, NY - 1], v[:, None, 0]) for v in (before, after)]
+            return jnp.concatenate([ends[0], side, ends[1]], axis=1)
+
+        side_even = exchange_narrow(rim(side_even, core == 0), 0)
+        side_odd = exchange_narrow(rim(side_odd, core == 1), 1)
+        faces = (even, odd, side_even, side_odd)
+        cot_patch, keep, send = weight_gradient(slot_pos, meta, cg, [f[0] for f in faces], xt)
         w_forward = weights.reshape(OFFSETS * CH, CH)
-        w_backward = weights[::-1].transpose(0, 2, 1).reshape(OFFSETS * CH, CH)
-
-        total = keep + swap(send, "core", 1)
-        total = scatter(total, first)
-        total = scatter(total, second)
-        total = double(total, "z", (2, 1, 3))
-        total = double(total, "z", (4,))
-        total = gather(total, second)
-        total = gather(total, first)
-        grad_weight = finish(meta, total, swap(total, "core", 1))
-
-        outputs = grad_input = None
-        for s in range(0, SLOTS, 2):
-            outputs = convolve(slot_pos, occupancy, in_patch, w_forward, outputs, s, 2)
-        for s in range(0, SLOTS, 2):
-            grad_input = convolve(slot_pos, occupancy, cot_patch, w_backward, grad_input, s, 2)
-        return outputs, grad_input, grad_weight
+        done = {"outputs": None, "grad_input": None, "patch": None}
+
+        def backward(at, pos):
+            done["grad_input"] = convolve(pos, occupancy, cot_patch, w_backward, done["grad_input"], *at)
+            return "grad_input"
+
+        def forward(at, pos):
+            done["outputs"] = convolve(pos, occupancy, done["patch"], w_forward, done["outputs"], *at)
+            return "outputs"
+
+        def gather_patches(at, pos):
+            done["patch"] = patches(pos, meta, xg, [f[1] for f in faces])
+            return "patch"
+
+        def stage(value, start, *work):
+            value, pos = tie(value, slot_pos)
+            parts = start(value)
+            names = {call(at, pos) for call, at in work}
+            held = tie(parts, *[done[n] for n in sorted(names)])
+            for n, v in zip(sorted(names), held[1:]):
+                done[n] = v
+            return value, held[0]
+
+        _, (got,) = stage(send, lambda v: copies(v, "core", (1,)), (backward, (0, 1)))
+        total = keep + got
+        total = add(*stage(total, lambda v: scatter(v, first), (backward, (1, 4))))
+        total = add(*stage(total, lambda v: scatter(v, second), (backward, (5, 2))))
+        total = add(*stage(total, lambda v: copies(v, "z", (2, 1, 3)), (gather_patches, None)))
+        total = add(*stage(total, lambda v: copies(v, "z", (4,)), (backward, (7, 1)), (forward, (0, 1))))
+        total = join(*stage(total, lambda v: copies(v, second, (2, 1, 3)), (forward, (1, 2))))
+        total = join(*stage(total, lambda v: copies(v, first, (2, 1, 3)), (forward, (3, 4))))
+        total, (got,) = stage(total, lambda v: copies(v, "core", (1,)), (forward, (7, 1)))
+        grad_weight = finish(meta, total, got)
+        return done["outputs"], done["grad_input"], grad_weight
 
     return shards
 

time: 143 us -> 117 us (0.82)
  waiting for transfers between devices: 29 us -> 6.88 us
  Pallas kernels: 43.9 us -> 57.7 us
  starting transfers between devices: 58.5 us -> 45.2 us
  local copies, waits for them, and re-layouts: 10.4 us -> 3.92 us
    ppermute x18, waiting for transfers between devices: 21.3 us -> 0.95 us  [swap(): lax.ppermute(value, AXES, [(number(a), number(mate(a, axis, k))) for a in...]
    ppermute x18, starting transfers between devices: 45.2 us -> 37 us  [swap(): lax.ppermute(value, AXES, [(number(a), number(mate(a, axis, k))) for a in...]
    unnamed x33 -> x16, local copies, waits for them, and re-layouts: 8.93 us -> 1.46 us
    pallas_call x8, Pallas kernels: 23.1 us -> 30.4 us  [convolve(): pl.pallas_call(lambda *refs: conv_kernel(first, *refs), out_shape=jax.Sha...]
    ppermute x4, starting transfers between devices: 13.3 us -> 8.24 us  [the longest x2 4.45 us: exchange_narrow(): return lax.ppermute(value, AXES, pairs)]
    pallas_call x1, Pallas kernels: 3.66 us -> 7.97 us  [patches(): pl.pallas_call(patches_kernel, out_shape=PATCH_SHAPE, grid=(SLOTS,), in_s...]
    pallas_call x1, Pallas kernels: 4.19 us -> 6.18 us  [place(): pl.pallas_call(place_kernel, out_shape=(grid, grid, pltpu.HBM((SLOTS, CH,...]
    ppermute x4, waiting for transfers between devices: 7.7 us -> 5.93 us  [the longest x2 5.92 us: exchange_narrow(): return lax.ppermute(value, AXES, pairs)]
  transfers between devices with their start and end apart: 22 -> 22, of which waited for: 15 -> 3; matrix products, arithmetic and copies ran while one was open for 1% -> 2% of each run, Pallas kernels for 19% -> 33%
where the time goes in v2:
time: 117 us; the launch traced here: 116 us
  Pallas kernels  57.7 us (49%)
  starting transfers between devices  45.2 us (39%)
  waiting for transfers between devices  6.88 us (6%)
  local copies, waits for them, and re-layouts  3.92 us (3%)
  other arithmetic  1.63 us (1%)
    ppermute x18, starting transfers between devices, swap(): lax.ppermute(value, AXES, [(number(a), number(mate(a, axis, k))) for a in...  37 us
    pallas_call x8, Pallas kernels, convolve(): pl.pallas_call(lambda *refs: conv_kernel(first, *refs), out_shape=jax.Sha...  30.4 us
    pallas_call x1, Pallas kernels, weight_gradient(): pl.pallas_call(weight_kernel, out_shape=(PATCH_SHAPE, half, half), grid=(...  10.9 us
    pallas_call x1, Pallas kernels, patches(): pl.pallas_call(patches_kernel, out_shape=PATCH_SHAPE, grid=(SLOTS,), in_s...  7.97 us
    pallas_call x1, Pallas kernels, place(): pl.pallas_call(place_kernel, out_shape=(grid, grid, pltpu.HBM((SLOTS, CH,...  6.18 us
    ppermute x2, waiting for transfers between devices, exchange_narrow(): return lax.ppermute(value, AXES, pairs)  5.92 us
    ppermute x2, starting transfers between devices, exchange_narrow(): return lax.ppermute(value, AXES, pairs)  4.45 us
    ppermute x2, starting transfers between devices, exchange_wide(): return lax.ppermute(value, AXES, pairs)  3.79 us
  transfers between devices with their start and end apart: 22, of which 3 were waited for; matrix products, arithmetic and copies ran while one was open for 2% of the time, Pallas kernels for 33%

profile of v2, /device:TPU:1, one launch (start us, length us, event | category | flops | bytes accessed | tf_op | source)
XLA Modules:
  0.0 116.2 jit_solution(2177571371332214)
XLA Ops:
  0.7 0.8 copy-done.2
  2.2 6.2 %place.1 = (bf16[32,16,16,128]{3,2,1,0:T(8,128)(2,1)}, bf16[32,16,16,128]{3,2,1,0:T(8,128)(2,1)}, bf16[8,128,512]{2,1,0:T(8,128)(2,1)}, bf16[2,16,16,128]{3,2,1,...) custom-call(s32[8]{0:T(128)S(1)} %copy-done.4, ...), custom_call_target="tpu_custom_call" | custom-call | tf_op jit(solution)/shard_map/place/pallas_call | solution.py:97
  8.4 2.5 %collective-permute-start = (bf16[2,16,16,128]{3,2,1,0:T(8,128)(2,1)S(1)}, bf16[2,16,16,128]{3,2,1,0:T(8,128)(2,1)}, u32[]{:S(2)}, u32[]{:S(2)}) collective-permute-start(bf16[2,16,16,128]{3,2,1,0:T(8,128)(2,1)S(1)} %get-tuple-element.65), channel_id=1, source_target_pairs={{0,4},{1,5},{2,6},{3,7},{4,0},{5,1},{6,2},{7,3},{8,12},{9,13},{10,... | collective-permute-start | bytes 393224 | tf_op jit(solution)/shard_map/ppermute | solution.py:348
  10.8 1.3 %collective-permute-start.1 = (bf16[2,16,16,128]{3,2,1,0:T(8,128)(2,1)S(1)}, bf16[2,16,16,128]{3,2,1,0:T(8,128)(2,1)}, u32[]{:S(2)}, u32[]{:S(2)}) collective-permute-start(bf16[2,16,16,128]{3,2,1,0:T(8,128)(2,1)S(1)} %get-tuple-element.66), channel_id=1, source_target_pairs={{4,8},{5,9},{6,10},{7,11},{8,4},{9,5},{10,6},{11,7},{12,16},{13,17... | collective-permute-start | bytes 393224 | tf_op jit(solution)/shard_map/ppermute | solution.py:348
  12.2 1.3 %copy.14 = bf16[27,128,128]{2,1,0:T(8,128)(2,1)S(1)} copy(bf16[27,128,128]{1,2,0:T(8,128)(2,1)S(1)} %reverse_bitcast_fusion) | data formatting | bytes 1769472 | tf_op jit(solution)/shard_map/transpose | solution.py:386
  13.6 1.1 broadcast_select_fusion.1
  14.8 4.4 %collective-permute-start.3 = (bf16[2,34,16,128]{3,2,1,0:T(8,128)(2,1)S(1)}, bf16[2,34,16,128]{3,2,1,0:T(8,128)(2,1)S(1)}, u32[]{:S(2)}, u32[]{:S(2)}) collective-permute-start(bf16[2,34,16,128]{3,2,1,0:T(8,128)(2,1)S(1)} %pad_maximum_fusion.2), channel_id=1, source_target_pairs={{1,2},{2,1},{5,6},{6,5},{9,10},{10,9},{13,14},{14,13},{17,18},{18,... | collective-permute-start | bytes 835592 | tf_op jit(solution)/shard_map/ppermute | solution.py:352
  19.4 1.0 slice_bitcast_fusion.4
  20.3 5.9 %collective-permute-done.3 = bf16[2,34,16,128]{3,2,1,0:T(8,128)(2,1)S(1)} collective-permute-done((bf16[2,34,16,128]{3,2,1,0:T(8,128)(2,1)S(1)}, bf16[2,34,16,128]{3,2,1,0:T(8,128)(2,1)S(1)}, u32[]{:S(2)}, u32[]{:S(2)}) %collective-permute-start.3) | collective-permute-done | bytes 278560 | tf_op jit(solution)/shard_map/ppermute | solution.py:352
  26.3 10.9 %weight_gradient.1 = (bf16[8,10,64,1152]{3,2,1,0:T(8,128)(2,1)}, f32[16,112,128]{2,1,0:T(8,128)S(1)}, f32[16,112,128]{2,1,0:T(8,128)S(1)}) custom-call(s32[8]{0:T(128)S(1)} %copy-done.5, s32[4]{0:T(128)S(1)} %pad_add_fusion.meta_ref, bf16[32,16,16,128]{3,2,1,0:T(8,128)(2,1)S(1)} %copy-done.6, bf16[16,16,128]{2,1,0:T(8,128)(2,1)S(1)} %get-tuple-element.143.refs_1_, ...), custom_call_target="tpu_custom_call" | custom-call | flops 3623878656 | bytes 31457280 | tf_op jit(solution)/shard_map/weight_gradient/pallas_call | solution.py:234
  37.2 3.1 %convolve.8.refs_4_ = bf16[8,512,128]{2,1,0:T(8,128)(2,1)} custom-call(s32[8]{0:T(128)S(1)} %copy-done.5, s32[8,512]{1,0:T(8,128)S(1)} %copy-done.3, bf16[8,10,64,1152]{3,2,1,0:T(8,128)(2,1)} %get-tuple-element.77.refs_2_, bf16[3456,128]{1,0:T(8,128)(2,1)S(1)} %bitcast.28), custom_call_target="tpu_custom_call" | custom-call | flops 905969664 | bytes 1048576 | tf_op jit(solution)/shard_map/convolve/pallas_call | solution.py:270
  40.5 3.9 %collective-permute-start.5 = (f32[4,112,128]{2,1,0:T(8,128)S(1)}, f32[4,112,128]{2,1,0:T(8,128)S(1)}, u32[]{:S(2)}, u32[]{:S(2)}) collective-permute-start(f32[4,112,128]{2,1,0:T(8,128)S(1)} %get-tuple-element.123), channel_id=1, source_target_pairs={{0,128},{1,9},{2,130},{3,11},{4,132},{5,13},{6,134},{7,15},{8,136}... | collective-permute-start | bytes 688136 | tf_op jit(solution)/shard_map/ppermute | solution.py:344
  44.4 2.3 %collective-permute-start.6 = (f32[4,112,128]{2,1,0:T(8,128)S(1)}, f32[4,112,128]{2,1,0:T(8,128)S(1)}, u32[]{:S(2)}, u32[]{:S(2)}) collective-permute-start(f32[4,112,128]{2,1,0:T(8,128)S(1)} %get-tuple-element.122), channel_id=1, source_target_pairs={{0,2},{1,5},{2,0},{3,7},{4,6},{5,1},{6,4},{7,3},{8,10},{9,13},{10,... | collective-permute-start | bytes 688136 | tf_op jit(solution)/shard_map/ppermute | solution.py:344
  46.7 6.8 %convolve.9.refs_4_ = bf16[8,512,128]{2,1,0:T(8,128)(2,1)} custom-call(s32[8]{0:T(128)S(1)} %copy-done.5, s32[8,512]{1,0:T(8,128)S(1)} %copy-done.3, bf16[8,10,64,1152]{3,2,1,0:T(8,128)(2,1)} %get-tuple-element.77.refs_2_, bf16[3456,128]{1,0:T(8,128)(2,1)S(1)} %bitcast.29, bf16[8,512,128]{2,1,0:T(8,128)(2,1)} %convolve.8.refs_4_), custom_call_target="tpu_custom_call", output_to_operand_aliasing={{}: (4, {})} | custom-call | flops 3623878656 | bytes 4194304 | tf_op jit(solution)/shard_map/convolve/pallas_call | solution.py:270
  53.6 6.7 %collective-permute-start.10 = (f32[1,112,128]{2,1,0:T(8,128)S(1)}, f32[1,112,128]{2,1,0:T(8,128)S(1)}, u32[]{:S(2)}, u32[]{:S(2)}) collective-permute-start(f32[1,112,128]{2,1,0:T(8,128)S(1)} %get-tuple-element.130), channel_id=1, source_target_pairs={{0,12},{1,131},{2,14},{3,129},{4,8},{5,135},{6,10},{7,133},{8,4},{... | collective-permute-start | bytes 172040 | tf_op jit(solution)/shard_map/ppermute | solution.py:344
  60.4 0.7 collective-permute-start.9
  61.1 3.2 %convolve.10.refs_4_ = bf16[8,512,128]{2,1,0:T(8,128)(2,1)} custom-call(s32[8]{0:T(128)S(1)} %copy-done.5, s32[8,512]{1,0:T(8,128)S(1)} %copy-done.3, bf16[8,10,64,1152]{3,2,1,0:T(8,128)(2,1)} %get-tuple-element.77.refs_2_, bf16[3456,128]{1,0:T(8,128)(2,1)S(1)} %bitcast.30, bf16[8,512,128]{2,1,0:T(8,128)(2,1)} %convolve.9.refs_4_), custom_call_target="tpu_custom_call", output_to_operand_aliasing={{}: (4, {})} | custom-call | flops 1811939328 | bytes 2097152 | tf_op jit(solution)/shard_map/convolve/pallas_call | solution.py:270
  64.2 0.7 collective-permute-done.8
  65.1 2.9 %collective-permute-start.12 = (f32[1,112,128]{2,1,0:T(8,128)S(1)}, f32[1,112,128]{2,1,0:T(8,128)S(1)}, u32[]{:S(2)}, u32[]{:S(2)}) collective-permute-start(f32[1,112,128]{2,1,0:T(8,128)S(1)} %add_add_fusion.2), channel_id=1, source_target_pairs={{0,16},{1,17},{2,18},{3,19},{4,20},{5,21},{6,22},{7,23},{8,24},{9,... | collective-permute-start | bytes 172040 | tf_op jit(solution)/shard_map/ppermute | solution.py:344
  68.6 8.0 %patches.1.refs_2_ = bf16[8,10,64,1152]{3,2,1,0:T(8,128)(2,1)} custom-call(s32[8]{0:T(128)S(1)} %copy-done.5, s32[4]{0:T(128)S(1)} %pad_add_fusion.meta_ref, bf16[32,16,16,128]{3,2,1,0:T(8,128)(2,1)S(1)} %copy-done.1, bf16[16,16,128]{2,1,0:T(8,128)(2,1)S(1)} %get-tuple-element.144.refs_1_, bf16[16,16,128]{2,1,0:T(8,128)(2,1)S(1)} %get-tuple-element.133.refs_2_, ...), custom_call_target="tpu_custom_call" | custom-call | bytes 31457280 | tf_op jit(solution)/shard_map/patches/pallas_call | solution.py:219
  76.6 4.3 %collective-permute-start.14 = (f32[1,112,128]{2,1,0:T(8,128)S(1)}, f32[1,112,128]{2,1,0:T(8,128)S(1)}, u32[]{:S(2)}, u32[]{:S(2)}) collective-permute-start(f32[1,112,128]{2,1,0:T(8,128)S(1)} %add_add_fusion.1), channel_id=1, source_target_pairs={{0,64},{1,65},{2,66},{3,67},{4,68},{5,69},{6,70},{7,71},{8,72},{9,... | collective-permute-start | bytes 172040 | tf_op jit(solution)/shard_map/ppermute | solution.py:344
  80.9 2.1 %convolve.11 = bf16[8,512,128]{2,1,0:T(8,128)(2,1)} custom-call(s32[8]{0:T(128)S(1)} %copy-done.5, s32[8,512]{1,0:T(8,128)S(1)} %copy-done.3, bf16[8,10,64,1152]{3,2,1,0:T(8,128)(2,1)} %get-tuple-element.77.refs_2_, bf16[3456,128]{1,0:T(8,128)(2,1)S(1)} %bitcast.31, bf16[8,512,128]{2,1,0:T(8,128)(2,1)} %convolve.10.refs_4_), custom_call_target="tpu_custom_call", output_to_operand_aliasing={{}: (4, {})} | custom-call | flops 905969664 | bytes 1048576 | tf_op jit(solution)/shard_map/convolve/pallas_call | solution.py:270
  83.0 3.1 %convolve.12.refs_4_ = bf16[8,512,128]{2,1,0:T(8,128)(2,1)} custom-call(s32[8]{0:T(128)S(1)} %copy-done.5, s32[8,512]{1,0:T(8,128)S(1)} %copy-done.3, bf16[8,10,64,1152]{3,2,1,0:T(8,128)(2,1)} %patches.1.refs_2_, bf16[3456,128]{1,0:T(8,128)(2,1)S(1)} %bitcast.24), custom_call_target="tpu_custom_call" | custom-call | flops 905969664 | bytes 1048576 | tf_op jit(solution)/shard_map/convolve/pallas_call | solution.py:270
  86.1 2.0 %collective-permute-start.15 = (f32[1,112,128]{2,1,0:T(8,128)S(1)}, f32[1,112,128]{2,1,0:T(8,128)S(1)}, u32[]{:S(2)}, u32[]{:S(2)}) collective-permute-start(f32[1,112,128]{2,1,0:T(8,128)S(1)} %add.55), channel_id=1, source_target_pairs={{0,8},{1,129},{2,10},{3,131},{4,12},{5,133},{6,14},{7,135},{8,0},{... | collective-permute-start | bytes 172040 | tf_op jit(solution)/shard_map/ppermute | solution.py:344
  88.1 1.6 %collective-permute-start.17 = (f32[1,112,128]{2,1,0:T(8,128)S(1)}, f32[1,112,128]{2,1,0:T(8,128)S(1)}, u32[]{:S(2)}, u32[]{:S(2)}) collective-permute-start(f32[1,112,128]{2,1,0:T(8,128)S(1)} %add.55), channel_id=1, source_target_pairs={{0,12},{1,131},{2,14},{3,129},{4,8},{5,135},{6,10},{7,133},{8,4},{... | collective-permute-start | bytes 172040 | tf_op jit(solution)/shard_map/ppermute | solution.py:344
  89.8 4.2 %convolve.13.refs_4_ = bf16[8,512,128]{2,1,0:T(8,128)(2,1)} custom-call(s32[8]{0:T(128)S(1)} %copy-done.5, s32[8,512]{1,0:T(8,128)S(1)} %copy-done.3, bf16[8,10,64,1152]{3,2,1,0:T(8,128)(2,1)} %patches.1.refs_2_, bf16[3456,128]{1,0:T(8,128)(2,1)S(1)} %bitcast.25, bf16[8,512,128]{2,1,0:T(8,128)(2,1)} %convolve.12.refs_4_), custom_call_target="tpu_custom_call", output_to_operand_aliasing={{}: (4, {})} | custom-call | flops 1811939328 | bytes 2097152 | tf_op jit(solution)/shard_map/convolve/pallas_call | solution.py:270
  94.0 2.5 %collective-permute-start.18 = (f32[4,112,128]{2,1,0:T(8,128)S(1)}, f32[4,112,128]{2,1,0:T(8,128)S(1)}, u32[]{:S(2)}, u32[]{:S(2)}) collective-permute-start(f32[4,112,128]{2,1,0:T(8,128)S(1)} %pad_maximum_fusion.3), channel_id=1, source_target_pairs={{0,128},{1,9},{2,130},{3,11},{4,132},{5,13},{6,134},{7,15},{8,136}... | collective-permute-start | bytes 688136 | tf_op jit(solution)/shard_map/ppermute | solution.py:344
  96.6 1.3 %collective-permute-start.19 = (f32[4,112,128]{2,1,0:T(8,128)S(1)}, f32[4,112,128]{2,1,0:T(8,128)S(1)}, u32[]{:S(2)}, u32[]{:S(2)}) collective-permute-start(f32[4,112,128]{2,1,0:T(8,128)S(1)} %pad_maximum_fusion.3), channel_id=1, source_target_pairs={{0,2},{1,5},{2,0},{3,7},{4,6},{5,1},{6,4},{7,3},{8,10},{9,13},{10,... | collective-permute-start | bytes 688136 | tf_op jit(solution)/shard_map/ppermute | solution.py:344
  98.2 5.8 %convolve.14.refs_4_ = bf16[8,512,128]{2,1,0:T(8,128)(2,1)} custom-call(s32[8]{0:T(128)S(1)} %copy-done.5, s32[8,512]{1,0:T(8,128)S(1)} %copy-done.3, bf16[8,10,64,1152]{3,2,1,0:T(8,128)(2,1)} %patches.1.refs_2_, bf16[3456,128]{1,0:T(8,128)(2,1)S(1)} %bitcast.26, bf16[8,512,128]{2,1,0:T(8,128)(2,1)} %convolve.13.refs_4_), custom_call_target="tpu_custom_call", output_to_operand_aliasing={{}: (4, {})} | custom-call | flops 3623878656 | bytes 4194304 | tf_op jit(solution)/shard_map/convolve/pallas_call | solution.py:270
  104.3 7.6 %collective-permute-start.21 = (f32[16,112,128]{2,1,0:T(8,128)S(1)}, f32[16,112,128]{2,1,0:T(8,128)S(1)}, u32[]{:S(2)}, u32[]{:S(2)}) collective-permute-start(f32[16,112,128]{2,1,0:T(8,128)S(1)} %pad_maximum_fusion.own_ref), channel_id=1, source_target_pairs={{0,1},{1,0},{2,3},{3,2},{4,5},{5,4},{6,7},{7,6},{8,9},{9,8},{10,11... | collective-permute-start | bytes 2752520 | tf_op jit(solution)/shard_map/ppermute | solution.py:344
  111.9 2.1 %convolve.15 = bf16[8,512,128]{2,1,0:T(8,128)(2,1)} custom-call(s32[8]{0:T(128)S(1)} %copy-done.5, s32[8,512]{1,0:T(8,128)S(1)} %copy-done.3, bf16[8,10,64,1152]{3,2,1,0:T(8,128)(2,1)} %patches.1.refs_2_, bf16[3456,128]{1,0:T(8,128)(2,1)S(1)} %bitcast.27, bf16[8,512,128]{2,1,0:T(8,128)(2,1)} %convolve.14.refs_4_), custom_call_target="tpu_custom_call", output_to_operand_aliasing={{}: (4, {})} | custom-call | flops 905969664 | bytes 1048576 | tf_op jit(solution)/shard_map/convolve/pallas_call | solution.py:270
  114.0 2.2 %finish.1 = f32[27,128,128]{2,1,0:T(8,128)} custom-call(s32[4]{0:T(128)S(1)} %pad_add_fusion.meta_ref, f32[16,112,128]{2,1,0:T(8,128)S(1)} %pad_maximum_fusion.own_ref, f32[16,112,128]{2,1,0:T(8,128)S(1)} %collective-permute-done.21.other_ref), custom_call_target="tpu_custom_call" | custom-call | tf_op jit(solution)/shard_map/finish/pallas_call | solution.py:305
  (59 shorter events, 2.9 us)
Async XLA Ops:
  0.6 11.5 %copy-start = (bf16[27,128,128]{2,1,0:T(8,128)(2,1)S(1)}, bf16[27,128,128]{2,1,0:T(8,128)(2,1)}, u32[]{:S(2)}) copy-start(bf16[27,128,128]{2,1,0:T(8,128)(2,1)} %param.6) | copy-start | bytes 2654212
  0.7 0.8 copy-start.2
  1.5 0.7 copy-start.4
  8.4 5.2 %collective-permute-start = (bf16[2,16,16,128]{3,2,1,0:T(8,128)(2,1)S(1)}, bf16[2,16,16,128]{3,2,1,0:T(8,128)(2,1)}, u32[]{:S(2)}, u32[]{:S(2)}) collective-permute-start(bf16[2,16,16,128]{3,2,1,0:T(8,128)(2,1)S(1)} %get-tuple-element.65), channel_id=1, source_target_pairs={{0,4},{1,5},{2,6},{3,7},{4,0},{5,1},{6,2},{7,3},{8,12},{9,13},{10,... | collective-permute-start | bytes 393224 | tf_op jit(solution)/shard_map/ppermute | solution.py:348
  10.8 2.8 %collective-permute-start.1 = (bf16[2,16,16,128]{3,2,1,0:T(8,128)(2,1)S(1)}, bf16[2,16,16,128]{3,2,1,0:T(8,128)(2,1)}, u32[]{:S(2)}, u32[]{:S(2)}) collective-permute-start(bf16[2,16,16,128]{3,2,1,0:T(8,128)(2,1)S(1)} %get-tuple-element.66), channel_id=1, source_target_pairs={{4,8},{5,9},{6,10},{7,11},{8,4},{9,5},{10,6},{11,7},{12,16},{13,17... | collective-permute-start | bytes 393224 | tf_op jit(solution)/shard_map/ppermute | solution.py:348
  13.6 12.7 %copy-start.5 = (s32[8]{0:T(128)S(1)}, s32[8]{0:T(128)}, u32[]{:S(2)}) copy-start(s32[8]{0:T(128)} %refs_0_.7) | copy-start | bytes 100
  13.6 12.7 %copy-start.6 = (bf16[32,16,16,128]{3,2,1,0:T(8,128)(2,1)S(1)}, bf16[32,16,16,128]{3,2,1,0:T(8,128)(2,1)}, u32[]{:S(2)}) copy-start(bf16[32,16,16,128]{3,2,1,0:T(8,128)(2,1)} %get-tuple-element.62.refs_0_) | copy-start | bytes 6291460
  13.6 12.7 %copy-start.7 = (bf16[8,128,512]{2,1,0:T(8,128)(2,1)S(1)}, bf16[8,128,512]{2,1,0:T(8,128)(2,1)}, u32[]{:S(2)}) copy-start(bf16[8,128,512]{2,1,0:T(8,128)(2,1)} %get-tuple-element.72.refs_5_) | copy-start | bytes 3145732
  14.8 11.4 %collective-permute-start.3 = (bf16[2,34,16,128]{3,2,1,0:T(8,128)(2,1)S(1)}, bf16[2,34,16,128]{3,2,1,0:T(8,128)(2,1)S(1)}, u32[]{:S(2)}, u32[]{:S(2)}) collective-permute-start(bf16[2,34,16,128]{3,2,1,0:T(8,128)(2,1)S(1)} %pad_maximum_fusion.2), channel_id=1, source_target_pairs={{1,2},{2,1},{5,6},{6,5},{9,10},{10,9},{13,14},{14,13},{17,18},{18,... | collective-permute-start | bytes 835592 | tf_op jit(solution)/shard_map/ppermute | solution.py:352
  19.3 7.0 %collective-permute-start.2 = (bf16[2,34,16,128]{3,2,1,0:T(8,128)(2,1)S(1)}, bf16[2,34,16,128]{3,2,1,0:T(8,128)(2,1)S(1)}, u32[]{:S(2)}, u32[]{:S(2)}) collective-permute-start(bf16[2,34,16,128]{3,2,1,0:T(8,128)(2,1)S(1)} %pad_maximum_fusion.1), channel_id=1, source_target_pairs={{0,1},{1,0},{2,3},{3,2},{4,5},{5,4},{6,7},{7,6},{8,9},{9,8},{10,11... | collective-permute-start | bytes 835592 | tf_op jit(solution)/shard_map/ppermute | solution.py:352
  26.3 10.9 %copy-start.3 = (s32[8,512]{1,0:T(8,128)S(1)}, s32[8,512]{1,0:T(8,128)}, u32[]{:S(2)}) copy-start(s32[8,512]{1,0:T(8,128)} %refs_1_.15) | copy-start | bytes 49156
  37.2 3.1 %collective-permute-start.4 = (f32[16,112,128]{2,1,0:T(8,128)S(1)}, f32[16,112,128]{2,1,0:T(8,128)S(1)}, u32[]{:S(2)}, u32[]{:S(2)}) collective-permute-start(f32[16,112,128]{2,1,0:T(8,128)S(1)} %get-tuple-element.75), channel_id=1, source_target_pairs={{0,1},{1,0},{2,3},{3,2},{4,5},{5,4},{6,7},{7,6},{8,9},{9,8},{10,11... | collective-permute-start | bytes 2752520 | tf_op jit(solution)/shard_map/ppermute | solution.py:344
  40.5 13.0 %collective-permute-start.5 = (f32[4,112,128]{2,1,0:T(8,128)S(1)}, f32[4,112,128]{2,1,0:T(8,128)S(1)}, u32[]{:S(2)}, u32[]{:S(2)}) collective-permute-start(f32[4,112,128]{2,1,0:T(8,128)S(1)} %get-tuple-element.123), channel_id=1, source_target_pairs={{0,128},{1,9},{2,130},{3,11},{4,132},{5,13},{6,134},{7,15},{8,136}... | collective-permute-start | bytes 688136 | tf_op jit(solution)/shard_map/ppermute | solution.py:344
  44.4 9.1 %collective-permute-start.6 = (f32[4,112,128]{2,1,0:T(8,128)S(1)}, f32[4,112,128]{2,1,0:T(8,128)S(1)}, u32[]{:S(2)}, u32[]{:S(2)}) collective-permute-start(f32[4,112,128]{2,1,0:T(8,128)S(1)} %get-tuple-element.122), channel_id=1, source_target_pairs={{0,2},{1,5},{2,0},{3,7},{4,6},{5,1},{6,4},{7,3},{8,10},{9,13},{10,... | collective-permute-start | bytes 688136 | tf_op jit(solution)/shard_map/ppermute | solution.py:344
  46.7 6.9 %collective-permute-start.7 = (f32[4,112,128]{2,1,0:T(8,128)S(1)}, f32[4,112,128]{2,1,0:T(8,128)S(1)}, u32[]{:S(2)}, u32[]{:S(2)}) collective-permute-start(f32[4,112,128]{2,1,0:T(8,128)S(1)} %get-tuple-element.121), channel_id=1, source_target_pairs={{0,130},{1,13},{2,128},{3,15},{4,134},{5,9},{6,132},{7,11},{8,138}... | collective-permute-start | bytes 688136 | tf_op jit(solution)/shard_map/ppermute | solution.py:344
  53.6 10.6 %collective-permute-start.10 = (f32[1,112,128]{2,1,0:T(8,128)S(1)}, f32[1,112,128]{2,1,0:T(8,128)S(1)}, u32[]{:S(2)}, u32[]{:S(2)}) collective-permute-start(f32[1,112,128]{2,1,0:T(8,128)S(1)} %get-tuple-element.130), channel_id=1, source_target_pairs={{0,12},{1,131},{2,14},{3,129},{4,8},{5,135},{6,10},{7,133},{8,4},{... | collective-permute-start | bytes 172040 | tf_op jit(solution)/shard_map/ppermute | solution.py:344
  60.4 4.5 %collective-permute-start.8 = (f32[1,112,128]{2,1,0:T(8,128)S(1)}, f32[1,112,128]{2,1,0:T(8,128)S(1)}, u32[]{:S(2)}, u32[]{:S(2)}) collective-permute-start(f32[1,112,128]{2,1,0:T(8,128)S(1)} %get-tuple-element.132), channel_id=1, source_target_pairs={{0,8},{1,129},{2,10},{3,131},{4,12},{5,133},{6,14},{7,135},{8,0},{... | collective-permute-start | bytes 172040 | tf_op jit(solution)/shard_map/ppermute | solution.py:344
  60.4 8.2 %copy-start.1 = (bf16[32,16,16,128]{3,2,1,0:T(8,128)(2,1)S(1)}, bf16[32,16,16,128]{3,2,1,0:T(8,128)(2,1)}, u32[]{:S(2)}) copy-start(bf16[32,16,16,128]{3,2,1,0:T(8,128)(2,1)} %get-tuple-element.94.refs_0_) | copy-start | bytes 6291460
  60.4 4.5 %collective-permute-start.9 = (f32[1,112,128]{2,1,0:T(8,128)S(1)}, f32[1,112,128]{2,1,0:T(8,128)S(1)}, u32[]{:S(2)}, u32[]{:S(2)}) collective-permute-start(f32[1,112,128]{2,1,0:T(8,128)S(1)} %get-tuple-element.131), channel_id=1, source_target_pairs={{0,4},{1,3},{2,6},{3,1},{4,0},{5,7},{6,2},{7,5},{8,12},{9,11},{10,... | collective-permute-start | bytes 172040 | tf_op jit(solution)/shard_map/ppermute | solution.py:344
  64.9 11.6 %collective-permute-start.11 = (f32[1,112,128]{2,1,0:T(8,128)S(1)}, f32[1,112,128]{2,1,0:T(8,128)S(1)}, u32[]{:S(2)}, u32[]{:S(2)}) collective-permute-start(f32[1,112,128]{2,1,0:T(8,128)S(1)} %add_add_fusion.2), channel_id=1, source_target_pairs={{0,32},{1,33},{2,34},{3,35},{4,36},{5,37},{6,38},{7,39},{8,40},{9,... | collective-permute-start | bytes 172040 | tf_op jit(solution)/shard_map/ppermute | solution.py:344
  65.1 11.4 %collective-permute-start.12 = (f32[1,112,128]{2,1,0:T(8,128)S(1)}, f32[1,112,128]{2,1,0:T(8,128)S(1)}, u32[]{:S(2)}, u32[]{:S(2)}) collective-permute-start(f32[1,112,128]{2,1,0:T(8,128)S(1)} %add_add_fusion.2), channel_id=1, source_target_pairs={{0,16},{1,17},{2,18},{3,19},{4,20},{5,21},{6,22},{7,23},{8,24},{9,... | collective-permute-start | bytes 172040 | tf_op jit(solution)/shard_map/ppermute | solution.py:344
  68.0 8.5 %collective-permute-start.13 = (f32[1,112,128]{2,1,0:T(8,128)S(1)}, f32[1,112,128]{2,1,0:T(8,128)S(1)}, u32[]{:S(2)}, u32[]{:S(2)}) collective-permute-start(f32[1,112,128]{2,1,0:T(8,128)S(1)} %add_add_fusion.2), channel_id=1, source_target_pairs={{0,48},{1,49},{2,50},{3,51},{4,52},{5,53},{6,54},{7,55},{8,56},{9,... | collective-permute-start | bytes 172040 | tf_op jit(solution)/shard_map/ppermute | solution.py:344
  76.6 9.5 %collective-permute-start.14 = (f32[1,112,128]{2,1,0:T(8,128)S(1)}, f32[1,112,128]{2,1,0:T(8,128)S(1)}, u32[]{:S(2)}, u32[]{:S(2)}) collective-permute-start(f32[1,112,128]{2,1,0:T(8,128)S(1)} %add_add_fusion.1), channel_id=1, source_target_pairs={{0,64},{1,65},{2,66},{3,67},{4,68},{5,69},{6,70},{7,71},{8,72},{9,... | collective-permute-start | bytes 172040 | tf_op jit(solution)/shard_map/ppermute | solution.py:344
  86.1 7.9 %collective-permute-start.15 = (f32[1,112,128]{2,1,0:T(8,128)S(1)}, f32[1,112,128]{2,1,0:T(8,128)S(1)}, u32[]{:S(2)}, u32[]{:S(2)}) collective-permute-start(f32[1,112,128]{2,1,0:T(8,128)S(1)} %add.55), channel_id=1, source_target_pairs={{0,8},{1,129},{2,10},{3,131},{4,12},{5,133},{6,14},{7,135},{8,0},{... | collective-permute-start | bytes 172040 | tf_op jit(solution)/shard_map/ppermute | solution.py:344
  88.1 5.9 %collective-permute-start.16 = (f32[1,112,128]{2,1,0:T(8,128)S(1)}, f32[1,112,128]{2,1,0:T(8,128)S(1)}, u32[]{:S(2)}, u32[]{:S(2)}) collective-permute-start(f32[1,112,128]{2,1,0:T(8,128)S(1)} %add.55), channel_id=1, source_target_pairs={{0,4},{1,3},{2,6},{3,1},{4,0},{5,7},{6,2},{7,5},{8,12},{9,11},{10,... | collective-permute-start | bytes 172040 | tf_op jit(solution)/shard_map/ppermute | solution.py:344
  88.1 5.9 %collective-permute-start.17 = (f32[1,112,128]{2,1,0:T(8,128)S(1)}, f32[1,112,128]{2,1,0:T(8,128)S(1)}, u32[]{:S(2)}, u32[]{:S(2)}) collective-permute-start(f32[1,112,128]{2,1,0:T(8,128)S(1)} %add.55), channel_id=1, source_target_pairs={{0,12},{1,131},{2,14},{3,129},{4,8},{5,135},{6,10},{7,133},{8,4},{... | collective-permute-start | bytes 172040 | tf_op jit(solution)/shard_map/ppermute | solution.py:344
  94.0 10.0 %collective-permute-start.18 = (f32[4,112,128]{2,1,0:T(8,128)S(1)}, f32[4,112,128]{2,1,0:T(8,128)S(1)}, u32[]{:S(2)}, u32[]{:S(2)}) collective-permute-start(f32[4,112,128]{2,1,0:T(8,128)S(1)} %pad_maximum_fusion.3), channel_id=1, source_target_pairs={{0,128},{1,9},{2,130},{3,11},{4,132},{5,13},{6,134},{7,15},{8,136}... | collective-permute-start | bytes 688136 | tf_op jit(solution)/shard_map/ppermute | solution.py:344
  96.6 7.4 %collective-permute-start.19 = (f32[4,112,128]{2,1,0:T(8,128)S(1)}, f32[4,112,128]{2,1,0:T(8,128)S(1)}, u32[]{:S(2)}, u32[]{:S(2)}) collective-permute-start(f32[4,112,128]{2,1,0:T(8,128)S(1)} %pad_maximum_fusion.3), channel_id=1, source_target_pairs={{0,2},{1,5},{2,0},{3,7},{4,6},{5,1},{6,4},{7,3},{8,10},{9,13},{10,... | collective-permute-start | bytes 688136 | tf_op jit(solution)/shard_map/ppermute | solution.py:344
  97.8 6.4 %collective-permute-start.20 = (f32[4,112,128]{2,1,0:T(8,128)S(1)}, f32[4,112,128]{2,1,0:T(8,128)S(1)}, u32[]{:S(2)}, u32[]{:S(2)}) collective-permute-start(f32[4,112,128]{2,1,0:T(8,128)S(1)} %pad_maximum_fusion.3), channel_id=1, source_target_pairs={{0,130},{1,13},{2,128},{3,15},{4,134},{5,9},{6,132},{7,11},{8,138}... | collective-permute-start | bytes 688136 | tf_op jit(solution)/shard_map/ppermute | solution.py:344
  104.3 9.7 %collective-permute-start.21 = (f32[16,112,128]{2,1,0:T(8,128)S(1)}, f32[16,112,128]{2,1,0:T(8,128)S(1)}, u32[]{:S(2)}, u32[]{:S(2)}) collective-permute-start(f32[16,112,128]{2,1,0:T(8,128)S(1)} %pad_maximum_fusion.own_ref), channel_id=1, source_target_pairs={{0,1},{1,0},{2,3},{3,2},{4,5},{5,4},{6,7},{7,6},{8,9},{9,8},{10,11... | collective-permute-start | bytes 2752520 | tf_op jit(solution)/shard_map/ppermute | solution.py:344

commit v3 on v2

--- a/solution.py
+++ b/solution.py
@@ -17,6 +17,7 @@
 KROW = 9 * CH
 BLOCKS = 16
 BROWS = 112
+PROWS = 80
 F32 = jnp.float32
 BF16 = jnp.bfloat16
 VMEM = pl.BlockSpec(memory_space=pltpu.VMEM)
@@ -113,56 +114,57 @@
     )(slot_pos, meta, occupancy, pin(features, pltpu.HBM), pin(cotangent, pltpu.HBM))
 
 
-def assemble(meta_ref, grid_ref, even_ref, odd_ref, side_even_ref, side_odd_ref, halo):
+def shifted(v):
+    n = v.shape[0]
+    flat = v.astype(F32).reshape(n * NZ, CH)
+    z = lax.broadcasted_iota(jnp.int32, flat.shape, 0) & (NZ - 1)
+    back = jnp.where(z == 0, 0.0, pltpu.roll(flat, 1, axis=0))
+    ahead = jnp.where(z == NZ - 1, 0.0, pltpu.roll(flat, n * NZ - 1, axis=0))
+    return [a.reshape(n, 2, 8, CH) for a in (back, flat, ahead)]
+
+
+def assemble(meta_ref, grid_ref, side_even_ref, side_odd_ref, halo, planes=None):
     core, odd_x = meta_ref[0], meta_ref[3]
 
-    def shifted(v):
-        n = v.shape[0]
-        flat = v.astype(F32).reshape(n * NZ, CH)
-        z = lax.broadcasted_iota(jnp.int32, flat.shape, 0) & (NZ - 1)
-        back = jnp.where(z == 0, 0.0, pltpu.roll(flat, 1, axis=0))
-        ahead = jnp.where(z == NZ - 1, 0.0, pltpu.roll(flat, n * NZ - 1, axis=0))
-        return [a.reshape(n, 2, 8, CH) for a in (back, flat, ahead)]
-
-    def put_plane(x, v):
-        for r, a in enumerate(shifted(v)):
+    def body(x, carry):
+        for r, a in enumerate(shifted(grid_ref[x])):
             for bz in range(2):
-                halo[r, bz, x, pl.ds(1, NY)] = a[:, bz]
-
-    def body(x, carry):
-        put_plane(x + 1, grid_ref[x])
+                halo[r, bz, x + 1, pl.ds(1, NY)] = a[:, bz]
         return carry
 
     lax.fori_loop(0, NX, body, 0)
-    put_plane((NX + 1) * (1 - odd_x), even_ref[...])
-    put_plane((NX + 1) * odd_x, odd_ref[...])
     for y, ref in (((NY + 1) * (1 - core), side_even_ref), ((NY + 1) * core, side_odd_ref)):
         for r, a in enumerate(shifted(ref[...])):
             for bz in range(2):
-                halo[r, bz, :, y] = a[:, bz]
+                halo[r, bz, pl.ds(1, NX), y] = a[:, bz]
+    for i, x in enumerate(((NX + 1) * (1 - odd_x), (NX + 1) * odd_x)):
+        if planes is None:
+            halo[:, :, x] = jnp.zeros((3, 2, NY + 2, 8, CH), F32)
+        else:
+            for r, a in enumerate(shifted(planes[i][...])):
+                for bz in range(2):
+                    halo[r, bz, x] = a[:, bz]
 
 
 def build_patches(pos, halo, patch_ref):
     bx, by, bz = brick_of(pos)
     for x in range(10):
-        for q in range(3):
-            for r in range(3):
-                rows = halo[r, bz, bx * 8 + x, pl.ds(by * 8 + q, 8)]
-                k = (q * 3 + r) * CH
-                patch_ref[0, x, :, k : k + CH] = rows.reshape(64, CH).astype(BF16)
+        for r in range(3):
+            rows = halo[r, bz, bx * 8 + x, pl.ds(by * 8, 10)]
+            patch_ref[0, x, :, r * CH : (r + 1) * CH] = rows.reshape(PROWS, CH).astype(BF16)
 
 
 def patch_rows(patch_ref, p):
-    return patch_ref[0, pl.ds(p, 8)].reshape(VOX, KROW)
-
-
-def patches_kernel(pos_ref, meta_ref, *refs):
-    patch_ref, halo = refs[5:]
+    parts = [patch_ref[0, pl.ds(p, 8), pl.ds(q * 8, 64)].reshape(VOX, 3 * CH) for q in range(3)]
+    return jnp.concatenate(parts, axis=1)
+
+
+def patches_kernel(pos_ref, meta_ref, grid_ref, side_even_ref, side_odd_ref, even_ref, odd_ref, patch_ref, halo):
     s = pl.program_id(0)
 
     @pl.when(s == 0)
     def _():
-        assemble(meta_ref, *refs[:5], halo)
+        assemble(meta_ref, grid_ref, side_even_ref, side_odd_ref, halo, (even_ref, odd_ref))
 
     pos = pos_ref[s]
 
@@ -171,13 +173,12 @@
         build_patches(pos, halo, patch_ref)
 
 
-def weight_kernel(pos_ref, meta_ref, *refs):
-    xt_ref, patch_ref, keep_ref, send_ref, halo, total = refs[5:]
+def weight_kernel(pos_ref, meta_ref, grid_ref, side_even_ref, side_odd_ref, xt_ref, patch_ref, total, halo):
     s = pl.program_id(0)
 
     @pl.when(s == 0)
     def _():
-        assemble(meta_ref, *refs[:5], halo)
+        assemble(meta_ref, grid_ref, side_even_ref, side_odd_ref, halo)
 
         def clear(o, carry):
             total[pl.ds(pl.multiple_of(o * CH, CH), CH)] = jnp.zeros((CH, CH), F32)
@@ -196,26 +197,71 @@
                 row = (OFFSETS - 1 - (p * 9 + k)) * CH
                 total[row : row + CH] += terms[:, k * CH : (k + 1) * CH]
 
-    @pl.when(s == SLOTS - 1)
-    def _():
-        core, own, other = meta_ref[0], meta_ref[1], meta_ref[2]
-
-        def emit(j, carry):
-            at = pl.multiple_of((core * BLOCKS + (j ^ own)) * BROWS, 8)
-            keep_ref[j] = total[pl.ds(at, BROWS)]
-            at = pl.multiple_of(((1 - core) * BLOCKS + (j ^ other)) * BROWS, 8)
-            send_ref[j] = total[pl.ds(at, BROWS)]
-            return carry
-
-        lax.fori_loop(0, BLOCKS, emit, 0)
-
-
-PATCH_SHAPE = pltpu.HBM((SLOTS, 10, 64, KROW), BF16)
-PATCH_SPEC = pl.BlockSpec((1, 10, 64, KROW), lambda s, *_: (s, 0, 0, 0))
+
+def rim_kernel(pos_ref, meta_ref, even_ref, odd_ref, xt_ref, total_ref, patch_in, patch_out, keep_ref, send_ref, rims, rows, total, sems):
+    core, own, other, odd_x = meta_ref[0], meta_ref[1], meta_ref[2], meta_ref[3]
+    for i, ref in enumerate((even_ref, odd_ref)):
+        at = 1 - odd_x if i == 0 else odd_x
+        for r, a in enumerate(shifted(ref[...])):
+            for bz in range(2):
+                rims[at, r, bz] = a[:, bz]
+
+    def clear(o, carry):
+        at = pl.ds(pl.multiple_of(o * CH, CH), CH)
+        total[at] = total_ref[at]
+        return carry
+
+    lax.fori_loop(0, OFFSETS + 1, clear, 0)
+
+    def store(s, end):
+        return pltpu.make_async_copy(rows.at[s], patch_out.at[s, 9 * end], sems.at[s])
+
+    for s in range(SLOTS):
+        pos = pos_ref[s]
+        for end, edge in ((0, 0), (1, 3)):
+
+            @pl.when((pos >= 0) & ((pos >> 2) == edge))
+            def _():
+                _, by, bz = brick_of(pos)
+                for r in range(3):
+                    part = rims[end, r, bz, pl.ds(by * 8, 10)]
+                    rows[s, :, r * CH : (r + 1) * CH] = part.reshape(PROWS, CH).astype(BF16)
+                store(s, end).start()
+                patch = jnp.concatenate([rows[s, pl.ds(q * 8, 64)] for q in range(3)], axis=1)
+                blank = jnp.zeros_like(patch)
+                if end == 0:
+                    left, right = xt_ref[s, :, :CH], jnp.concatenate([patch, blank], axis=0)
+                else:
+                    left, right = xt_ref[s, :, VOX - CH :], jnp.concatenate([blank, patch], axis=0)
+                terms = jnp.dot(left, right, preferred_element_type=F32)
+                for k in range(9):
+                    row = (OFFSETS - 1 - (18 * end + k)) * CH
+                    total[row : row + CH] += terms[:, k * CH : (k + 1) * CH]
+
+    def emit(j, carry):
+        at = pl.multiple_of((core * BLOCKS + (j ^ own)) * BROWS, 8)
+        keep_ref[j] = total[pl.ds(at, BROWS)]
+        at = pl.multiple_of(((1 - core) * BLOCKS + (j ^ other)) * BROWS, 8)
+        send_ref[j] = total[pl.ds(at, BROWS)]
+        return carry
+
+    lax.fori_loop(0, BLOCKS, emit, 0)
+    for s in range(SLOTS):
+        pos = pos_ref[s]
+        for end, edge in ((0, 0), (1, 3)):
+
+            @pl.when((pos >= 0) & ((pos >> 2) == edge))
+            def _():
+                store(s, end).wait()
+
+
+PATCH_SHAPE = pltpu.HBM((SLOTS, 10, PROWS, 3 * CH), BF16)
+PATCH_SPEC = pl.BlockSpec((1, 10, PROWS, 3 * CH), lambda s, *_: (s, 0, 0, 0))
 HALO = pltpu.VMEM((3, 2, NX + 2, NY + 2, 8, CH), F32)
-
-
-def patches(slot_pos, meta, grid, faces):
+TOTAL = pltpu.VMEM(((OFFSETS + 1) * CH, CH), F32)
+
+
+def patches(slot_pos, meta, grid, sides, planes):
     return pl.pallas_call(
         patches_kernel,
         out_shape=PATCH_SHAPE,
@@ -224,24 +270,43 @@
         out_specs=PATCH_SPEC,
         scratch_shapes=[HALO],
         compiler_params=pltpu.CompilerParams(vmem_limit_bytes=28 << 20),
-        cost_estimate=pl.CostEstimate(flops=0, bytes_accessed=30 << 20, transcendentals=0),
+        cost_estimate=pl.CostEstimate(flops=0, bytes_accessed=20 << 20, transcendentals=0),
         name="patches",
-    )(slot_pos, meta, grid, *faces)
-
-
-def weight_gradient(slot_pos, meta, grid, faces, xt):
-    half = pltpu.VMEM((BLOCKS, BROWS, CH), F32)
+    )(slot_pos, meta, grid, *sides, *planes)
+
+
+def weight_gradient(slot_pos, meta, grid, sides, xt):
     return pl.pallas_call(
         weight_kernel,
+        out_shape=(PATCH_SHAPE, TOTAL),
+        grid=(SLOTS,),
+        in_specs=[SMEM, SMEM] + [VMEM] * 3 + [pl.BlockSpec((1, CH, VOX), lambda s: (s, 0, 0))],
+        out_specs=(PATCH_SPEC, VMEM),
+        scratch_shapes=[HALO],
+        compiler_params=pltpu.CompilerParams(vmem_limit_bytes=30 << 20),
+        cost_estimate=pl.CostEstimate(flops=2 * 4096 * OFFSETS * CH * CH, bytes_accessed=20 << 20, transcendentals=0),
+        name="weight_gradient",
+    )(slot_pos, meta, grid, *sides, xt)
+
+
+def rim_terms(slot_pos, meta, planes, xt, total, patch):
+    half = pltpu.VMEM((BLOCKS, BROWS, CH), F32)
+    hbm = pl.BlockSpec(memory_space=pltpu.HBM)
+    return pl.pallas_call(
+        rim_kernel,
         out_shape=(PATCH_SHAPE, half, half),
-        grid=(SLOTS,),
-        in_specs=[SMEM, SMEM] + [VMEM] * 5 + [pl.BlockSpec((1, CH, VOX), lambda s: (s, 0, 0))],
-        out_specs=(PATCH_SPEC, VMEM, VMEM),
-        scratch_shapes=[HALO, pltpu.VMEM(((OFFSETS + 1) * CH, CH), F32)],
-        compiler_params=pltpu.CompilerParams(vmem_limit_bytes=32 << 20),
-        cost_estimate=pl.CostEstimate(flops=2 * 4096 * OFFSETS * CH * CH, bytes_accessed=30 << 20, transcendentals=0),
-        name="weight_gradient",
-    )(slot_pos, meta, grid, *faces, xt)
+        in_specs=[SMEM, SMEM] + [VMEM] * 4 + [hbm],
+        out_specs=(hbm, VMEM, VMEM),
+        input_output_aliases={6: 0},
+        scratch_shapes=[
+            pltpu.VMEM((2, 3, 2, NY + 2, 8, CH), F32),
+            pltpu.VMEM((SLOTS, PROWS, 3 * CH), BF16),
+            TOTAL,
+            pltpu.SemaphoreType.DMA((SLOTS,)),
+        ],
+        compiler_params=pltpu.CompilerParams(vmem_limit_bytes=20 << 20),
+        name="rim_terms",
+    )(slot_pos, meta, *planes, xt, total, patch)
 
 
 def conv_kernel(first, pos_ref, occ_ref, patch_ref, w_ref, *rest):
@@ -271,7 +336,7 @@
         lambda *refs: conv_kernel(first, *refs),
         out_shape=jax.ShapeDtypeStruct((SLOTS, VOX, CH), BF16),
         grid=(count,),
-        in_specs=[SMEM, VMEM, pl.BlockSpec((1, 10, 64, KROW), lambda i: (first + i, 0, 0, 0)), VMEM]
+        in_specs=[SMEM, VMEM, pl.BlockSpec((1, 10, PROWS, 3 * CH), lambda i: (first + i, 0, 0, 0)), VMEM]
         + [pl.BlockSpec(memory_space=pl.ANY)] * len(extra),
         out_specs=pl.BlockSpec((1, VOX, CH), lambda i: (first + i, 0, 0)),
         input_output_aliases=aliased,
@@ -380,21 +445,23 @@
         odd_x = x_at & 1
         meta = jnp.stack([core, jnp.where(core == 0, yx, xy), jnp.where(core == 0, xy, yx), odd_x]).astype(jnp.int32)
         xg, cg, xt, even, odd, side_even, side_odd = place(slot_pos, meta, occupancy, features, cotangent)
-        even, odd, source = tie(even, odd, weights)
+        side_even, side_odd, source = tie(side_even, side_odd, weights)
+        side_even = exchange_narrow(side_even, 0)
+        side_odd = exchange_narrow(side_odd, 1)
+        w_backward = source[::-1].transpose(0, 2, 1).reshape(OFFSETS * CH, CH)
+        side_even, side_odd, w_backward = tie(side_even, side_odd, w_backward)
+        y_before, y_after = jnp.where(core == 0, side_odd, side_even), jnp.where(core == 0, side_even, side_odd)
+
+        def rim(plane, last):
+            ends = [jnp.where(last, v[:, NX - 1 :], v[:, :1]) for v in (y_before, y_after)]
+            return jnp.concatenate([ends[0], plane, ends[1]], axis=1)
+
+        even, odd, pos = tie(rim(even, odd_x == 0), rim(odd, odd_x == 1), slot_pos)
         even = exchange_wide(even, 0)
         odd = exchange_wide(odd, 1)
-        w_backward = source[::-1].transpose(0, 2, 1).reshape(OFFSETS * CH, CH)
-        even, odd, w_backward = tie(even, odd, w_backward)
-        before, after = jnp.where(odd_x == 0, odd, even), jnp.where(odd_x == 0, even, odd)
-
-        def rim(side, top):
-            ends = [jnp.where(top, v[:, None, NY - 1], v[:, None, 0]) for v in (before, after)]
-            return jnp.concatenate([ends[0], side, ends[1]], axis=1)
-
-        side_even = exchange_narrow(rim(side_even, core == 0), 0)
-        side_odd = exchange_narrow(rim(side_odd, core == 1), 1)
-        faces = (even, odd, side_even, side_odd)
-        cot_patch, keep, send = weight_gradient(slot_pos, meta, cg, [f[0] for f in faces], xt)
+        cot_patch, total = weight_gradient(pos, meta, cg, (side_even[0], side_odd[0]), xt)
+        even, odd, total = tie(even, odd, total)
+        cot_patch, keep, send = rim_terms(slot_pos, meta, (even[0], odd[0]), xt, total, cot_patch)
         w_forward = weights.reshape(OFFSETS * CH, CH)
         done = {"outputs": None, "grad_input": None, "patch": None}
 
@@ -407,7 +474,7 @@
             return "outputs"
 
         def gather_patches(at, pos):
-            done["patch"] = patches(pos, meta, xg, [f[1] for f in faces])
+            done["patch"] = patches(pos, meta, xg, (side_even[1], side_odd[1]), (even[1], odd[1]))
             return "patch"
 
         def stage(value, start, *work):

time: 117 us -> 110 us (0.940); the launches traced: 116 us -> 110 us
  Pallas kernels: 57.7 us -> 48.7 us
  waiting for transfers between devices: 6.88 us -> 8.83 us
  local copies, waits for them, and re-layouts: 3.92 us -> 5.61 us
    pallas_call x8, Pallas kernels: 30.4 us -> 24.8 us  [convolve(): pl.pallas_call(lambda *refs: conv_kernel(first, *refs), out_shape=jax.Sha...]
    ppermute x18, waiting for transfers between devices: 0.95 us -> 5.95 us  [swap(): lax.ppermute(value, AXES, [(number(a), number(mate(a, axis, k))) for a in...]
    ppermute x2, waiting for transfers between devices: 5.92 us -> 2.88 us  [exchange_narrow(): return lax.ppermute(value, AXES, pairs)]
    ppermute x2, starting transfers between devices: 3.79 us -> 0.76 us  [exchange_wide(): return lax.ppermute(value, AXES, pairs)]
    pallas_call x1, Pallas kernels: 7.97 us -> 6.1 us  [patches(): pl.pallas_call(patches_kernel, out_shape=PATCH_SHAPE, grid=(SLOTS,), in_s...]
    transpose x2, local copies, waits for them, and re-layouts: 1.4 us -> 2.94 us  [shards(): w_backward = source[::-1].transpose(0, 2, 1).reshape(OFFSETS * CH, CH)]
    pallas_call x1 -> x2, Pallas kernels: 10.9 us -> 9.39 us  [the longest x1 8.13 us: weight_gradient(): pl.pallas_call(weight_kernel, out_shape=(PATCH_SHAPE, TOTAL), grid=(SLOTS...]
    ppermute x2, starting transfers between devices: 4.45 us -> 5.92 us  [exchange_narrow(): return lax.ppermute(value, AXES, pairs)]
  transfers between devices with their start and end apart: 22 -> 22, of which waited for: 3 -> 6; matrix products, arithmetic and copies ran while one was open for 2% -> 3% of each run, Pallas kernels for 33% -> 35%
where the time goes in v3:
time: 110 us
  Pallas kernels  48.7 us (44%)
  starting transfers between devices  44.9 us (41%)
  waiting for transfers between devices  8.83 us (8%)
  local copies, waits for them, and re-layouts  5.61 us (5%)
  other arithmetic  1.46 us (1%)
    ppermute x18, starting transfers between devices, swap(): lax.ppermute(value, AXES, [(number(a), number(mate(a, axis, k))) for a in...  38.2 us
    pallas_call x8, Pallas kernels, convolve(): pl.pallas_call(lambda *refs: conv_kernel(first, *refs), out_shape=jax.Sha...  24.8 us
    pallas_call x1, Pallas kernels, weight_gradient(): pl.pallas_call(weight_kernel, out_shape=(PATCH_SHAPE, TOTAL), grid=(SLOTS...  8.13 us
    pallas_call x1, Pallas kernels, place(): pl.pallas_call(place_kernel, out_shape=(grid, grid, pltpu.HBM((SLOTS, CH,...  6.2 us
    pallas_call x1, Pallas kernels, patches(): pl.pallas_call(patches_kernel, out_shape=PATCH_SHAPE, grid=(SLOTS,), in_s...  6.1 us
    ppermute x18, waiting for transfers between devices, swap(): lax.ppermute(value, AXES, [(number(a), number(mate(a, axis, k))) for a in...  5.95 us
    ppermute x2, starting transfers between devices, exchange_narrow(): return lax.ppermute(value, AXES, pairs)  5.92 us
    transpose x2, local copies, waits for them, and re-layouts, shards(): w_backward = source[::-1].transpose(0, 2, 1).reshape(OFFSETS * CH, CH)  2.94 us
  transfers between devices with their start and end apart: 22, of which 6 were waited for; matrix products, arithmetic and copies ran while one was open for 3% of the time, Pallas kernels for 35%

profile of v3, /device:TPU:1, one launch (start us, length us, event | category | flops | bytes accessed | tf_op | source)
XLA Modules:
  0.0 110.5 jit_solution(6294479534018903465)
XLA Ops:
  2.2 6.2 %place.1 = (bf16[32,16,16,128]{3,2,1,0:T(8,128)(2,1)}, bf16[32,16,16,128]{3,2,1,0:T(8,128)(2,1)}, bf16[8,128,512]{2,1,0:T(8,128)(2,1)}, bf16[2,16,16,128]{3,2,1,...) custom-call(s32[8]{0:T(128)S(1)} %copy-done.5, ...), custom_call_target="tpu_custom_call" | custom-call | tf_op jit(solution)/shard_map/place/pallas_call | solution.py:98
  8.4 4.0 %collective-permute-start = (bf16[2,32,16,128]{3,2,1,0:T(8,128)(2,1)}, bf16[2,32,16,128]{3,2,1,0:T(8,128)(2,1)}, u32[]{:S(2)}, u32[]{:S(2)}) collective-permute-start(bf16[2,32,16,128]{3,2,1,0:T(8,128)(2,1)} %get-tuple-element.72), channel_id=1, source_target_pairs={{0,1},{1,0},{2,3},{3,2},{4,5},{5,4},{6,7},{7,6},{8,9},{9,8},{10,11... | collective-permute-start | bytes 786440 | tf_op jit(solution)/shard_map/ppermute | solution.py:417
  12.4 1.9 %collective-permute-start.1 = (bf16[2,32,16,128]{3,2,1,0:T(8,128)(2,1)S(1)}, bf16[2,32,16,128]{3,2,1,0:T(8,128)(2,1)}, u32[]{:S(2)}, u32[]{:S(2)}) collective-permute-start(bf16[2,32,16,128]{3,2,1,0:T(8,128)(2,1)S(1)} %get-tuple-element.73), channel_id=1, source_target_pairs={{1,2},{2,1},{5,6},{6,5},{9,10},{10,9},{13,14},{14,13},{17,18},{18,... | collective-permute-start | bytes 786440 | tf_op jit(solution)/shard_map/ppermute | solution.py:417
  15.3 2.0 %copy.15 = bf16[27,128,128]{2,1,0:T(8,128)(2,1)S(1)} copy(bf16[27,128,128]{1,2,0:T(8,128)(2,1)} %reverse_bitcast_fusion) | data formatting | bytes 1769472 | tf_op jit(solution)/shard_map/transpose | solution.py:451
  17.3 2.9 %collective-permute-done.1 = bf16[2,32,16,128]{3,2,1,0:T(8,128)(2,1)} collective-permute-done((bf16[2,32,16,128]{3,2,1,0:T(8,128)(2,1)S(1)}, bf16[2,32,16,128]{3,2,1,0:T(8,128)(2,1)}, u32[]{:S(2)}, u32[]{:S(2)}) %collective-permute-start.1) | collective-permute-done | bytes 262176 | tf_op jit(solution)/shard_map/ppermute | solution.py:417
  20.2 1.1 broadcast_select_fusion.1
  21.2 1.1 %slice_bitcast_fusion = (bf16[32,16,128]{2,1,0:T(8,128)(2,1)S(1)}, bf16[32,16,128]{2,1,0:T(8,128)(2,1)S(1)}, bf16[32,16,128]{2,1,0:T(8,128)(2,1)S(1)}, bf16[32,16,128]{2,1,0:T(8,128)(2,1)S(1)}) fusion(bf16[2,32,16,128]{3,2,1,0:T(8,128)(2,1)} %collective-permute-done.1, bf16[2,32,16,128]{3,2,1,0:T(8,128)(2,1)} %collective-permute-done), kind=kLoop, calls=%fused_computation.8 | loop fusion | bytes 1048576 | tf_op jit(solution)/shard_map/squeeze | solution.py:477
  23.3 8.1 %weight_gradient.1 = (bf16[8,10,80,384]{3,2,1,0:T(8,128)(2,1)}, f32[3584,128]{1,0:T(8,128)S(1)}) custom-call(s32[8]{0:T(128)S(1)} %copy-done.6, s32[4]{0:T(128)S(1)} %pad_add_fusion.meta_ref, bf16[32,16,16,128]{3,2,1,0:T(8,128)(2,1)S(1)} %copy-done.7, bf16[32,16,128]{2,1,0:T(8,128)(2,1)S(1)} %get-tuple-element.159.side_even_ref, ...), custom_call_target="tpu_custom_call" | custom-call | flops 3623878656 | bytes 20971520 | tf_op jit(solution)/shard_map/weight_gradient/pallas_call | solution.py:279
  31.5 1.3 %rim_terms.1 = (bf16[8,10,80,384]{3,2,1,0:T(8,128)(2,1)}, f32[16,112,128]{2,1,0:T(8,128)S(1)}, f32[16,112,128]{2,1,0:T(8,128)S(1)}) custom-call(s32[8]{0:T(128)S(1)} %copy-done.6, s32[4]{0:T(128)S(1)} %pad_add_fusion.meta_ref, bf16[18,16,128]{2,1,0:T(8,128)(2,1)S(1)} %get-tuple-element.156.even_ref, ...), custom_call_target="tpu_custom_call", output_to_operand_aliasing={{0}: (6, {})} | custom-call | tf_op jit(solution)/shard_map/rim_terms/pallas_call | solution.py:295
  32.8 2.8 %convolve.8.refs_4_ = bf16[8,512,128]{2,1,0:T(8,128)(2,1)} custom-call(s32[8]{0:T(128)S(1)} %copy-done.6, s32[8,512]{1,0:T(8,128)S(1)} %copy-done.4, bf16[8,10,80,384]{3,2,1,0:T(8,128)(2,1)} %get-tuple-element.93.refs_2_, bf16[3456,128]{1,0:T(8,128)(2,1)S(1)} %bitcast.28), custom_call_target="tpu_custom_call" | custom-call | flops 905969664 | bytes 1048576 | tf_op jit(solution)/shard_map/convolve/pallas_call | solution.py:335
  35.8 6.7 %collective-permute-start.7 = (f32[4,112,128]{2,1,0:T(8,128)S(1)}, f32[4,112,128]{2,1,0:T(8,128)S(1)}, u32[]{:S(2)}, u32[]{:S(2)}) collective-permute-start(f32[4,112,128]{2,1,0:T(8,128)S(1)} %get-tuple-element.137), channel_id=1, source_target_pairs={{0,130},{1,13},{2,128},{3,15},{4,134},{5,9},{6,132},{7,11},{8,138}... | collective-permute-start | bytes 688136 | tf_op jit(solution)/shard_map/ppermute | solution.py:409
  42.6 1.2 %collective-permute-start.5 = (f32[4,112,128]{2,1,0:T(8,128)S(1)}, f32[4,112,128]{2,1,0:T(8,128)S(1)}, u32[]{:S(2)}, u32[]{:S(2)}) collective-permute-start(f32[4,112,128]{2,1,0:T(8,128)S(1)} %get-tuple-element.139), channel_id=1, source_target_pairs={{0,128},{1,9},{2,130},{3,11},{4,132},{5,13},{6,134},{7,15},{8,136}... | collective-permute-start | bytes 688136 | tf_op jit(solution)/shard_map/ppermute | solution.py:409
  43.8 5.1 %convolve.9.refs_4_ = bf16[8,512,128]{2,1,0:T(8,128)(2,1)} custom-call(s32[8]{0:T(128)S(1)} %copy-done.6, s32[8,512]{1,0:T(8,128)S(1)} %copy-done.4, bf16[8,10,80,384]{3,2,1,0:T(8,128)(2,1)} %get-tuple-element.93.refs_2_, bf16[3456,128]{1,0:T(8,128)(2,1)S(1)} %bitcast.29, bf16[8,512,128]{2,1,0:T(8,128)(2,1)} %convolve.8.refs_4_), custom_call_target="tpu_custom_call", output_to_operand_aliasing={{}: (4, {})} | custom-call | flops 3623878656 | bytes 4194304 | tf_op jit(solution)/shard_map/convolve/pallas_call | solution.py:335
  49.8 10.1 %collective-permute-start.10 = (f32[1,112,128]{2,1,0:T(8,128)S(1)}, f32[1,112,128]{2,1,0:T(8,128)S(1)}, u32[]{:S(2)}, u32[]{:S(2)}) collective-permute-start(f32[1,112,128]{2,1,0:T(8,128)S(1)} %get-tuple-element.150), channel_id=1, source_target_pairs={{0,12},{1,131},{2,14},{3,129},{4,8},{5,135},{6,10},{7,133},{8,4},{... | collective-permute-start | bytes 172040 | tf_op jit(solution)/shard_map/ppermute | solution.py:409
  59.9 1.3 %collective-permute-start.8 = (f32[1,112,128]{2,1,0:T(8,128)S(1)}, f32[1,112,128]{2,1,0:T(8,128)S(1)}, u32[]{:S(2)}, u32[]{:S(2)}) collective-permute-start(f32[1,112,128]{2,1,0:T(8,128)S(1)} %get-tuple-element.152), channel_id=1, source_target_pairs={{0,8},{1,129},{2,10},{3,131},{4,12},{5,133},{6,14},{7,135},{8,0},{... | collective-permute-start | bytes 172040 | tf_op jit(solution)/shard_map/ppermute | solution.py:409
  61.2 2.0 %convolve.10.refs_4_ = bf16[8,512,128]{2,1,0:T(8,128)(2,1)} custom-call(s32[8]{0:T(128)S(1)} %copy-done.6, s32[8,512]{1,0:T(8,128)S(1)} %copy-done.4, bf16[8,10,80,384]{3,2,1,0:T(8,128)(2,1)} %get-tuple-element.93.refs_2_, bf16[3456,128]{1,0:T(8,128)(2,1)S(1)} %bitcast.30, bf16[8,512,128]{2,1,0:T(8,128)(2,1)} %convolve.9.refs_4_), custom_call_target="tpu_custom_call", output_to_operand_aliasing={{}: (4, {})} | custom-call | flops 1811939328 | bytes 2097152 | tf_op jit(solution)/shard_map/convolve/pallas_call | solution.py:335
  63.1 1.6 %collective-permute-done.8 = f32[1,112,128]{2,1,0:T(8,128)S(1)} collective-permute-done((f32[1,112,128]{2,1,0:T(8,128)S(1)}, f32[1,112,128]{2,1,0:T(8,128)S(1)}, u32[]{:S(2)}, u32[]{:S(2)}) %collective-permute-start.8) | collective-permute-done | bytes 57376 | tf_op jit(solution)/shard_map/ppermute | solution.py:409
  65.0 3.4 %collective-permute-start.11 = (f32[1,112,128]{2,1,0:T(8,128)S(1)}, f32[1,112,128]{2,1,0:T(8,128)S(1)}, u32[]{:S(2)}, u32[]{:S(2)}) collective-permute-start(f32[1,112,128]{2,1,0:T(8,128)S(1)} %add_add_fusion.2), channel_id=1, source_target_pairs={{0,32},{1,33},{2,34},{3,35},{4,36},{5,37},{6,38},{7,39},{8,40},{9,... | collective-permute-start | bytes 172040 | tf_op jit(solution)/shard_map/ppermute | solution.py:409
  68.4 6.1 %patches.1.refs_2_ = bf16[8,10,80,384]{3,2,1,0:T(8,128)(2,1)} custom-call(s32[8]{0:T(128)S(1)} %copy-done.6, s32[4]{0:T(128)S(1)} %pad_add_fusion.meta_ref, bf16[32,16,16,128]{3,2,1,0:T(8,128)(2,1)S(1)} %copy-done.1, bf16[32,16,128]{2,1,0:T(8,128)(2,1)S(1)} %get-tuple-element.160.side_even_ref, bf16[32,16,128]{2,1,0:T(8,128)(2,1)S(1)} %get-tuple-element.142.side_odd_ref, ...), custom_call_target="tpu_custom_call" | custom-call | bytes 20971520 | tf_op jit(solution)/shard_map/patches/pallas_call | solution.py:265
  74.5 1.1 collective-permute-start.14
  75.6 1.8 %convolve.11 = bf16[8,512,128]{2,1,0:T(8,128)(2,1)} custom-call(s32[8]{0:T(128)S(1)} %copy-done.6, s32[8,512]{1,0:T(8,128)S(1)} %copy-done.4, bf16[8,10,80,384]{3,2,1,0:T(8,128)(2,1)} %get-tuple-element.93.refs_2_, bf16[3456,128]{1,0:T(8,128)(2,1)S(1)} %bitcast.31, bf16[8,512,128]{2,1,0:T(8,128)(2,1)} %convolve.10.refs_4_), custom_call_target="tpu_custom_call", output_to_operand_aliasing={{}: (4, {})} | custom-call | flops 905969664 | bytes 1048576 | tf_op jit(solution)/shard_map/convolve/pallas_call | solution.py:335
  77.4 2.8 %convolve.12.refs_4_ = bf16[8,512,128]{2,1,0:T(8,128)(2,1)} custom-call(s32[8]{0:T(128)S(1)} %copy-done.6, s32[8,512]{1,0:T(8,128)S(1)} %copy-done.4, bf16[8,10,80,384]{3,2,1,0:T(8,128)(2,1)} %patches.1.refs_2_, bf16[3456,128]{1,0:T(8,128)(2,1)S(1)} %bitcast.24), custom_call_target="tpu_custom_call" | custom-call | flops 905969664 | bytes 1048576 | tf_op jit(solution)/shard_map/convolve/pallas_call | solution.py:335
  80.2 2.0 %collective-permute-done.14 = f32[1,112,128]{2,1,0:T(8,128)S(1)} collective-permute-done((f32[1,112,128]{2,1,0:T(8,128)S(1)}, f32[1,112,128]{2,1,0:T(8,128)S(1)}, u32[]{:S(2)}, u32[]{:S(2)}) %collective-permute-start.14) | collective-permute-done | bytes 57376 | tf_op jit(solution)/shard_map/ppermute | solution.py:409
  82.2 1.7 %collective-permute-start.17 = (f32[1,112,128]{2,1,0:T(8,128)S(1)}, f32[1,112,128]{2,1,0:T(8,128)S(1)}, u32[]{:S(2)}, u32[]{:S(2)}) collective-permute-start(f32[1,112,128]{2,1,0:T(8,128)S(1)} %add.55), channel_id=1, source_target_pairs={{0,12},{1,131},{2,14},{3,129},{4,8},{5,135},{6,10},{7,133},{8,4},{... | collective-permute-start | bytes 172040 | tf_op jit(solution)/shard_map/ppermute | solution.py:409
  83.9 2.3 %collective-permute-start.15 = (f32[1,112,128]{2,1,0:T(8,128)S(1)}, f32[1,112,128]{2,1,0:T(8,128)S(1)}, u32[]{:S(2)}, u32[]{:S(2)}) collective-permute-start(f32[1,112,128]{2,1,0:T(8,128)S(1)} %add.55), channel_id=1, source_target_pairs={{0,8},{1,129},{2,10},{3,131},{4,12},{5,133},{6,14},{7,135},{8,0},{... | collective-permute-start | bytes 172040 | tf_op jit(solution)/shard_map/ppermute | solution.py:409
  86.2 3.9 %convolve.13.refs_4_ = bf16[8,512,128]{2,1,0:T(8,128)(2,1)} custom-call(s32[8]{0:T(128)S(1)} %copy-done.6, s32[8,512]{1,0:T(8,128)S(1)} %copy-done.4, bf16[8,10,80,384]{3,2,1,0:T(8,128)(2,1)} %patches.1.refs_2_, bf16[3456,128]{1,0:T(8,128)(2,1)S(1)} %bitcast.25, bf16[8,512,128]{2,1,0:T(8,128)(2,1)} %convolve.12.refs_4_), custom_call_target="tpu_custom_call", output_to_operand_aliasing={{}: (4, {})} | custom-call | flops 1811939328 | bytes 2097152 | tf_op jit(solution)/shard_map/convolve/pallas_call | solution.py:335
  90.6 3.5 %collective-permute-start.18 = (f32[4,112,128]{2,1,0:T(8,128)S(1)}, f32[4,112,128]{2,1,0:T(8,128)S(1)}, u32[]{:S(2)}, u32[]{:S(2)}) collective-permute-start(f32[4,112,128]{2,1,0:T(8,128)S(1)} %pad_maximum_fusion.1), channel_id=1, source_target_pairs={{0,128},{1,9},{2,130},{3,11},{4,132},{5,13},{6,134},{7,15},{8,136}... | collective-permute-start | bytes 688136 | tf_op jit(solution)/shard_map/ppermute | solution.py:409
  94.1 4.6 %convolve.14.refs_4_ = bf16[8,512,128]{2,1,0:T(8,128)(2,1)} custom-call(s32[8]{0:T(128)S(1)} %copy-done.6, s32[8,512]{1,0:T(8,128)S(1)} %copy-done.4, bf16[8,10,80,384]{3,2,1,0:T(8,128)(2,1)} %patches.1.refs_2_, bf16[3456,128]{1,0:T(8,128)(2,1)S(1)} %bitcast.26, bf16[8,512,128]{2,1,0:T(8,128)(2,1)} %convolve.13.refs_4_), custom_call_target="tpu_custom_call", output_to_operand_aliasing={{}: (4, {})} | custom-call | flops 3623878656 | bytes 4194304 | tf_op jit(solution)/shard_map/convolve/pallas_call | solution.py:335
  98.7 1.2 %collective-permute-done.18 = f32[4,112,128]{2,1,0:T(8,128)S(1)} collective-permute-done((f32[4,112,128]{2,1,0:T(8,128)S(1)}, f32[4,112,128]{2,1,0:T(8,128)S(1)}, u32[]{:S(2)}, u32[]{:S(2)}) %collective-permute-start.18) | collective-permute-done | bytes 229408 | tf_op jit(solution)/shard_map/ppermute | solution.py:409
  100.0 6.1 %collective-permute-start.21 = (f32[16,112,128]{2,1,0:T(8,128)S(1)}, f32[16,112,128]{2,1,0:T(8,128)S(1)}, u32[]{:S(2)}, u32[]{:S(2)}) collective-permute-start(f32[16,112,128]{2,1,0:T(8,128)S(1)} %pad_maximum_fusion.own_ref), channel_id=1, source_target_pairs={{0,1},{1,0},{2,3},{3,2},{4,5},{5,4},{6,7},{7,6},{8,9},{9,8},{10,11... | collective-permute-start | bytes 2752520 | tf_op jit(solution)/shard_map/ppermute | solution.py:409
  106.2 1.8 %convolve.15 = bf16[8,512,128]{2,1,0:T(8,128)(2,1)} custom-call(s32[8]{0:T(128)S(1)} %copy-done.6, s32[8,512]{1,0:T(8,128)S(1)} %copy-done.4, bf16[8,10,80,384]{3,2,1,0:T(8,128)(2,1)} %patches.1.refs_2_, bf16[3456,128]{1,0:T(8,128)(2,1)S(1)} %bitcast.27, bf16[8,512,128]{2,1,0:T(8,128)(2,1)} %convolve.14.refs_4_), custom_call_target="tpu_custom_call", output_to_operand_aliasing={{}: (4, {})} | custom-call | flops 905969664 | bytes 1048576 | tf_op jit(solution)/shard_map/convolve/pallas_call | solution.py:335
  108.3 2.2 %finish.1 = f32[27,128,128]{2,1,0:T(8,128)} custom-call(s32[4]{0:T(128)S(1)} %pad_add_fusion.meta_ref, f32[16,112,128]{2,1,0:T(8,128)S(1)} %pad_maximum_fusion.own_ref, f32[16,112,128]{2,1,0:T(8,128)S(1)} %collective-permute-done.21.other_ref), custom_call_target="tpu_custom_call" | custom-call | tf_op jit(solution)/shard_map/finish/pallas_call | solution.py:370
  (60 shorter events, 5.5 us)
Async XLA Ops:
  0.6 13.7 %copy-start = (bf16[27,128,128]{2,1,0:T(8,128)(2,1)S(1)}, bf16[27,128,128]{2,1,0:T(8,128)(2,1)}, u32[]{:S(2)}) copy-start(bf16[27,128,128]{2,1,0:T(8,128)(2,1)} %param.6) | copy-start | bytes 2654212
  0.7 0.8 copy-start.3
  1.5 0.7 copy-start.5
  8.4 8.9 %collective-permute-start = (bf16[2,32,16,128]{3,2,1,0:T(8,128)(2,1)}, bf16[2,32,16,128]{3,2,1,0:T(8,128)(2,1)}, u32[]{:S(2)}, u32[]{:S(2)}) collective-permute-start(bf16[2,32,16,128]{3,2,1,0:T(8,128)(2,1)} %get-tuple-element.72), channel_id=1, source_target_pairs={{0,1},{1,0},{2,3},{3,2},{4,5},{5,4},{6,7},{7,6},{8,9},{9,8},{10,11... | collective-permute-start | bytes 786440 | tf_op jit(solution)/shard_map/ppermute | solution.py:417
  12.4 7.8 %collective-permute-start.1 = (bf16[2,32,16,128]{3,2,1,0:T(8,128)(2,1)S(1)}, bf16[2,32,16,128]{3,2,1,0:T(8,128)(2,1)}, u32[]{:S(2)}, u32[]{:S(2)}) collective-permute-start(bf16[2,32,16,128]{3,2,1,0:T(8,128)(2,1)S(1)} %get-tuple-element.73), channel_id=1, source_target_pairs={{1,2},{2,1},{5,6},{6,5},{9,10},{10,9},{13,14},{14,13},{17,18},{18,... | collective-permute-start | bytes 786440 | tf_op jit(solution)/shard_map/ppermute | solution.py:417
  15.3 7.9 %copy-start.2 = (bf16[8,128,512]{2,1,0:T(8,128)(2,1)S(1)}, bf16[8,128,512]{2,1,0:T(8,128)(2,1)}, u32[]{:S(2)}) copy-start(bf16[8,128,512]{2,1,0:T(8,128)(2,1)} %get-tuple-element.83.xt_ref) | copy-start | bytes 3145732
  15.3 8.0 %copy-start.6 = (s32[8]{0:T(128)S(1)}, s32[8]{0:T(128)}, u32[]{:S(2)}) copy-start(s32[8]{0:T(128)} %refs_0_.7) | copy-start | bytes 100
  17.3 6.0 %copy-start.7 = (bf16[32,16,16,128]{3,2,1,0:T(8,128)(2,1)S(1)}, bf16[32,16,16,128]{3,2,1,0:T(8,128)(2,1)}, u32[]{:S(2)}) copy-start(bf16[32,16,16,128]{3,2,1,0:T(8,128)(2,1)} %get-tuple-element.82.grid_ref) | copy-start | bytes 6291460
  22.5 8.9 %collective-permute-start.2 = (bf16[2,18,16,128]{3,2,1,0:T(8,128)(2,1)S(1)}, bf16[2,18,16,128]{3,2,1,0:T(8,128)(2,1)S(1)}, u32[]{:S(2)}, u32[]{:S(2)}) collective-permute-start(bf16[2,18,16,128]{3,2,1,0:T(8,128)(2,1)S(1)} %pad_maximum_fusion.2), channel_id=1, source_target_pairs={{0,4},{1,5},{2,6},{3,7},{4,0},{5,1},{6,2},{7,3},{8,12},{9,13},{10,... | collective-permute-start | bytes 442376 | tf_op jit(solution)/shard_map/ppermute | solution.py:413
  22.6 8.8 %collective-permute-start.3 = (bf16[2,18,16,128]{3,2,1,0:T(8,128)(2,1)S(1)}, bf16[2,18,16,128]{3,2,1,0:T(8,128)(2,1)S(1)}, u32[]{:S(2)}, u32[]{:S(2)}) collective-permute-start(bf16[2,18,16,128]{3,2,1,0:T(8,128)(2,1)S(1)} %pad_maximum_fusion.3), channel_id=1, source_target_pairs={{4,8},{5,9},{6,10},{7,11},{8,4},{9,5},{10,6},{11,7},{12,16},{13,17... | collective-permute-start | bytes 442376 | tf_op jit(solution)/shard_map/ppermute | solution.py:413
  31.4 1.4 %copy-start.4 = (s32[8,512]{1,0:T(8,128)S(1)}, s32[8,512]{1,0:T(8,128)}, u32[]{:S(2)}) copy-start(s32[8,512]{1,0:T(8,128)} %refs_1_.15) | copy-start | bytes 49156
  32.7 3.0 %collective-permute-start.4 = (f32[16,112,128]{2,1,0:T(8,128)S(1)}, f32[16,112,128]{2,1,0:T(8,128)S(1)}, u32[]{:S(2)}, u32[]{:S(2)}) collective-permute-start(f32[16,112,128]{2,1,0:T(8,128)S(1)} %get-tuple-element.91), channel_id=1, source_target_pairs={{0,1},{1,0},{2,3},{3,2},{4,5},{5,4},{6,7},{7,6},{8,9},{9,8},{10,11... | collective-permute-start | bytes 2752520 | tf_op jit(solution)/shard_map/ppermute | solution.py:409
  35.8 13.1 %collective-permute-start.7 = (f32[4,112,128]{2,1,0:T(8,128)S(1)}, f32[4,112,128]{2,1,0:T(8,128)S(1)}, u32[]{:S(2)}, u32[]{:S(2)}) collective-permute-start(f32[4,112,128]{2,1,0:T(8,128)S(1)} %get-tuple-element.137), channel_id=1, source_target_pairs={{0,130},{1,13},{2,128},{3,15},{4,134},{5,9},{6,132},{7,11},{8,138}... | collective-permute-start | bytes 688136 | tf_op jit(solution)/shard_map/ppermute | solution.py:409
  42.5 6.4 %collective-permute-start.6 = (f32[4,112,128]{2,1,0:T(8,128)S(1)}, f32[4,112,128]{2,1,0:T(8,128)S(1)}, u32[]{:S(2)}, u32[]{:S(2)}) collective-permute-start(f32[4,112,128]{2,1,0:T(8,128)S(1)} %get-tuple-element.138), channel_id=1, source_target_pairs={{0,2},{1,5},{2,0},{3,7},{4,6},{5,1},{6,4},{7,3},{8,10},{9,13},{10,... | collective-permute-start | bytes 688136 | tf_op jit(solution)/shard_map/ppermute | solution.py:409
  42.6 7.1 %collective-permute-start.5 = (f32[4,112,128]{2,1,0:T(8,128)S(1)}, f32[4,112,128]{2,1,0:T(8,128)S(1)}, u32[]{:S(2)}, u32[]{:S(2)}) collective-permute-start(f32[4,112,128]{2,1,0:T(8,128)S(1)} %get-tuple-element.139), channel_id=1, source_target_pairs={{0,128},{1,9},{2,130},{3,11},{4,132},{5,13},{6,134},{7,15},{8,136}... | collective-permute-start | bytes 688136 | tf_op jit(solution)/shard_map/ppermute | solution.py:409
  49.8 13.4 %collective-permute-start.10 = (f32[1,112,128]{2,1,0:T(8,128)S(1)}, f32[1,112,128]{2,1,0:T(8,128)S(1)}, u32[]{:S(2)}, u32[]{:S(2)}) collective-permute-start(f32[1,112,128]{2,1,0:T(8,128)S(1)} %get-tuple-element.150), channel_id=1, source_target_pairs={{0,12},{1,131},{2,14},{3,129},{4,8},{5,135},{6,10},{7,133},{8,4},{... | collective-permute-start | bytes 172040 | tf_op jit(solution)/shard_map/ppermute | solution.py:409
  59.9 3.2 %collective-permute-start.9 = (f32[1,112,128]{2,1,0:T(8,128)S(1)}, f32[1,112,128]{2,1,0:T(8,128)S(1)}, u32[]{:S(2)}, u32[]{:S(2)}) collective-permute-start(f32[1,112,128]{2,1,0:T(8,128)S(1)} %get-tuple-element.151), channel_id=1, source_target_pairs={{0,4},{1,3},{2,6},{3,1},{4,0},{5,7},{6,2},{7,5},{8,12},{9,11},{10,... | collective-permute-start | bytes 172040 | tf_op jit(solution)/shard_map/ppermute | solution.py:409
  59.9 8.5 %copy-start.1 = (bf16[32,16,16,128]{3,2,1,0:T(8,128)(2,1)S(1)}, bf16[32,16,16,128]{3,2,1,0:T(8,128)(2,1)}, u32[]{:S(2)}) copy-start(bf16[32,16,16,128]{3,2,1,0:T(8,128)(2,1)} %get-tuple-element.110.grid_ref) | copy-start | bytes 6291460
  59.9 4.8 %collective-permute-start.8 = (f32[1,112,128]{2,1,0:T(8,128)S(1)}, f32[1,112,128]{2,1,0:T(8,128)S(1)}, u32[]{:S(2)}, u32[]{:S(2)}) collective-permute-start(f32[1,112,128]{2,1,0:T(8,128)S(1)} %get-tuple-element.152), channel_id=1, source_target_pairs={{0,8},{1,129},{2,10},{3,131},{4,12},{5,133},{6,14},{7,135},{8,0},{... | collective-permute-start | bytes 172040 | tf_op jit(solution)/shard_map/ppermute | solution.py:409
  64.8 9.7 %collective-permute-start.13 = (f32[1,112,128]{2,1,0:T(8,128)S(1)}, f32[1,112,128]{2,1,0:T(8,128)S(1)}, u32[]{:S(2)}, u32[]{:S(2)}) collective-permute-start(f32[1,112,128]{2,1,0:T(8,128)S(1)} %add_add_fusion.2), channel_id=1, source_target_pairs={{0,48},{1,49},{2,50},{3,51},{4,52},{5,53},{6,54},{7,55},{8,56},{9,... | collective-permute-start | bytes 172040 | tf_op jit(solution)/shard_map/ppermute | solution.py:409
  64.9 9.6 %collective-permute-start.12 = (f32[1,112,128]{2,1,0:T(8,128)S(1)}, f32[1,112,128]{2,1,0:T(8,128)S(1)}, u32[]{:S(2)}, u32[]{:S(2)}) collective-permute-start(f32[1,112,128]{2,1,0:T(8,128)S(1)} %add_add_fusion.2), channel_id=1, source_target_pairs={{0,16},{1,17},{2,18},{3,19},{4,20},{5,21},{6,22},{7,23},{8,24},{9,... | collective-permute-start | bytes 172040 | tf_op jit(solution)/shard_map/ppermute | solution.py:409
  65.0 9.5 %collective-permute-start.11 = (f32[1,112,128]{2,1,0:T(8,128)S(1)}, f32[1,112,128]{2,1,0:T(8,128)S(1)}, u32[]{:S(2)}, u32[]{:S(2)}) collective-permute-start(f32[1,112,128]{2,1,0:T(8,128)S(1)} %add_add_fusion.2), channel_id=1, source_target_pairs={{0,32},{1,33},{2,34},{3,35},{4,36},{5,37},{6,38},{7,39},{8,40},{9,... | collective-permute-start | bytes 172040 | tf_op jit(solution)/shard_map/ppermute | solution.py:409
  74.5 7.7 %collective-permute-start.14 = (f32[1,112,128]{2,1,0:T(8,128)S(1)}, f32[1,112,128]{2,1,0:T(8,128)S(1)}, u32[]{:S(2)}, u32[]{:S(2)}) collective-permute-start(f32[1,112,128]{2,1,0:T(8,128)S(1)} %add_add_fusion.1), channel_id=1, source_target_pairs={{0,64},{1,65},{2,66},{3,67},{4,68},{5,69},{6,70},{7,71},{8,72},{9,... | collective-permute-start | bytes 172040 | tf_op jit(solution)/shard_map/ppermute | solution.py:409
  82.2 7.9 %collective-permute-start.17 = (f32[1,112,128]{2,1,0:T(8,128)S(1)}, f32[1,112,128]{2,1,0:T(8,128)S(1)}, u32[]{:S(2)}, u32[]{:S(2)}) collective-permute-start(f32[1,112,128]{2,1,0:T(8,128)S(1)} %add.55), channel_id=1, source_target_pairs={{0,12},{1,131},{2,14},{3,129},{4,8},{5,135},{6,10},{7,133},{8,4},{... | collective-permute-start | bytes 172040 | tf_op jit(solution)/shard_map/ppermute | solution.py:409
  83.9 6.2 %collective-permute-start.16 = (f32[1,112,128]{2,1,0:T(8,128)S(1)}, f32[1,112,128]{2,1,0:T(8,128)S(1)}, u32[]{:S(2)}, u32[]{:S(2)}) collective-permute-start(f32[1,112,128]{2,1,0:T(8,128)S(1)} %add.55), channel_id=1, source_target_pairs={{0,4},{1,3},{2,6},{3,1},{4,0},{5,7},{6,2},{7,5},{8,12},{9,11},{10,... | collective-permute-start | bytes 172040 | tf_op jit(solution)/shard_map/ppermute | solution.py:409
  83.9 6.2 %collective-permute-start.15 = (f32[1,112,128]{2,1,0:T(8,128)S(1)}, f32[1,112,128]{2,1,0:T(8,128)S(1)}, u32[]{:S(2)}, u32[]{:S(2)}) collective-permute-start(f32[1,112,128]{2,1,0:T(8,128)S(1)} %add.55), channel_id=1, source_target_pairs={{0,8},{1,129},{2,10},{3,131},{4,12},{5,133},{6,14},{7,135},{8,0},{... | collective-permute-start | bytes 172040 | tf_op jit(solution)/shard_map/ppermute | solution.py:409
  90.2 8.6 %collective-permute-start.20 = (f32[4,112,128]{2,1,0:T(8,128)S(1)}, f32[4,112,128]{2,1,0:T(8,128)S(1)}, u32[]{:S(2)}, u32[]{:S(2)}) collective-permute-start(f32[4,112,128]{2,1,0:T(8,128)S(1)} %pad_maximum_fusion.1), channel_id=1, source_target_pairs={{0,130},{1,13},{2,128},{3,15},{4,134},{5,9},{6,132},{7,11},{8,138}... | collective-permute-start | bytes 688136 | tf_op jit(solution)/shard_map/ppermute | solution.py:409
  90.3 8.5 %collective-permute-start.19 = (f32[4,112,128]{2,1,0:T(8,128)S(1)}, f32[4,112,128]{2,1,0:T(8,128)S(1)}, u32[]{:S(2)}, u32[]{:S(2)}) collective-permute-start(f32[4,112,128]{2,1,0:T(8,128)S(1)} %pad_maximum_fusion.1), channel_id=1, source_target_pairs={{0,2},{1,5},{2,0},{3,7},{4,6},{5,1},{6,4},{7,3},{8,10},{9,13},{10,... | collective-permute-start | bytes 688136 | tf_op jit(solution)/shard_map/ppermute | solution.py:409
  90.6 9.4 %collective-permute-start.18 = (f32[4,112,128]{2,1,0:T(8,128)S(1)}, f32[4,112,128]{2,1,0:T(8,128)S(1)}, u32[]{:S(2)}, u32[]{:S(2)}) collective-permute-start(f32[4,112,128]{2,1,0:T(8,128)S(1)} %pad_maximum_fusion.1), channel_id=1, source_target_pairs={{0,128},{1,9},{2,130},{3,11},{4,132},{5,13},{6,134},{7,15},{8,136}... | collective-permute-start | bytes 688136 | tf_op jit(solution)/shard_map/ppermute | solution.py:409
  100.0 8.2 %collective-permute-start.21 = (f32[16,112,128]{2,1,0:T(8,128)S(1)}, f32[16,112,128]{2,1,0:T(8,128)S(1)}, u32[]{:S(2)}, u32[]{:S(2)}) collective-permute-start(f32[16,112,128]{2,1,0:T(8,128)S(1)} %pad_maximum_fusion.own_ref), channel_id=1, source_target_pairs={{0,1},{1,0},{2,3},{3,2},{4,5},{5,4},{6,7},{7,6},{8,9},{9,8},{10,11... | collective-permute-start | bytes 2752520 | tf_op jit(solution)/shard_map/ppermute | solution.py:409

commit v4 on v3

--- a/solution.py
+++ b/solution.py
@@ -22,6 +22,7 @@
 BF16 = jnp.bfloat16
 VMEM = pl.BlockSpec(memory_space=pltpu.VMEM)
 SMEM = pl.BlockSpec(memory_space=pltpu.SMEM)
+HBM = pl.BlockSpec(memory_space=pltpu.HBM)
 
 
 def pin(value, space):
@@ -36,7 +37,7 @@
     return jnp.where(occ_ref[...] == 1, 1.0, 0.0).astype(F32).T
 
 
-def place_kernel(pos_ref, meta_ref, occ_ref, feat_hbm, cot_hbm, xg_hbm, cg_hbm, xt_hbm, even_ref, odd_ref, side_even_ref, side_odd_ref, cells, slots, grids, xt, load_sems, grid_sems, xt_sem):
+def place_kernel(pos_ref, meta_ref, occ_hbm, feat_hbm, cot_hbm, xg_hbm, cg_hbm, xt_hbm, even_ref, odd_ref, side_even_ref, side_odd_ref, occ, cells, slots, grids, xt, load_sems, grid_sems, xt_sem, occ_sem):
     def load(t, s):
         return pltpu.make_async_copy((cot_hbm, feat_hbm)[t].at[s], slots.at[t, s], load_sems.at[t, s])
 
@@ -44,10 +45,11 @@
         part = pl.ds(n * 8, 8)
         return pltpu.make_async_copy(grids.at[t, part], (cg_hbm, xg_hbm)[t].at[part], grid_sems.at[t, n])
 
+    load_occ = pltpu.make_async_copy(occ_hbm, occ, occ_sem)
+    load_occ.start()
     for t in range(2):
         for s in range(SLOTS):
             load(t, s).start()
-    columns = mask_columns(occ_ref)
     core, odd_x = meta_ref[0], meta_ref[3]
     for t in range(2):
 
@@ -56,6 +58,9 @@
             return carry
 
         lax.fori_loop(0, NX, clear, 0)
+        if t == 0:
+            load_occ.wait()
+            columns = mask_columns(occ)
         for s in range(SLOTS):
             load(t, s).wait()
             pos = pos_ref[s]
@@ -98,9 +103,10 @@
     return pl.pallas_call(
         place_kernel,
         out_shape=(grid, grid, pltpu.HBM((SLOTS, CH, VOX), BF16), plane, plane, side, side),
-        in_specs=[SMEM, SMEM, VMEM, hbm, hbm],
+        in_specs=[SMEM, SMEM, hbm, hbm, hbm],
         out_specs=(hbm,) * 3 + (VMEM,) * 4,
         scratch_shapes=[
+            pltpu.VMEM((SLOTS, VOX), jnp.int32),
             pltpu.VMEM((NX, NY, 2, 8, CH), F32),
             pltpu.VMEM((2, SLOTS, VOX, CH), BF16),
             pltpu.VMEM((2, NX, NY, NZ, CH), BF16),
@@ -108,10 +114,11 @@
             pltpu.SemaphoreType.DMA((2, SLOTS)),
             pltpu.SemaphoreType.DMA((2, 4)),
             pltpu.SemaphoreType.DMA,
+            pltpu.SemaphoreType.DMA,
         ],
         compiler_params=pltpu.CompilerParams(vmem_limit_bytes=24 << 20),
         name="place",
-    )(slot_pos, meta, occupancy, pin(features, pltpu.HBM), pin(cotangent, pltpu.HBM))
+    )(slot_pos, meta, *[pin(a, pltpu.HBM) for a in (occupancy, features, cotangent)])
 
 
 def shifted(v):
@@ -123,27 +130,36 @@
     return [a.reshape(n, 2, 8, CH) for a in (back, flat, ahead)]
 
 
-def assemble(meta_ref, grid_ref, side_even_ref, side_odd_ref, halo, planes=None):
+def assemble(meta_ref, t, grid_hbm, side_even_ref, side_odd_ref, halo, cells, sems, planes=None):
     core, odd_x = meta_ref[0], meta_ref[3]
 
+    def load(n):
+        part = pl.ds(n * 8, 8)
+        return pltpu.make_async_copy(grid_hbm.at[part], cells.at[part], sems.at[n])
+
+    for n in range(4):
+        load(n).start()
+
     def body(x, carry):
-        for r, a in enumerate(shifted(grid_ref[x])):
+        for r, a in enumerate(shifted(cells[x])):
             for bz in range(2):
                 halo[r, bz, x + 1, pl.ds(1, NY)] = a[:, bz]
         return carry
 
-    lax.fori_loop(0, NX, body, 0)
     for y, ref in (((NY + 1) * (1 - core), side_even_ref), ((NY + 1) * core, side_odd_ref)):
-        for r, a in enumerate(shifted(ref[...])):
+        for r, a in enumerate(shifted(ref[t])):
             for bz in range(2):
                 halo[r, bz, pl.ds(1, NX), y] = a[:, bz]
     for i, x in enumerate(((NX + 1) * (1 - odd_x), (NX + 1) * odd_x)):
         if planes is None:
             halo[:, :, x] = jnp.zeros((3, 2, NY + 2, 8, CH), F32)
         else:
-            for r, a in enumerate(shifted(planes[i][...])):
+            for r, a in enumerate(shifted(planes[i][t])):
                 for bz in range(2):
                     halo[r, bz, x] = a[:, bz]
+    for n in range(4):
+        load(n).wait()
+        lax.fori_loop(n * 8, n * 8 + 8, body, 0)
 
 
 def build_patches(pos, halo, patch_ref):
@@ -159,12 +175,12 @@
     return jnp.concatenate(parts, axis=1)
 
 
-def patches_kernel(pos_ref, meta_ref, grid_ref, side_even_ref, side_odd_ref, even_ref, odd_ref, patch_ref, halo):
+def patches_kernel(pos_ref, meta_ref, grid_hbm, side_even_ref, side_odd_ref, even_ref, odd_ref, patch_ref, halo, cells, sems):
     s = pl.program_id(0)
 
     @pl.when(s == 0)
     def _():
-        assemble(meta_ref, grid_ref, side_even_ref, side_odd_ref, halo, (even_ref, odd_ref))
+        assemble(meta_ref, 1, grid_hbm, side_even_ref, side_odd_ref, halo, cells, sems, (even_ref, odd_ref))
 
     pos = pos_ref[s]
 
@@ -173,12 +189,12 @@
         build_patches(pos, halo, patch_ref)
 
 
-def weight_kernel(pos_ref, meta_ref, grid_ref, side_even_ref, side_odd_ref, xt_ref, patch_ref, total, halo):
+def weight_kernel(pos_ref, meta_ref, grid_hbm, side_even_ref, side_odd_ref, xt_ref, patch_ref, total, halo, cells, sems):
     s = pl.program_id(0)
 
     @pl.when(s == 0)
     def _():
-        assemble(meta_ref, grid_ref, side_even_ref, side_odd_ref, halo)
+        assemble(meta_ref, 0, grid_hbm, side_even_ref, side_odd_ref, halo, cells, sems)
 
         def clear(o, carry):
             total[pl.ds(pl.multiple_of(o * CH, CH), CH)] = jnp.zeros((CH, CH), F32)
@@ -202,7 +218,7 @@
     core, own, other, odd_x = meta_ref[0], meta_ref[1], meta_ref[2], meta_ref[3]
     for i, ref in enumerate((even_ref, odd_ref)):
         at = 1 - odd_x if i == 0 else odd_x
-        for r, a in enumerate(shifted(ref[...])):
+        for r, a in enumerate(shifted(ref[0])):
             for bz in range(2):
                 rims[at, r, bz] = a[:, bz]
 
@@ -266,13 +282,13 @@
         patches_kernel,
         out_shape=PATCH_SHAPE,
         grid=(SLOTS,),
-        in_specs=[SMEM, SMEM] + [VMEM] * 5,
+        in_specs=[SMEM, SMEM, HBM] + [VMEM] * 4,
         out_specs=PATCH_SPEC,
-        scratch_shapes=[HALO],
+        scratch_shapes=[HALO, pltpu.VMEM((NX, NY, NZ, CH), BF16), pltpu.SemaphoreType.DMA((4,))],
         compiler_params=pltpu.CompilerParams(vmem_limit_bytes=28 << 20),
         cost_estimate=pl.CostEstimate(flops=0, bytes_accessed=20 << 20, transcendentals=0),
         name="patches",
-    )(slot_pos, meta, grid, *sides, *planes)
+    )(slot_pos, meta, pin(grid, pltpu.HBM), *sides, *planes)
 
 
 def weight_gradient(slot_pos, meta, grid, sides, xt):
@@ -280,13 +296,13 @@
         weight_kernel,
         out_shape=(PATCH_SHAPE, TOTAL),
         grid=(SLOTS,),
-        in_specs=[SMEM, SMEM] + [VMEM] * 3 + [pl.BlockSpec((1, CH, VOX), lambda s: (s, 0, 0))],
+        in_specs=[SMEM, SMEM, HBM] + [VMEM] * 2 + [pl.BlockSpec((1, CH, VOX), lambda s: (s, 0, 0))],
         out_specs=(PATCH_SPEC, VMEM),
-        scratch_shapes=[HALO],
+        scratch_shapes=[HALO, pltpu.VMEM((NX, NY, NZ, CH), BF16), pltpu.SemaphoreType.DMA((4,))],
         compiler_params=pltpu.CompilerParams(vmem_limit_bytes=30 << 20),
         cost_estimate=pl.CostEstimate(flops=2 * 4096 * OFFSETS * CH * CH, bytes_accessed=20 << 20, transcendentals=0),
         name="weight_gradient",
-    )(slot_pos, meta, grid, *sides, xt)
+    )(slot_pos, meta, pin(grid, pltpu.HBM), *sides, xt)
 
 
 def rim_terms(slot_pos, meta, planes, xt, total, patch):
@@ -309,6 +325,23 @@
     )(slot_pos, meta, *planes, xt, total, patch)
 
 
+def flip_kernel(w_ref, out_ref):
+    for o in range(OFFSETS):
+        out_ref[o * CH : (o + 1) * CH] = w_ref[OFFSETS - 1 - o].T
+
+
+def flip(weights):
+    return pl.pallas_call(
+        flip_kernel,
+        out_shape=pltpu.VMEM((OFFSETS * CH, CH), BF16),
+        in_specs=[VMEM],
+        out_specs=VMEM,
+        compiler_params=pltpu.CompilerParams(vmem_limit_bytes=8 << 20),
+        cost_estimate=pl.CostEstimate(flops=0, bytes_accessed=2 << 20, transcendentals=0),
+        name="flip",
+    )(weights)
+
+
 def conv_kernel(first, pos_ref, occ_ref, patch_ref, w_ref, *rest):
     out_ref = rest[-1]
     s = first + pl.program_id(0)
@@ -343,7 +376,7 @@
         compiler_params=pltpu.CompilerParams(vmem_limit_bytes=16 << 20),
         cost_estimate=pl.CostEstimate(flops=count * 4 * VOX * OFFSETS * CH * CH, bytes_accessed=count << 20, transcendentals=0),
         name="convolve",
-    )(slot_pos, occupancy, pin(patch, pltpu.HBM), weights, *extra)
+    )(slot_pos, occupancy, pin(patch, pltpu.HBM), pin(weights, pltpu.VMEM), *extra)
 
 
 def finish_kernel(meta_ref, own_ref, other_ref, out_ref, rows):
@@ -409,7 +442,12 @@
         return lax.ppermute(value, AXES, [(number(a), number(mate(a, axis, k))) for a in everyone])
 
     def exchange_wide(value, start):
-        pairs = [(i * narrow + j, k * narrow + j) for a in range(start, wide - 1, 2) for i, k in ((a, a + 1), (a + 1, a)) for j in range(narrow)]
+        pairs = [(i * narrow + j, k * narrow + j) for a in range(start, wide - 1, 2) for i, k in ((a, a + 1), (a + 1, a)) for j in range(narrow) if a + 1 != wide // 2]
+        return lax.ppermute(value, AXES, pairs)
+
+    def exchange_far(value):
+        a = wide // 2 - 1
+        pairs = [(i * narrow + j, k * narrow + j) for i, k in ((a, a + 1), (a + 1, a)) for j in range(narrow)]
         return lax.ppermute(value, AXES, pairs)
 
     def exchange_narrow(value, start):
@@ -438,6 +476,7 @@
         return jnp.concatenate([value, parts[1], parts[0], parts[2]], axis=0)
 
     def shards(features, weights, cotangent, occupancy, slot_pos):
+        slot_pos = pin(slot_pos, pltpu.HBM)
         core = lax.axis_index("core")
         x_at = lax.axis_index("x")
         y_at = lax.axis_index("y_hi") * n_y_lo + lax.axis_index("y_lo")
@@ -448,20 +487,22 @@
         side_even, side_odd, source = tie(side_even, side_odd, weights)
         side_even = exchange_narrow(side_even, 0)
         side_odd = exchange_narrow(side_odd, 1)
-        w_backward = source[::-1].transpose(0, 2, 1).reshape(OFFSETS * CH, CH)
-        side_even, side_odd, w_backward = tie(side_even, side_odd, w_backward)
-        y_before, y_after = jnp.where(core == 0, side_odd, side_even), jnp.where(core == 0, side_even, side_odd)
+        side_even, side_odd, w_backward = tie(side_even, side_odd, flip(source))
 
         def rim(plane, last):
-            ends = [jnp.where(last, v[:, NX - 1 :], v[:, :1]) for v in (y_before, y_after)]
-            return jnp.concatenate([ends[0], plane, ends[1]], axis=1)
-
-        even, odd, pos = tie(rim(even, odd_x == 0), rim(odd, odd_x == 1), slot_pos)
+            ends = [jnp.where(last, v[:, NX - 1 :], v[:, :1]) for v in (side_even, side_odd)]
+            first = core == 0
+            return jnp.concatenate([jnp.where(first, ends[1], ends[0]), plane, jnp.where(first, ends[0], ends[1])], axis=1)
+
+        even, odd = rim(even, odd_x == 0), rim(odd, odd_x == 1)
+        far = exchange_far(odd)
+        even, odd, pos = tie(even, odd, slot_pos)
         even = exchange_wide(even, 0)
         odd = exchange_wide(odd, 1)
-        cot_patch, total = weight_gradient(pos, meta, cg, (side_even[0], side_odd[0]), xt)
-        even, odd, total = tie(even, odd, total)
-        cot_patch, keep, send = rim_terms(slot_pos, meta, (even[0], odd[0]), xt, total, cot_patch)
+        cot_patch, total = weight_gradient(pos, meta, cg, (side_even, side_odd), xt)
+        even, odd, far, total = tie(even, odd, far, total)
+        odd = odd + far
+        cot_patch, keep, send = rim_terms(slot_pos, meta, (even, odd), xt, total, cot_patch)
         w_forward = weights.reshape(OFFSETS * CH, CH)
         done = {"outputs": None, "grad_input": None, "patch": None}
 
@@ -474,7 +515,7 @@
             return "outputs"
 
         def gather_patches(at, pos):
-            done["patch"] = patches(pos, meta, xg, (side_even[1], side_odd[1]), (even[1], odd[1]))
+            done["patch"] = patches(pos, meta, xg, (side_even, side_odd), (even, odd))
             return "patch"
 
         def stage(value, start, *work):

time: 110 us -> 111 us (level)
  Pallas kernels: 48.7 us -> 61.9 us
  local copies, waits for them, and re-layouts: 5.61 us -> 0.08 us
  waiting for transfers between devices: 8.83 us -> 5.3 us
  starting transfers between devices: 44.9 us -> 41.8 us
    pallas_call x8, Pallas kernels: 24.8 us -> 31.6 us  [convolve(): pl.pallas_call(lambda *refs: conv_kernel(first, *refs), out_shape=jax.Sha...]
    ppermute x18, waiting for transfers between devices: 5.95 us -> 0.15 us  [swap(): lax.ppermute(value, AXES, [(number(a), number(mate(a, axis, k))) for a in...]
    transpose x2 -> x0, local copies, waits for them, and re-layouts: 2.94 us -> none  [shards(): w_backward = source[::-1].transpose(0, 2, 1).reshape(OFFSETS * CH, CH)]
    ppermute x18, starting transfers between devices: 38.2 us -> 35.8 us  [swap(): lax.ppermute(value, AXES, [(number(a), number(mate(a, axis, k))) for a in...]
    ppermute x2, waiting for transfers between devices: 2.88 us -> 5.14 us  [exchange_narrow(): return lax.ppermute(value, AXES, pairs)]
    pallas_call x1, Pallas kernels: 8.13 us -> 10.3 us  [weight_gradient(): pl.pallas_call(weight_kernel, out_shape=(PATCH_SHAPE, TOTAL), grid=(SLOTS...]
    pallas_call x1, Pallas kernels: 1.26 us -> 3.01 us  [rim_terms(): pl.pallas_call(rim_kernel, out_shape=(PATCH_SHAPE, half, half), in_specs=...]
    pallas_call x1, Pallas kernels: 6.2 us -> 7.75 us  [place(): pl.pallas_call(place_kernel, out_shape=(grid, grid, pltpu.HBM((SLOTS, CH,...]
  transfers between devices with their start and end apart: 22 -> 23, of which waited for: 6 -> 2; matrix products, arithmetic and copies ran while one was open for 3% -> 0% of each run, Pallas kernels for 35% -> 44%
where the time goes in v4:
time: 111 us; the launch traced here: 110 us
  Pallas kernels  61.9 us (56%)
  starting transfers between devices  41.8 us (38%)
  waiting for transfers between devices  5.3 us (5%)
    ppermute x18, starting transfers between devices, swap(): lax.ppermute(value, AXES, [(number(a), number(mate(a, axis, k))) for a in...  35.8 us
    pallas_call x8, Pallas kernels, convolve(): pl.pallas_call(lambda *refs: conv_kernel(first, *refs), out_shape=jax.Sha...  31.6 us
    pallas_call x1, Pallas kernels, weight_gradient(): pl.pallas_call(weight_kernel, out_shape=(PATCH_SHAPE, TOTAL), grid=(SLOTS...  10.3 us
    pallas_call x1, Pallas kernels, place(): pl.pallas_call(place_kernel, out_shape=(grid, grid, pltpu.HBM((SLOTS, CH,...  7.75 us
    pallas_call x1, Pallas kernels, patches(): pl.pallas_call(patches_kernel, out_shape=PATCH_SHAPE, grid=(SLOTS,), in_s...  6.7 us
    ppermute x2, waiting for transfers between devices, exchange_narrow(): return lax.ppermute(value, AXES, pairs)  5.14 us
    ppermute x2, starting transfers between devices, exchange_narrow(): return lax.ppermute(value, AXES, pairs)  4.5 us
    pallas_call x1, Pallas kernels, rim_terms(): pl.pallas_call(rim_kernel, out_shape=(PATCH_SHAPE, half, half), in_specs=...  3.01 us
  transfers between devices with their start and end apart: 23, of which 2 were waited for; matrix products, arithmetic and copies ran while one was open for 0% of the time, Pallas kernels for 44%

profile of v4, /device:TPU:1, one launch (start us, length us, event | category | flops | bytes accessed | tf_op | source)
XLA Modules:
  0.0 110.5 jit_solution(11238809645409388980)
XLA Ops:
  0.7 7.8 %place.1 = (bf16[32,16,16,128]{3,2,1,0:T(8,128)(2,1)}, bf16[32,16,16,128]{3,2,1,0:T(8,128)(2,1)}, bf16[8,128,512]{2,1,0:T(8,128)(2,1)}, bf16[2,16,16,128]{3,2,1,...) custom-call(s32[8]{0:T(128)} %refs_0_.7, ...), custom_call_target="tpu_custom_call" | custom-call | tf_op jit(solution)/shard_map/place/pallas_call | solution.py:103
  8.5 2.3 %collective-permute-start = (bf16[2,32,16,128]{3,2,1,0:T(8,128)(2,1)S(1)}, bf16[2,32,16,128]{3,2,1,0:T(8,128)(2,1)S(1)}, u32[]{:S(2)}, u32[]{:S(2)}) collective-permute-start(bf16[2,32,16,128]{3,2,1,0:T(8,128)(2,1)S(1)} %get-tuple-element.73), channel_id=1, source_target_pairs={{0,1},{1,0},{2,3},{3,2},{4,5},{5,4},{6,7},{7,6},{8,9},{9,8},{10,11... | collective-permute-start | bytes 786440 | tf_op jit(solution)/shard_map/ppermute | solution.py:455
  10.8 2.2 %collective-permute-start.1 = (bf16[2,32,16,128]{3,2,1,0:T(8,128)(2,1)S(1)}, bf16[2,32,16,128]{3,2,1,0:T(8,128)(2,1)S(1)}, u32[]{:S(2)}, u32[]{:S(2)}) collective-permute-start(bf16[2,32,16,128]{3,2,1,0:T(8,128)(2,1)S(1)} %get-tuple-element.74), channel_id=1, source_target_pairs={{1,2},{2,1},{5,6},{6,5},{9,10},{10,9},{13,14},{14,13},{17,18},{18,... | collective-permute-start | bytes 786440 | tf_op jit(solution)/shard_map/ppermute | solution.py:455
  13.0 0.3 flip.1.refs_3_
  13.3 5.1 %collective-permute-done.1.side_odd_ref = bf16[2,32,16,128]{3,2,1,0:T(8,128)(2,1)S(1)} collective-permute-done((bf16[2,32,16,128]{3,2,1,0:T(8,128)(2,1)S(1)}, bf16[2,32,16,128]{3,2,1,0:T(8,128)(2,1)S(1)}, u32[]{:S(2)}, u32[]{:S(2)}) %collective-permute-start.1) | collective-permute-done | bytes 262176 | tf_op jit(solution)/shard_map/ppermute | solution.py:455
  18.5 0.7 collective-permute-start.4
  19.3 0.7 collective-permute-start.3
  20.0 10.3 %weight_gradient.1 = (bf16[8,10,80,384]{3,2,1,0:T(8,128)(2,1)}, f32[3584,128]{1,0:T(8,128)S(1)}) custom-call(s32[8]{0:T(128)} %refs_0_.7, s32[4]{0:T(128)S(1)} %pad_add_fusion.meta_ref, bf16[32,16,16,128]{3,2,1,0:T(8,128)(2,1)} %get-tuple-element.83.grid_hbm, bf16[2,32,16,128]{3,2,1,0:T(8,128)(2,1)S(1)} %collective-permute-done.side_even_ref, ...), custom_call_target="tpu_custom_call" | custom-call | flops 3623878656 | bytes 20971520 | tf_op jit(solution)/shard_map/weight_gradient/pallas_call | solution.py:295
  30.4 3.0 %rim_terms.1 = (bf16[8,10,80,384]{3,2,1,0:T(8,128)(2,1)}, f32[16,112,128]{2,1,0:T(8,128)S(1)}, f32[16,112,128]{2,1,0:T(8,128)S(1)}) custom-call(s32[8]{0:T(128)} %refs_0_.7, s32[4]{0:T(128)S(1)} %pad_add_fusion.meta_ref, bf16[2,18,16,128]{3,2,1,0:T(8,128)(2,1)S(1)} %collective-permute-done.2.even_ref, ...), custom_call_target="tpu_custom_call", output_to_operand_aliasing={{0}: (6, {})} | custom-call | tf_op jit(solution)/shard_map/rim_terms/pallas_call | solution.py:311
  33.5 2.8 %convolve.8.refs_4_ = bf16[8,512,128]{2,1,0:T(8,128)(2,1)} custom-call(s32[8]{0:T(128)} %refs_0_.7, s32[8,512]{1,0:T(8,128)S(1)} %copy-done.2, bf16[8,10,80,384]{3,2,1,0:T(8,128)(2,1)} %get-tuple-element.95.refs_2_, bf16[3456,128]{1,0:T(8,128)(2,1)S(1)} %flip.1.refs_3_), custom_call_target="tpu_custom_call" | custom-call | flops 905969664 | bytes 1048576 | tf_op jit(solution)/shard_map/convolve/pallas_call | solution.py:368
  36.5 2.8 %collective-permute-start.8 = (f32[4,112,128]{2,1,0:T(8,128)S(1)}, f32[4,112,128]{2,1,0:T(8,128)S(1)}, u32[]{:S(2)}, u32[]{:S(2)}) collective-permute-start(f32[4,112,128]{2,1,0:T(8,128)S(1)} %get-tuple-element.139), channel_id=1, source_target_pairs={{0,130},{1,13},{2,128},{3,15},{4,134},{5,9},{6,132},{7,11},{8,138}... | collective-permute-start | bytes 688136 | tf_op jit(solution)/shard_map/ppermute | solution.py:442
  39.4 0.8 collective-permute-start.7
  40.1 0.7 collective-permute-start.6
  40.8 6.2 %convolve.9.refs_4_ = bf16[8,512,128]{2,1,0:T(8,128)(2,1)} custom-call(s32[8]{0:T(128)} %refs_0_.7, s32[8,512]{1,0:T(8,128)S(1)} %copy-done.2, bf16[8,10,80,384]{3,2,1,0:T(8,128)(2,1)} %get-tuple-element.95.refs_2_, bf16[3456,128]{1,0:T(8,128)(2,1)S(1)} %flip.1.refs_3_, bf16[8,512,128]{2,1,0:T(8,128)(2,1)} %convolve.8.refs_4_), custom_call_target="tpu_custom_call", output_to_operand_aliasing={{}: (4, {})} | custom-call | flops 3623878656 | bytes 4194304 | tf_op jit(solution)/shard_map/convolve/pallas_call | solution.py:368
  47.1 11.0 %collective-permute-start.11 = (f32[1,112,128]{2,1,0:T(8,128)S(1)}, f32[1,112,128]{2,1,0:T(8,128)S(1)}, u32[]{:S(2)}, u32[]{:S(2)}) collective-permute-start(f32[1,112,128]{2,1,0:T(8,128)S(1)} %get-tuple-element.146), channel_id=1, source_target_pairs={{0,12},{1,131},{2,14},{3,129},{4,8},{5,135},{6,10},{7,133},{8,4},{... | collective-permute-start | bytes 172040 | tf_op jit(solution)/shard_map/ppermute | solution.py:442
  58.1 1.3 %collective-permute-start.9 = (f32[1,112,128]{2,1,0:T(8,128)S(1)}, f32[1,112,128]{2,1,0:T(8,128)S(1)}, u32[]{:S(2)}, u32[]{:S(2)}) collective-permute-start(f32[1,112,128]{2,1,0:T(8,128)S(1)} %get-tuple-element.148), channel_id=1, source_target_pairs={{0,8},{1,129},{2,10},{3,131},{4,12},{5,133},{6,14},{7,135},{8,0},{... | collective-permute-start | bytes 172040 | tf_op jit(solution)/shard_map/ppermute | solution.py:442
  59.4 4.0 %convolve.10.refs_4_ = bf16[8,512,128]{2,1,0:T(8,128)(2,1)} custom-call(s32[8]{0:T(128)} %refs_0_.7, s32[8,512]{1,0:T(8,128)S(1)} %copy-done.2, bf16[8,10,80,384]{3,2,1,0:T(8,128)(2,1)} %get-tuple-element.95.refs_2_, bf16[3456,128]{1,0:T(8,128)(2,1)S(1)} %flip.1.refs_3_, bf16[8,512,128]{2,1,0:T(8,128)(2,1)} %convolve.9.refs_4_), custom_call_target="tpu_custom_call", output_to_operand_aliasing={{}: (4, {})} | custom-call | flops 1811939328 | bytes 2097152 | tf_op jit(solution)/shard_map/convolve/pallas_call | solution.py:368
  63.6 3.4 %collective-permute-start.12 = (f32[1,112,128]{2,1,0:T(8,128)S(1)}, f32[1,112,128]{2,1,0:T(8,128)S(1)}, u32[]{:S(2)}, u32[]{:S(2)}) collective-permute-start(f32[1,112,128]{2,1,0:T(8,128)S(1)} %add_add_fusion.2), channel_id=1, source_target_pairs={{0,32},{1,33},{2,34},{3,35},{4,36},{5,37},{6,38},{7,39},{8,40},{9,... | collective-permute-start | bytes 172040 | tf_op jit(solution)/shard_map/ppermute | solution.py:442
  67.0 6.7 %patches.1.refs_2_ = bf16[8,10,80,384]{3,2,1,0:T(8,128)(2,1)} custom-call(s32[8]{0:T(128)} %refs_0_.7, s32[4]{0:T(128)S(1)} %pad_add_fusion.meta_ref, bf16[32,16,16,128]{3,2,1,0:T(8,128)(2,1)} %get-tuple-element.112.grid_hbm, bf16[2,32,16,128]{3,2,1,0:T(8,128)(2,1)S(1)} %collective-permute-done.side_even_ref, ...), custom_call_target="tpu_custom_call" | custom-call | bytes 20971520 | tf_op jit(solution)/shard_map/patches/pallas_call | solution.py:281
  73.8 1.3 %collective-permute-start.15 = (f32[1,112,128]{2,1,0:T(8,128)S(1)}, f32[1,112,128]{2,1,0:T(8,128)S(1)}, u32[]{:S(2)}, u32[]{:S(2)}) collective-permute-start(f32[1,112,128]{2,1,0:T(8,128)S(1)} %add_add_fusion.1), channel_id=1, source_target_pairs={{0,64},{1,65},{2,66},{3,67},{4,68},{5,69},{6,70},{7,71},{8,72},{9,... | collective-permute-start | bytes 172040 | tf_op jit(solution)/shard_map/ppermute | solution.py:442
  75.1 2.8 %convolve.11 = bf16[8,512,128]{2,1,0:T(8,128)(2,1)} custom-call(s32[8]{0:T(128)} %refs_0_.7, s32[8,512]{1,0:T(8,128)S(1)} %copy-done.2, bf16[8,10,80,384]{3,2,1,0:T(8,128)(2,1)} %get-tuple-element.95.refs_2_, bf16[3456,128]{1,0:T(8,128)(2,1)S(1)} %flip.1.refs_3_, bf16[8,512,128]{2,1,0:T(8,128)(2,1)} %convolve.10.refs_4_), custom_call_target="tpu_custom_call", output_to_operand_aliasing={{}: (4, {})} | custom-call | flops 905969664 | bytes 1048576 | tf_op jit(solution)/shard_map/convolve/pallas_call | solution.py:368
  77.9 2.8 %convolve.12.refs_4_ = bf16[8,512,128]{2,1,0:T(8,128)(2,1)} custom-call(s32[8]{0:T(128)} %refs_0_.7, s32[8,512]{1,0:T(8,128)S(1)} %copy-done.2, bf16[8,10,80,384]{3,2,1,0:T(8,128)(2,1)} %patches.1.refs_2_, bf16[3456,128]{1,0:T(8,128)(2,1)S(1)} %bitcast.5), custom_call_target="tpu_custom_call" | custom-call | flops 905969664 | bytes 1048576 | tf_op jit(solution)/shard_map/convolve/pallas_call | solution.py:368
  80.8 2.7 %collective-permute-start.18 = (f32[1,112,128]{2,1,0:T(8,128)S(1)}, f32[1,112,128]{2,1,0:T(8,128)S(1)}, u32[]{:S(2)}, u32[]{:S(2)}) collective-permute-start(f32[1,112,128]{2,1,0:T(8,128)S(1)} %add.59), channel_id=1, source_target_pairs={{0,12},{1,131},{2,14},{3,129},{4,8},{5,135},{6,10},{7,133},{8,4},{... | collective-permute-start | bytes 172040 | tf_op jit(solution)/shard_map/ppermute | solution.py:442
  83.5 1.3 %collective-permute-start.16 = (f32[1,112,128]{2,1,0:T(8,128)S(1)}, f32[1,112,128]{2,1,0:T(8,128)S(1)}, u32[]{:S(2)}, u32[]{:S(2)}) collective-permute-start(f32[1,112,128]{2,1,0:T(8,128)S(1)} %add.59), channel_id=1, source_target_pairs={{0,8},{1,129},{2,10},{3,131},{4,12},{5,133},{6,14},{7,135},{8,0},{... | collective-permute-start | bytes 172040 | tf_op jit(solution)/shard_map/ppermute | solution.py:442
  84.8 3.9 %convolve.13.refs_4_ = bf16[8,512,128]{2,1,0:T(8,128)(2,1)} custom-call(s32[8]{0:T(128)} %refs_0_.7, s32[8,512]{1,0:T(8,128)S(1)} %copy-done.2, bf16[8,10,80,384]{3,2,1,0:T(8,128)(2,1)} %patches.1.refs_2_, bf16[3456,128]{1,0:T(8,128)(2,1)S(1)} %bitcast.6, bf16[8,512,128]{2,1,0:T(8,128)(2,1)} %convolve.12.refs_4_), custom_call_target="tpu_custom_call", output_to_operand_aliasing={{}: (4, {})} | custom-call | flops 1811939328 | bytes 2097152 | tf_op jit(solution)/shard_map/convolve/pallas_call | solution.py:368
  88.8 0.9 collective-permute-start.21
  89.6 1.1 collective-permute-start.20
  90.7 2.0 %collective-permute-start.19 = (f32[4,112,128]{2,1,0:T(8,128)S(1)}, f32[4,112,128]{2,1,0:T(8,128)S(1)}, u32[]{:S(2)}, u32[]{:S(2)}) collective-permute-start(f32[4,112,128]{2,1,0:T(8,128)S(1)} %pad_maximum_fusion.1), channel_id=1, source_target_pairs={{0,128},{1,9},{2,130},{3,11},{4,132},{5,13},{6,134},{7,15},{8,136}... | collective-permute-start | bytes 688136 | tf_op jit(solution)/shard_map/ppermute | solution.py:442
  92.7 6.2 %convolve.14.refs_4_ = bf16[8,512,128]{2,1,0:T(8,128)(2,1)} custom-call(s32[8]{0:T(128)} %refs_0_.7, s32[8,512]{1,0:T(8,128)S(1)} %copy-done.2, bf16[8,10,80,384]{3,2,1,0:T(8,128)(2,1)} %patches.1.refs_2_, bf16[3456,128]{1,0:T(8,128)(2,1)S(1)} %bitcast.7, bf16[8,512,128]{2,1,0:T(8,128)(2,1)} %convolve.13.refs_4_), custom_call_target="tpu_custom_call", output_to_operand_aliasing={{}: (4, {})} | custom-call | flops 3623878656 | bytes 4194304 | tf_op jit(solution)/shard_map/convolve/pallas_call | solution.py:368
  99.0 6.4 %collective-permute-start.22 = (f32[16,112,128]{2,1,0:T(8,128)S(1)}, f32[16,112,128]{2,1,0:T(8,128)S(1)}, u32[]{:S(2)}, u32[]{:S(2)}) collective-permute-start(f32[16,112,128]{2,1,0:T(8,128)S(1)} %pad_maximum_fusion.own_ref), channel_id=1, source_target_pairs={{0,1},{1,0},{2,3},{3,2},{4,5},{5,4},{6,7},{7,6},{8,9},{9,8},{10,11... | collective-permute-start | bytes 2752520 | tf_op jit(solution)/shard_map/ppermute | solution.py:442
  105.4 2.8 %convolve.15 = bf16[8,512,128]{2,1,0:T(8,128)(2,1)} custom-call(s32[8]{0:T(128)} %refs_0_.7, s32[8,512]{1,0:T(8,128)S(1)} %copy-done.2, bf16[8,10,80,384]{3,2,1,0:T(8,128)(2,1)} %patches.1.refs_2_, bf16[3456,128]{1,0:T(8,128)(2,1)S(1)} %bitcast.8, bf16[8,512,128]{2,1,0:T(8,128)(2,1)} %convolve.14.refs_4_), custom_call_target="tpu_custom_call", output_to_operand_aliasing={{}: (4, {})} | custom-call | flops 905969664 | bytes 1048576 | tf_op jit(solution)/shard_map/convolve/pallas_call | solution.py:368
  108.2 2.2 %finish.1 = f32[27,128,128]{2,1,0:T(8,128)} custom-call(s32[4]{0:T(128)S(1)} %pad_add_fusion.meta_ref, f32[16,112,128]{2,1,0:T(8,128)S(1)} %pad_maximum_fusion.own_ref, f32[16,112,128]{2,1,0:T(8,128)S(1)} %collective-permute-done.22.other_ref), custom_call_target="tpu_custom_call" | custom-call | tf_op jit(solution)/shard_map/finish/pallas_call | solution.py:403
  (48 shorter events, 1.1 us)
Async XLA Ops:
  0.6 12.4 %copy-start = (bf16[27,128,128]{2,1,0:T(8,128)(2,1)S(1)}, bf16[27,128,128]{2,1,0:T(8,128)(2,1)}, u32[]{:S(2)}) copy-start(bf16[27,128,128]{2,1,0:T(8,128)(2,1)} %w_ref) | copy-start | bytes 2654212
  8.5 11.5 %copy-start.1 = (bf16[8,128,512]{2,1,0:T(8,128)(2,1)S(1)}, bf16[8,128,512]{2,1,0:T(8,128)(2,1)}, u32[]{:S(2)}) copy-start(bf16[8,128,512]{2,1,0:T(8,128)(2,1)} %get-tuple-element.84.xt_ref) | copy-start | bytes 3145732
  8.5 4.8 %collective-permute-start = (bf16[2,32,16,128]{3,2,1,0:T(8,128)(2,1)S(1)}, bf16[2,32,16,128]{3,2,1,0:T(8,128)(2,1)S(1)}, u32[]{:S(2)}, u32[]{:S(2)}) collective-permute-start(bf16[2,32,16,128]{3,2,1,0:T(8,128)(2,1)S(1)} %get-tuple-element.73), channel_id=1, source_target_pairs={{0,1},{1,0},{2,3},{3,2},{4,5},{5,4},{6,7},{7,6},{8,9},{9,8},{10,11... | collective-permute-start | bytes 786440 | tf_op jit(solution)/shard_map/ppermute | solution.py:455
  10.8 7.7 %collective-permute-start.1 = (bf16[2,32,16,128]{3,2,1,0:T(8,128)(2,1)S(1)}, bf16[2,32,16,128]{3,2,1,0:T(8,128)(2,1)S(1)}, u32[]{:S(2)}, u32[]{:S(2)}) collective-permute-start(bf16[2,32,16,128]{3,2,1,0:T(8,128)(2,1)S(1)} %get-tuple-element.74), channel_id=1, source_target_pairs={{1,2},{2,1},{5,6},{6,5},{9,10},{10,9},{13,14},{14,13},{17,18},{18,... | collective-permute-start | bytes 786440 | tf_op jit(solution)/shard_map/ppermute | solution.py:455
  18.5 11.8 %collective-permute-start.4 = (bf16[2,18,16,128]{3,2,1,0:T(8,128)(2,1)S(1)}, bf16[2,18,16,128]{3,2,1,0:T(8,128)(2,1)S(1)}, u32[]{:S(2)}, u32[]{:S(2)}) collective-permute-start(bf16[2,18,16,128]{3,2,1,0:T(8,128)(2,1)S(1)} %pad_maximum_fusion.3), channel_id=1, source_target_pairs={{124,128},{125,129},{126,130},{127,131},{128,124},{129,125},{130,1... | collective-permute-start | bytes 442376 | tf_op jit(solution)/shard_map/ppermute | solution.py:451
  19.2 11.1 %collective-permute-start.2 = (bf16[2,18,16,128]{3,2,1,0:T(8,128)(2,1)S(1)}, bf16[2,18,16,128]{3,2,1,0:T(8,128)(2,1)S(1)}, u32[]{:S(2)}, u32[]{:S(2)}) collective-permute-start(bf16[2,18,16,128]{3,2,1,0:T(8,128)(2,1)S(1)} %pad_maximum_fusion.2), channel_id=1, source_target_pairs={{0,4},{1,5},{2,6},{3,7},{4,0},{5,1},{6,2},{7,3},{8,12},{9,13},{10,... | collective-permute-start | bytes 442376 | tf_op jit(solution)/shard_map/ppermute | solution.py:446
  19.3 11.0 %collective-permute-start.3 = (bf16[2,18,16,128]{3,2,1,0:T(8,128)(2,1)S(1)}, bf16[2,18,16,128]{3,2,1,0:T(8,128)(2,1)S(1)}, u32[]{:S(2)}, u32[]{:S(2)}) collective-permute-start(bf16[2,18,16,128]{3,2,1,0:T(8,128)(2,1)S(1)} %pad_maximum_fusion.3), channel_id=1, source_target_pairs={{4,8},{5,9},{6,10},{7,11},{8,4},{9,5},{10,6},{11,7},{12,16},{13,17... | collective-permute-start | bytes 442376 | tf_op jit(solution)/shard_map/ppermute | solution.py:446
  30.4 3.1 %copy-start.2 = (s32[8,512]{1,0:T(8,128)S(1)}, s32[8,512]{1,0:T(8,128)}, u32[]{:S(2)}) copy-start(s32[8,512]{1,0:T(8,128)} %refs_1_.15) | copy-start | bytes 49156
  33.4 2.9 %collective-permute-start.5 = (f32[16,112,128]{2,1,0:T(8,128)S(1)}, f32[16,112,128]{2,1,0:T(8,128)S(1)}, u32[]{:S(2)}, u32[]{:S(2)}) collective-permute-start(f32[16,112,128]{2,1,0:T(8,128)S(1)} %get-tuple-element.93), channel_id=1, source_target_pairs={{0,1},{1,0},{2,3},{3,2},{4,5},{5,4},{6,7},{7,6},{8,9},{9,8},{10,11... | collective-permute-start | bytes 2752520 | tf_op jit(solution)/shard_map/ppermute | solution.py:442
  36.5 10.5 %collective-permute-start.8 = (f32[4,112,128]{2,1,0:T(8,128)S(1)}, f32[4,112,128]{2,1,0:T(8,128)S(1)}, u32[]{:S(2)}, u32[]{:S(2)}) collective-permute-start(f32[4,112,128]{2,1,0:T(8,128)S(1)} %get-tuple-element.139), channel_id=1, source_target_pairs={{0,130},{1,13},{2,128},{3,15},{4,134},{5,9},{6,132},{7,11},{8,138}... | collective-permute-start | bytes 688136 | tf_op jit(solution)/shard_map/ppermute | solution.py:442
  39.4 7.7 %collective-permute-start.7 = (f32[4,112,128]{2,1,0:T(8,128)S(1)}, f32[4,112,128]{2,1,0:T(8,128)S(1)}, u32[]{:S(2)}, u32[]{:S(2)}) collective-permute-start(f32[4,112,128]{2,1,0:T(8,128)S(1)} %get-tuple-element.140), channel_id=1, source_target_pairs={{0,2},{1,5},{2,0},{3,7},{4,6},{5,1},{6,4},{7,3},{8,10},{9,13},{10,... | collective-permute-start | bytes 688136 | tf_op jit(solution)/shard_map/ppermute | solution.py:442
  40.1 6.9 %collective-permute-start.6 = (f32[4,112,128]{2,1,0:T(8,128)S(1)}, f32[4,112,128]{2,1,0:T(8,128)S(1)}, u32[]{:S(2)}, u32[]{:S(2)}) collective-permute-start(f32[4,112,128]{2,1,0:T(8,128)S(1)} %get-tuple-element.141), channel_id=1, source_target_pairs={{0,128},{1,9},{2,130},{3,11},{4,132},{5,13},{6,134},{7,15},{8,136}... | collective-permute-start | bytes 688136 | tf_op jit(solution)/shard_map/ppermute | solution.py:442
  47.1 16.2 %collective-permute-start.11 = (f32[1,112,128]{2,1,0:T(8,128)S(1)}, f32[1,112,128]{2,1,0:T(8,128)S(1)}, u32[]{:S(2)}, u32[]{:S(2)}) collective-permute-start(f32[1,112,128]{2,1,0:T(8,128)S(1)} %get-tuple-element.146), channel_id=1, source_target_pairs={{0,12},{1,131},{2,14},{3,129},{4,8},{5,135},{6,10},{7,133},{8,4},{... | collective-permute-start | bytes 172040 | tf_op jit(solution)/shard_map/ppermute | solution.py:442
  58.1 5.3 %collective-permute-start.10 = (f32[1,112,128]{2,1,0:T(8,128)S(1)}, f32[1,112,128]{2,1,0:T(8,128)S(1)}, u32[]{:S(2)}, u32[]{:S(2)}) collective-permute-start(f32[1,112,128]{2,1,0:T(8,128)S(1)} %get-tuple-element.147), channel_id=1, source_target_pairs={{0,4},{1,3},{2,6},{3,1},{4,0},{5,7},{6,2},{7,5},{8,12},{9,11},{10,... | collective-permute-start | bytes 172040 | tf_op jit(solution)/shard_map/ppermute | solution.py:442
  58.1 5.3 %collective-permute-start.9 = (f32[1,112,128]{2,1,0:T(8,128)S(1)}, f32[1,112,128]{2,1,0:T(8,128)S(1)}, u32[]{:S(2)}, u32[]{:S(2)}) collective-permute-start(f32[1,112,128]{2,1,0:T(8,128)S(1)} %get-tuple-element.148), channel_id=1, source_target_pairs={{0,8},{1,129},{2,10},{3,131},{4,12},{5,133},{6,14},{7,135},{8,0},{... | collective-permute-start | bytes 172040 | tf_op jit(solution)/shard_map/ppermute | solution.py:442
  63.4 10.3 %collective-permute-start.14 = (f32[1,112,128]{2,1,0:T(8,128)S(1)}, f32[1,112,128]{2,1,0:T(8,128)S(1)}, u32[]{:S(2)}, u32[]{:S(2)}) collective-permute-start(f32[1,112,128]{2,1,0:T(8,128)S(1)} %add_add_fusion.2), channel_id=1, source_target_pairs={{0,48},{1,49},{2,50},{3,51},{4,52},{5,53},{6,54},{7,55},{8,56},{9,... | collective-permute-start | bytes 172040 | tf_op jit(solution)/shard_map/ppermute | solution.py:442
  63.5 10.3 %collective-permute-start.13 = (f32[1,112,128]{2,1,0:T(8,128)S(1)}, f32[1,112,128]{2,1,0:T(8,128)S(1)}, u32[]{:S(2)}, u32[]{:S(2)}) collective-permute-start(f32[1,112,128]{2,1,0:T(8,128)S(1)} %add_add_fusion.2), channel_id=1, source_target_pairs={{0,16},{1,17},{2,18},{3,19},{4,20},{5,21},{6,22},{7,23},{8,24},{9,... | collective-permute-start | bytes 172040 | tf_op jit(solution)/shard_map/ppermute | solution.py:442
  63.6 10.2 %collective-permute-start.12 = (f32[1,112,128]{2,1,0:T(8,128)S(1)}, f32[1,112,128]{2,1,0:T(8,128)S(1)}, u32[]{:S(2)}, u32[]{:S(2)}) collective-permute-start(f32[1,112,128]{2,1,0:T(8,128)S(1)} %add_add_fusion.2), channel_id=1, source_target_pairs={{0,32},{1,33},{2,34},{3,35},{4,36},{5,37},{6,38},{7,39},{8,40},{9,... | collective-permute-start | bytes 172040 | tf_op jit(solution)/shard_map/ppermute | solution.py:442
  73.8 7.0 %collective-permute-start.15 = (f32[1,112,128]{2,1,0:T(8,128)S(1)}, f32[1,112,128]{2,1,0:T(8,128)S(1)}, u32[]{:S(2)}, u32[]{:S(2)}) collective-permute-start(f32[1,112,128]{2,1,0:T(8,128)S(1)} %add_add_fusion.1), channel_id=1, source_target_pairs={{0,64},{1,65},{2,66},{3,67},{4,68},{5,69},{6,70},{7,71},{8,72},{9,... | collective-permute-start | bytes 172040 | tf_op jit(solution)/shard_map/ppermute | solution.py:442
  80.8 7.9 %collective-permute-start.18 = (f32[1,112,128]{2,1,0:T(8,128)S(1)}, f32[1,112,128]{2,1,0:T(8,128)S(1)}, u32[]{:S(2)}, u32[]{:S(2)}) collective-permute-start(f32[1,112,128]{2,1,0:T(8,128)S(1)} %add.59), channel_id=1, source_target_pairs={{0,12},{1,131},{2,14},{3,129},{4,8},{5,135},{6,10},{7,133},{8,4},{... | collective-permute-start | bytes 172040 | tf_op jit(solution)/shard_map/ppermute | solution.py:442
  83.5 5.2 %collective-permute-start.17 = (f32[1,112,128]{2,1,0:T(8,128)S(1)}, f32[1,112,128]{2,1,0:T(8,128)S(1)}, u32[]{:S(2)}, u32[]{:S(2)}) collective-permute-start(f32[1,112,128]{2,1,0:T(8,128)S(1)} %add.59), channel_id=1, source_target_pairs={{0,4},{1,3},{2,6},{3,1},{4,0},{5,7},{6,2},{7,5},{8,12},{9,11},{10,... | collective-permute-start | bytes 172040 | tf_op jit(solution)/shard_map/ppermute | solution.py:442
  83.5 5.2 %collective-permute-start.16 = (f32[1,112,128]{2,1,0:T(8,128)S(1)}, f32[1,112,128]{2,1,0:T(8,128)S(1)}, u32[]{:S(2)}, u32[]{:S(2)}) collective-permute-start(f32[1,112,128]{2,1,0:T(8,128)S(1)} %add.59), channel_id=1, source_target_pairs={{0,8},{1,129},{2,10},{3,131},{4,12},{5,133},{6,14},{7,135},{8,0},{... | collective-permute-start | bytes 172040 | tf_op jit(solution)/shard_map/ppermute | solution.py:442
  88.8 10.1 %collective-permute-start.21 = (f32[4,112,128]{2,1,0:T(8,128)S(1)}, f32[4,112,128]{2,1,0:T(8,128)S(1)}, u32[]{:S(2)}, u32[]{:S(2)}) collective-permute-start(f32[4,112,128]{2,1,0:T(8,128)S(1)} %pad_maximum_fusion.1), channel_id=1, source_target_pairs={{0,130},{1,13},{2,128},{3,15},{4,134},{5,9},{6,132},{7,11},{8,138}... | collective-permute-start | bytes 688136 | tf_op jit(solution)/shard_map/ppermute | solution.py:442
  89.6 9.3 %collective-permute-start.20 = (f32[4,112,128]{2,1,0:T(8,128)S(1)}, f32[4,112,128]{2,1,0:T(8,128)S(1)}, u32[]{:S(2)}, u32[]{:S(2)}) collective-permute-start(f32[4,112,128]{2,1,0:T(8,128)S(1)} %pad_maximum_fusion.1), channel_id=1, source_target_pairs={{0,2},{1,5},{2,0},{3,7},{4,6},{5,1},{6,4},{7,3},{8,10},{9,13},{10,... | collective-permute-start | bytes 688136 | tf_op jit(solution)/shard_map/ppermute | solution.py:442
  90.7 8.2 %collective-permute-start.19 = (f32[4,112,128]{2,1,0:T(8,128)S(1)}, f32[4,112,128]{2,1,0:T(8,128)S(1)}, u32[]{:S(2)}, u32[]{:S(2)}) collective-permute-start(f32[4,112,128]{2,1,0:T(8,128)S(1)} %pad_maximum_fusion.1), channel_id=1, source_target_pairs={{0,128},{1,9},{2,130},{3,11},{4,132},{5,13},{6,134},{7,15},{8,136}... | collective-permute-start | bytes 688136 | tf_op jit(solution)/shard_map/ppermute | solution.py:442
  99.0 9.2 %collective-permute-start.22 = (f32[16,112,128]{2,1,0:T(8,128)S(1)}, f32[16,112,128]{2,1,0:T(8,128)S(1)}, u32[]{:S(2)}, u32[]{:S(2)}) collective-permute-start(f32[16,112,128]{2,1,0:T(8,128)S(1)} %pad_maximum_fusion.own_ref), channel_id=1, source_target_pairs={{0,1},{1,0},{2,3},{3,2},{4,5},{5,4},{6,7},{7,6},{8,9},{9,8},{10,11... | collective-permute-start | bytes 2752520 | tf_op jit(solution)/shard_map/ppermute | solution.py:442
